TPU v7x, 32 devices: a whole 2x2x4 slice. The times are simulated.
32 devices in a mesh: group: 2 (over y), tile: 4 (over z), strip: 2 (over x), sub: 2 (over core).
Axes of the slice: x: 2, y: 2, z: 4, core: 2. Of those that a mesh axis runs over, the one named last changes fastest.
Arguments:
- right_side: float32 [32, 128, 1024], P('group', 'tile', ('strip', 'sub')), parts along dimension 0, may hold values from -24 to 24
- horiz_coef: float32 [256, 1024], P(('group', 'tile'), ('strip', 'sub')), parts along dimension 0, may hold values from 8 to 32
- vert_coef: float32 [256, 1024], P(('group', 'tile'), ('strip', 'sub')), parts along dimension 0, may hold values from 1 to 8
- panel_owner: int32 [16384, 1], P(('group', 'tile', 'strip', 'sub')), parts along dimension 0, may hold values from 0 to 3; in each aligned block of 512 rows (0 to 511, 512 to 1023, ...) at most 384 rows name the same one
- panel_cell: int32 [16384], P(('group', 'tile', 'strip', 'sub')), parts along dimension 0, may hold values from 0 to 8191
- panel_pressure: float32 [16384], P(('group', 'tile', 'strip', 'sub')), parts along dimension 0, may hold values from -48 to 48
Outputs:
- potential: float32 [32, 128, 1024], P('group', 'tile', ('strip', 'sub')), parts along dimension 0
- residual: float32 [32, 128, 1024], P('group', 'tile', ('strip', 'sub')), parts along dimension 0
There are 2 independent parts, one for each index of `group`. A program takes and returns all parts, laid end to end along the dimension named above; each array names one. Nothing has to cross between parts.
Inputs may be any that keep to these rules, and one draw needn't show every extreme that they name: `panel_owner`: among the 512 panels of one device at most 384 name one owner; some device reaches 384 in every draw.
All inputs are finite; a program needn't handle non-finite values.
Results may differ from a plain program's by a relative error of at most 0.00015.
Values sent between devices are 32-bit elements; how exact they have to be, the bound alone decides.
No kernel may reach another device: no remote copies, remote signals or barrier semaphores. Data moves between devices by JAX's collectives and lax.ppermute only.
A program may use at most 128 MiB of HBM per device.

v0:
```python
import jax
import jax.numpy as jnp
import numpy as np
from jax import lax
from jax.experimental import pallas as pl
from jax.experimental.pallas import tpu as pltpu

COARSE = 8
OMEGA = 0.8

HX = 12
HX2 = 9
HY = 42
SLABS = 3


def edge_pairs(count, odd):
    out = []
    for i in range(1 if odd else 0, count - 1, 2):
        out += [(i, i + 1), (i + 1, i)]
    return out


def lane_maps(cols):
    one = -np.ones(cols + 128, np.int64)
    half = cols // 2
    one[:cols] = np.arange(cols) // 2
    one[cols : cols + HY] = half + np.arange(HY) // 2
    one[cols + 128 - HY :] = 2 * half - HY // 2 + np.arange(HY) // 2
    h1 = HY // 2
    two = -np.ones(2 * half, np.int64)
    quarter = half // 2
    two[:half] = np.arange(half) // 2
    two[half : half + h1 - 1] = quarter + np.arange(h1 - 1) // 2
    two[2 * half - h1 + 1 :] = 2 * quarter - (h1 - 1) // 2 + np.arange(h1 - 1) // 2
    return one, two


def selection(lanes, width):
    return (lanes[:, None] == np.arange(width)[None, :]).astype(np.float32)


def exact_dot(left, right):
    high = left.astype(jnp.bfloat16)
    rest = left - high.astype(jnp.float32)
    mid = rest.astype(jnp.bfloat16)
    low = (rest - mid.astype(jnp.float32)).astype(jnp.bfloat16)
    dot = lambda part: jnp.dot(part, right, preferred_element_type=jnp.float32)
    return dot(high) + dot(mid) + dot(low)


def neighbours(u):
    rows, lanes = u.shape
    return (
        pltpu.roll(u, 1, 0)
        + pltpu.roll(u, rows - 1, 0)
        + pltpu.roll(u, 1, 1)
        + pltpu.roll(u, lanes - 1, 1)
    )


def weights(kh, kv, scale, inside, w_ref, a_ref, b_ref):
    for i, layers in enumerate((1.0, 2.0)):
        diag = 4.0 * scale * kh + layers * kv
        w = jnp.where(inside, OMEGA / jnp.where(inside, diag, 1.0), 0.0)
        if w_ref is not None:
            w_ref[i] = w
        a_ref[i] = w * (scale * kh)
        b_ref[i] = w * kv


def sweep(src, dst, wb, a_ref, b_ref, depth):
    def layer(z, c):
        i = jnp.minimum(z, 1)
        u = src[z + 1]
        dst[z + 1] = (
            (1.0 - OMEGA) * u
            + wb[z]
            + a_ref[i] * neighbours(u)
            + b_ref[i] * (src[z] + src[z + 2])
        )
        return c

    lax.fori_loop(0, depth, layer, 0)


def residual_of(src, z, b, kh, kv, scale):
    layers = jnp.where(z == 0, 1.0, 2.0)
    u = src[z + 1]
    return b + (scale * kh) * (neighbours(u) - 4.0 * u) + kv * (src[z] + src[z + 2] - layers * u)


def blocks_out(ref, l, x):
    for j in range(ref.shape[1]):
        ref[l, j, 0 : x.shape[0], :] = x[:, 128 * j : 128 * (j + 1)]


def blocks_in(ref, l):
    return jnp.concatenate([ref[l, j] for j in range(ref.shape[1])], 1)


def rows_doubled(ref, l, part):
    n = part.shape[0]
    for j in range(ref.shape[1]):
        for s in (0, 1):
            ref[l, j, pl.ds(s, n, stride=2), :] = part[:, 128 * j : 128 * (j + 1)]


def pack_rows_kernel(rs, kh, kv, a_out, b_out):
    depth, rows, _ = rs.shape
    even = lax.axis_index("tile") % 2 == 0

    def layer(l):
        return rs[l] if l < depth else (kh[...] if l == depth else kv[...])

    count = depth + 2
    half = count // 2

    def first(out):
        for l in range(count):
            x = layer(l)
            out[l] = x[0:8]
            out[count + l % half, 4 * (l // half) : 4 * (l // half) + 4, :] = x[8:HX]

    def last(out):
        for l in range(count):
            x = layer(l)
            out[l] = x[rows - 8 : rows]
            out[count + l % half, 4 * (l // half) : 4 * (l // half) + 4, :] = x[rows - HX : rows - 8]

    @pl.when(even)
    def _():
        last(a_out)
        first(b_out)

    @pl.when(jnp.logical_not(even))
    def _():
        first(a_out)
        last(b_out)


def forcing_kernel(rs, kh, kv, xa, xb, panels, ext, sub_out, strip_out):
    depth, rows, cols = rs.shape
    count = depth + 2
    half = count // 2
    tile = lax.axis_index("tile")
    even = tile % 2 == 0
    high = rows + HX

    def upper(x):
        for l in range(count):
            ext[l, 0:4, :] = x[count + l % half, 4 * (l // half) : 4 * (l // half) + 4, :]
            ext[l, 4:HX, :] = x[l]

    def lower(x):
        for l in range(count):
            ext[l, high : high + 8, :] = x[l]
            ext[l, high + 8 : high + HX, :] = x[count + l % half, 4 * (l // half) : 4 * (l // half) + 4, :]

    @pl.when(even)
    def _():
        lower(xa)
        upper(xb)

    @pl.when(jnp.logical_not(even))
    def _():
        upper(xa)
        lower(xb)

    for l in range(depth):
        ext[l, HX:high, :] = rs[l]
    ext[depth, HX:high, :] = kh[...]
    ext[depth + 1, HX:high, :] = kv[...]

    span = rows + 2 * HX
    total = jnp.zeros((span, cols), jnp.float32)
    left, right = [], []
    for g in range(panels.shape[0]):
        for k in range(4):
            code = panels[g, k : k + 1, :].astype(jnp.int32)
            value = panels[g, 4 + k : 5 + k, :]
            row = code // cols - (tile * rows - HX)
            col = code % cols
            hit = row == lax.broadcasted_iota(jnp.int32, (span, 128), 0)
            left.append(jnp.where(hit, value, 0.0))
            right.append(
                jnp.where(col == lax.broadcasted_iota(jnp.int32, (cols, 128), 0), 1.0, 0.0).astype(jnp.bfloat16)
            )
    left = jnp.concatenate(left, 1)
    right = jnp.concatenate(right, 1)
    high_part = left.astype(jnp.bfloat16)
    rest = left - high_part.astype(jnp.float32)
    mid_part = rest.astype(jnp.bfloat16)
    low_part = (rest - mid_part.astype(jnp.float32)).astype(jnp.bfloat16)
    for part in (high_part, mid_part, low_part):
        total = total + lax.dot_general(
            part, right, (((1,), (1,)), ((), ())), preferred_element_type=jnp.float32
        )
    ext[depth - 1] = ext[depth - 1] + total

    y = lax.axis_index("strip") * lax.axis_size("sub") + lax.axis_index("sub")
    y_even = y % 2 == 0
    lane = lax.broadcasted_iota(jnp.int32, (span, 128), 1)

    def slab(g, at_right):
        out = jnp.zeros((span, 128), jnp.float32)
        for k in range(SLABS):
            if at_right:
                x = pltpu.roll(ext[SLABS * g + k, :, cols - 128 : cols], (HY + HY * k) % 128, 1)
            else:
                x = ext[SLABS * g + k, :, 0:128]
                x = pltpu.roll(x, HY * k, 1) if k else x
            out = jnp.where((lane >= HY * k) & (lane < HY * (k + 1)), x, out)
        return out

    for g in range(count // SLABS):
        to_right = slab(g, True)
        to_left = slab(g, False)
        sub_out[g] = jnp.where(y_even, to_right, to_left)
        strip_out[g] = jnp.where(y_even, to_left, to_right)


def down_kernel(
    ext, ysub, ystrip, c1, c2,
    b_out, k_out, u_out, k1_out, b1_out, u1_out, c_out, a_msg, b_msg,
    b0, u0, u0n, r0, w0, al0, be0, w1, al1, be1, u1, u1n, r1,
):
    depth = ext.shape[0] - 2
    span, cols = ext.shape[1], ext.shape[2]
    count = depth + 2
    tiles = lax.axis_size("tile")
    tile = lax.axis_index("tile")
    y_count = lax.axis_size("strip") * lax.axis_size("sub")
    y = lax.axis_index("strip") * lax.axis_size("sub") + lax.axis_index("sub")
    y_even = y % 2 == 0
    rows = span - 2 * HX
    lane = lax.broadcasted_iota(jnp.int32, (span, 128), 1)

    for g in range(count // SLABS):
        from_right = jnp.where(y_even, ysub[g], ystrip[g])
        from_left = jnp.where(y_even, ystrip[g], ysub[g])
        for k in range(SLABS):
            l = SLABS * g + k
            right = pltpu.roll(from_right, 128 - HY * k, 1) if k else from_right
            left = pltpu.roll(from_left, 128 - HY - HY * k, 1) if (128 - HY - HY * k) % 128 else from_left
            b0[l, :, 0:cols] = ext[l]
            b0[l, :, cols : cols + 128] = jnp.where(lane < HY, right, jnp.where(lane >= 128 - HY, left, 0.0))

    def inside_of(shape, first_row, row_end, own, halo):
        row = first_row + lax.broadcasted_iota(jnp.int32, shape, 0)
        column = lax.broadcasted_iota(jnp.int32, shape, 1)
        right = (column >= own) & (column < own + halo) & (y < y_count - 1)
        left = (column >= shape[1] - halo) & (y > 0)
        return (row >= 0) & (row < row_end) & ((column < own) | right | left)

    lanes = cols + 128
    kh, kv = b0[depth], b0[depth + 1]
    weights(kh, kv, 1.0, inside_of((span, lanes), tile * rows - HX, tiles * rows, cols, HY), w0, al0, be0)
    zero = jnp.zeros((span, lanes), jnp.float32)
    u0[0] = zero
    u0[depth + 1] = zero
    u0n[0] = zero
    u0n[depth + 1] = zero

    def first(z, c):
        u0[z + 1] = w0[jnp.minimum(z, 1)] * b0[z]
        return c

    lax.fori_loop(0, depth, first, 0)
    sweep(u0, u0n, u0.at[pl.ds(1, depth)], al0, be0, depth)

    low, top = 8, span - 8
    pad = r0.shape[2] - span
    for l in range(count):
        for j in range(r0.shape[1]):
            r0[l, j, span : span + pad, :] = jnp.zeros((pad, 128), jnp.float32)
    blocks_out(r0, depth, kh)
    blocks_out(r0, depth + 1, kv)
    k_out[0] = kh[low:top]
    k_out[1] = kv[low:top]

    def rest(z, c):
        b = b0[z]
        blocks_out(r0, z, residual_of(u0n, z, b, b0[depth], b0[depth + 1], 1.0))
        b_out[z] = b[low:top]
        u_out[z] = u0n[z + 1][low:top]
        return c

    lax.fori_loop(0, depth, rest, 0)

    def coarse_rows(ref, l, n):
        return jnp.concatenate(
            [
                ref[l, j, pl.ds(0, n, stride=2), :] + ref[l, j, pl.ds(1, n, stride=2), :]
                for j in range(ref.shape[1])
            ],
            1,
        )

    span1 = r0.shape[2] // 2
    half = cols
    pairs = jnp.concatenate([coarse_rows(r0, l, span1) for l in range(count)], 0)
    b1 = exact_dot(pairs, c1[...]).reshape(count, span1, half)
    b1_out[...] = b1[0:depth]
    k1_out[...] = b1[depth:]
    kh1, kv1 = k1_out[0], k1_out[1]
    weights(
        kh1, kv1, 0.25,
        inside_of((span1, half), tile * (rows // 2) - HX // 2, tiles * (rows // 2), cols // 2, HY // 2),
        w1, al1, be1,
    )
    zero1 = jnp.zeros((span1, half), jnp.float32)
    u1[0] = zero1
    u1[depth + 1] = zero1
    u1n[0] = zero1
    u1n[depth + 1] = zero1

    def first1(z, c):
        u1[z + 1] = w1[jnp.minimum(z, 1)] * b1_out[z]
        return c

    lax.fori_loop(0, depth, first1, 0)
    sweep(u1, u1n, u1.at[pl.ds(1, depth)], al1, be1, depth)

    def rest1(z, c):
        blocks_out(r1, z, residual_of(u1n, z, b1_out[z], k1_out[0], k1_out[1], 0.25))
        u1_out[z] = u1n[z + 1]
        return c

    lax.fori_loop(0, depth, rest1, 0)
    blocks_out(r1, depth, kh1)
    blocks_out(r1, depth + 1, kv1)
    span2 = span1 // 2
    pairs = jnp.concatenate([coarse_rows(r1, l, span2) for l in range(count)], 0)
    b2 = exact_dot(pairs, c2[...]).reshape(count, span2, cols // 2)
    c_out[...] = b2

    own2 = HX // 4
    rows2 = rows // 4
    even = tile % 2 == 0

    def send(out, start):
        for l in range(count):
            out[count + l // 8, l % 8 : l % 8 + 1, :] = c_out[l, start : start + 1, :]
            out[l] = c_out[l, start + 1 : start + HX2, :]

    @pl.when(even)
    def _():
        send(a_msg, own2 - 1)
        send(b_msg, own2)

    @pl.when(jnp.logical_not(even))
    def _():
        send(a_msg, own2)
        send(b_msg, own2 - 1)


def up_kernel(
    c_in, xa, xb, b0, k0, u0, k1, b1, u1, p1, p2,
    potential, residual,
    b2, w2, al2, be2, wb2, u2, u2n, w1, al1, be1, wb1, f1, f1n, w0, al0, be0, wb0, f0, f0n, e1, e0,
):
    count = c_in.shape[0]
    depth = count - 2
    cols = potential.shape[2]
    rows = potential.shape[1]
    rows2 = rows // 4
    tiles = lax.axis_size("tile")
    tile = lax.axis_index("tile")
    y_count = lax.axis_size("strip") * lax.axis_size("sub")
    y = lax.axis_index("strip") * lax.axis_size("sub") + lax.axis_index("sub")
    even = tile % 2 == 0
    own2 = HX // 4
    span2 = b2.shape[1]
    end2 = rows2 + 2 * HX2

    def inside_of(shape, first_row, row_end, own, halo):
        row = first_row + lax.broadcasted_iota(jnp.int32, shape, 0)
        column = lax.broadcasted_iota(jnp.int32, shape, 1)
        right = (column >= own) & (column < own + halo) & (y < y_count - 1)
        left = (column >= shape[1] - halo) & (y > 0)
        return (row >= 0) & (row < row_end) & ((column < own) | right | left)

    def put(x, start):
        for l in range(count):
            b2[l, start : start + 1, :] = x[count + l // 8, l % 8 : l % 8 + 1, :]
            b2[l, start + 1 : start + HX2, :] = x[l]

    @pl.when(even)
    def _():
        put(xa, HX2 + rows2)
        put(xb, 0)

    @pl.when(jnp.logical_not(even))
    def _():
        put(xa, 0)
        put(xb, HX2 + rows2)

    lanes2 = b2.shape[2]
    for l in range(count):
        b2[l, HX2 : HX2 + rows2, :] = c_in[l, own2 : own2 + rows2, :]
        b2[l, end2:span2, :] = jnp.zeros((span2 - end2, lanes2), jnp.float32)
    row = lax.broadcasted_iota(jnp.int32, (span2, lanes2), 0)
    inside2 = inside_of((span2, lanes2), tile * rows2 - HX2, tiles * rows2, cols // 4, (HY - 2) // 4)
    weights(b2[depth], b2[depth + 1], 0.0625, inside2 & (row < end2), w2, al2, be2)

    def zero_ends(ref):
        z = jnp.zeros(ref.shape[1:], jnp.float32)
        ref[0] = z
        ref[depth + 1] = z

    for ref in (u2, u2n, f1, f1n, f0, f0n):
        zero_ends(ref)

    def first2(z, c):
        v = w2[jnp.minimum(z, 1)] * b2[z]
        wb2[z] = v
        u2[z + 1] = v
        return c

    lax.fori_loop(0, depth, first2, 0)
    src, dst = u2, u2n
    for _ in range(COARSE - 1):
        sweep(src, dst, wb2, al2, be2, depth)
        src, dst = dst, src

    span1, lanes1 = u1.shape[1], u1.shape[2]
    kh1, kv1 = k1[0], k1[1]
    weights(
        kh1, kv1, 0.25,
        inside_of((span1, lanes1), tile * (rows // 2) - HX // 2, tiles * (rows // 2), cols // 2, HY // 2),
        w1, al1, be1,
    )
    off2 = HX2 - own2
    coarse = jnp.concatenate([src[z + 1][off2 : off2 + span1 // 2] for z in range(depth)], 0)
    fine = exact_dot(coarse, p2[...])
    for z in range(depth):
        rows_doubled(e1, z, fine[z * (span1 // 2) : (z + 1) * (span1 // 2)])

    def first1(z, c):
        f1[z + 1] = u1[z] + blocks_in(e1, z)
        wb1[z] = w1[jnp.minimum(z, 1)] * b1[z]
        return c

    lax.fori_loop(0, depth, first1, 0)
    sweep(f1, f1n, wb1, al1, be1, depth)
    sweep(f1n, f1, wb1, al1, be1, depth)

    span0, lanes0 = b0.shape[1], b0.shape[2]
    above = (span0 - rows) // 2
    weights(
        k0[0], k0[1], 1.0,
        inside_of((span0, lanes0), tile * rows - above, tiles * rows, cols, HY),
        w0, al0, be0,
    )
    off1 = (HX - above) // 2
    fine = exact_dot(f1[pl.ds(1, depth)].reshape(depth * span1, lanes1), p1[...])
    for z in range(depth):
        rows_doubled(e0, z, fine[z * span1 + off1 : z * span1 + off1 + span0 // 2])

    def first0(z, c):
        f0[z + 1] = u0[z] + blocks_in(e0, z)
        wb0[z] = w0[jnp.minimum(z, 1)] * b0[z]
        return c

    lax.fori_loop(0, depth, first0, 0)
    sweep(f0, f0n, wb0, al0, be0, depth)
    sweep(f0n, f0, wb0, al0, be0, depth)

    def last(z, c):
        r = residual_of(f0, z, b0[z], k0[0], k0[1], 1.0)
        residual[z] = r[above : above + rows, 0:cols]
        potential[z] = f0[z + 1][above : above + rows, 0:cols]
        return c

    lax.fori_loop(0, depth, last, 0)


VM = pl.BlockSpec(memory_space=pltpu.VMEM)


def call(kernel, outs, scratch, *args):
    f32 = lambda shape: jax.ShapeDtypeStruct(shape, jnp.float32)
    return pl.pallas_call(
        kernel,
        out_shape=[f32(s) for s in outs],
        in_specs=[VM] * len(args),
        out_specs=[VM] * len(outs),
        scratch_shapes=[pltpu.VMEM(s, jnp.float32) for s in scratch],
        compiler_params=pltpu.CompilerParams(vmem_limit_bytes=40 << 20),
    )(*args)


def body(right_side, horiz_coef, vert_coef, panel_owner, panel_cell, panel_pressure):
    depth, rows, cols = right_side.shape
    tiles = lax.axis_size("tile")
    y_axes = ("strip", "sub")
    y_count = lax.axis_size("strip") * lax.axis_size("sub")
    count = depth + 2
    span = rows + 2 * HX
    one, two = lane_maps(cols)
    c1 = jnp.asarray(0.25 * selection(one, cols), jnp.bfloat16)
    c2 = jnp.asarray(0.25 * selection(two, cols // 2), jnp.bfloat16)
    p1 = jnp.asarray(selection(one, cols).T, jnp.bfloat16)
    p2 = jnp.asarray(selection(two, cols // 2).T, jnp.bfloat16)

    code = (panel_owner[:, 0] * (rows * cols) + panel_cell).astype(jnp.float32)
    panels = jnp.concatenate([code.reshape(4, -1), panel_pressure.reshape(4, -1)], 0)[None]
    step = 1
    while step < tiles:
        swap = [(i, i ^ step) for i in range(tiles)]
        panels = jnp.concatenate([panels, lax.ppermute(panels, "tile", swap)], 0)
        step *= 2

    message = (count + count // 2, 8, cols)
    a, b = call(pack_rows_kernel, [message] * 2, [], right_side, horiz_coef, vert_coef)
    a = lax.ppermute(a, "tile", edge_pairs(tiles, False))
    b = lax.ppermute(b, "tile", edge_pairs(tiles, True))

    slabs = (count // SLABS, span, 128)
    ext, sub, strip = call(
        forcing_kernel, [(count, span, cols), slabs, slabs], [],
        right_side, horiz_coef, vert_coef, a, b, panels,
    )
    sub = lax.ppermute(sub, y_axes, edge_pairs(y_count, False))
    strip = lax.ppermute(strip, y_axes, edge_pairs(y_count, True))

    lanes = cols + 128
    small = span - 16
    span1 = (span + 8) // 2
    span2 = span1 // 2
    message2 = (count + (count + 7) // 8, 8, cols // 2)
    field = (depth + 2, span, lanes)
    field1 = (depth + 2, span1, cols)
    pair, pair1 = (2, span, lanes), (2, span1, cols)
    b0, k0, u0, k1, b1, u1, c2_own, a2, b2 = call(
        down_kernel,
        [
            (depth, small, lanes), (2, small, lanes), (depth, small, lanes), (2, span1, cols),
            (depth, span1, cols), (depth, span1, cols), (count, span2, cols // 2), message2, message2,
        ],
        [
            (count, span, lanes), field, field, (count, lanes // 128, span + 8, 128), pair, pair, pair,
            pair1, pair1, pair1, field1, field1, (count, cols // 128, span1, 128),
        ],
        ext, sub, strip, c1, c2,
    )
    a2 = lax.ppermute(a2, "tile", edge_pairs(tiles, False))
    b2 = lax.ppermute(b2, "tile", edge_pairs(tiles, True))

    wide2 = 32
    pair2, pair0 = (2, wide2, cols // 2), (2, small, lanes)
    field2 = (depth + 2, wide2, cols // 2)
    field0 = (depth + 2, small, lanes)
    potential, residual = call(
        up_kernel, [right_side.shape, right_side.shape],
        [
            (count, wide2, cols // 2), pair2, pair2, pair2, (depth, wide2, cols // 2), field2, field2,
            pair1, pair1, pair1, (depth, span1, cols), field1, field1,
            pair0, pair0, pair0, (depth, small, lanes), field0, field0,
            (depth, cols // 128, span1, 128), (depth, lanes // 128, small, 128),
        ],
        c2_own, a2, b2, b0, k0, u0, k1, b1, u1, p1, p2,
    )
    return potential, residual


def solution(mesh):
    return jax.shard_map(
        body,
        mesh=mesh,
        in_specs=(
            jax.P("group", "tile", ("strip", "sub")),
            jax.P(("group", "tile"), ("strip", "sub")),
            jax.P(("group", "tile"), ("strip", "sub")),
            jax.P(("group", "tile", "strip", "sub"), None),
            jax.P(("group", "tile", "strip", "sub")),
            jax.P(("group", "tile", "strip", "sub")),
        ),
        out_specs=(
            jax.P("group", "tile", ("strip", "sub")),
            jax.P("group", "tile", ("strip", "sub")),
        ),
        check_vma=False,
    )
```

profile of v0, /device:TPU:10, one launch (start us, length us, event | category | flops | bytes accessed | tf_op | source)
XLA Modules:
  0.0 60.3 jit_solution(13980196919509406488)
XLA Ops:
  0.6 0.0 copy-start.7
  0.6 0.7 %broadcast_multiply_fusion = s32[512,1]{0,1:T(1,128)S(1)} fusion(s32[512,1]{0,1:T(1,128)} %param.13), kind=kLoop, calls=%fused_computation.4 | loop fusion | flops 512 | bytes 4096 | tf_op jit(solution)/shard_map/mul | solution.py:507
  1.3 0.0 copy-done.7
  1.3 0.0 copy-start.8
  1.3 0.7 %copy-done.8 = f32[512]{0:T(512)S(1)} copy-done((f32[512]{0:T(512)S(1)}, f32[512]{0:T(512)}, u32[]{:S(2)}) %copy-start.8) | copy-done | bytes 2072
  2.0 0.4 collective-permute-start.2
  2.5 0.0 copy-start
  2.5 1.0 %copy-done = f32[16,32,256]{2,1,0:T(8,128)S(1)} copy-done((f32[16,32,256]{2,1,0:T(8,128)S(1)}, f32[16,32,256]{2,1,0:T(8,128)}, u32[]{:S(2)}) %copy-start) | copy-done | bytes 524312
  3.5 0.0 copy-start.3
  3.5 0.8 %copy-done.3 = f32[32,256]{1,0:T(8,128)S(1)} copy-done((f32[32,256]{1,0:T(8,128)S(1)}, f32[32,256]{1,0:T(8,128)}, u32[]{:S(2)}) %copy-start.3) | copy-done | bytes 32792
  4.3 0.0 copy-start.4
  4.3 0.8 %copy-done.4 = f32[32,256]{1,0:T(8,128)S(1)} copy-done((f32[32,256]{1,0:T(8,128)S(1)}, f32[32,256]{1,0:T(8,128)}, u32[]{:S(2)}) %copy-start.4) | copy-done | bytes 32792
  5.1 1.6 %collective-permute-start = (f32[27,8,256]{2,1,0:T(8,128)S(1)}, f32[27,8,256]{2,1,0:T(8,128)S(1)}, u32[]{:S(2)}, u32[]{:S(2)}) collective-permute-start(f32[27,8,256]{2,1,0:T(8,128)S(1)} %get-tuple-element.16), channel_id=1, source_target_pairs={{0,4},{4,0},{8,12},{12,8},{1,5},{5,1},{9,13},{13,9},{2,6},{6,2},{1... | collective-permute-start | bytes 663560 | tf_op jit(solution)/shard_map/ppermute | solution.py:517
  6.7 3.5 %collective-permute-start.1 = (f32[27,8,256]{2,1,0:T(8,128)S(1)}, f32[27,8,256]{2,1,0:T(8,128)S(1)}, u32[]{:S(2)}, u32[]{:S(2)}) collective-permute-start(f32[27,8,256]{2,1,0:T(8,128)S(1)} %get-tuple-element.17), channel_id=1, source_target_pairs={{4,8},{8,4},{5,9},{9,5},{6,10},{10,6},{7,11},{11,7},{20,24},{24,20... | collective-permute-start | bytes 663560 | tf_op jit(solution)/shard_map/ppermute | solution.py:518
  10.2 0.0 collective-permute-done.2
  10.2 0.1 collective-permute-start.3
  10.3 4.6 %collective-permute-done.3 = f32[2,8,128]{2,1,0:T(8,128)S(1)} collective-permute-done((f32[2,8,128]{2,1,0:T(8,128)S(1)}, f32[2,8,128]{2,1,0:T(8,128)S(1)}, u32[]{:S(2)}, u32[]{:S(2)}) %collective-permute-start.3) | collective-permute-done | bytes 8224 | tf_op jit(solution)/shard_map/ppermute | solution.py:512
  14.9 0.0 copy-start.1
  15.0 0.0 copy-start.5
  15.0 0.0 collective-permute-done.xa
  15.0 0.5 collective-permute-done.1.xb
  15.5 1.3 %shard_map.114 = (f32[18,56,256]{2,1,0:T(8,128)S(1)}, f32[6,56,128]{2,1,0:T(8,128)S(1)}, f32[6,56,128]{2,1,0:T(8,128)S(1)}) custom-call(f32[16,32,256]{2,1,0:T(8,128)S(1)} %copy-done, f32[32,256]{1,0:T(8,128)S(1)} %copy-done.3, f32[32,256]{1,0:T(8,128)S(1)} %copy-done.4, f32[27,8,256]{2,1,0:T(8,128)S(1)} %collective-permute-done.xa, ...), custom_call_target="tpu_custom_call" | custom-call | tf_op jit(solution)/shard_map/pallas_call | solution.py:484
  16.8 0.1 collective-permute-start.4
  16.8 2.5 %collective-permute-start.5 = (f32[6,56,128]{2,1,0:T(8,128)S(1)}, f32[6,56,128]{2,1,0:T(8,128)S(1)}, u32[]{:S(2)}, u32[]{:S(2)}) collective-permute-start(f32[6,56,128]{2,1,0:T(8,128)S(1)} %get-tuple-element.20), channel_id=1, source_target_pairs={{1,2},{2,1},{5,6},{6,5},{9,10},{10,9},{13,14},{14,13},{17,18},{18,... | collective-permute-start | bytes 516104 | tf_op jit(solution)/shard_map/ppermute | solution.py:526
  19.4 0.0 collective-permute-done.4.ysub
  19.4 4.2 %collective-permute-done.5.ystrip = f32[6,56,128]{2,1,0:T(8,128)S(1)} collective-permute-done((f32[6,56,128]{2,1,0:T(8,128)S(1)}, f32[6,56,128]{2,1,0:T(8,128)S(1)}, u32[]{:S(2)}, u32[]{:S(2)}) %collective-permute-start.5) | collective-permute-done | bytes 172064 | tf_op jit(solution)/shard_map/ppermute | solution.py:526
  23.6 0.0 copy-done.1
  23.6 0.0 copy-done.5
  23.6 0.0 copy-start.2
  23.6 0.0 copy-start.6
  23.6 8.8 %shard_map.115 = (f32[16,40,384]{2,1,0:T(8,128)S(1)}, f32[2,40,384]{2,1,0:T(8,128)S(1)}, f32[16,40,384]{2,1,0:T(8,128)S(1)}, f32[2,32,256]{2,1,0:T(8,128)S(1)}, ...) custom-call(f32[18,56,256]{2,1,0:T(8,128)S(1)} %get-tuple-element.18, ...), custom_call_target="tpu_custom_call" | custom-call | tf_op jit(solution)/shard_map/pallas_call | solution.py:484
  32.4 1.7 %collective-permute-start.6 = (f32[21,8,128]{2,1,0:T(8,128)S(1)}, f32[21,8,128]{2,1,0:T(8,128)S(1)}, u32[]{:S(2)}, u32[]{:S(2)}) collective-permute-start(f32[21,8,128]{2,1,0:T(8,128)S(1)} %get-tuple-element.22), channel_id=1, source_target_pairs={{0,4},{4,0},{8,12},{12,8},{1,5},{5,1},{9,13},{13,9},{2,6},{6,2},{1... | collective-permute-start | bytes 258056 | tf_op jit(solution)/shard_map/ppermute | solution.py:548
  34.1 3.5 %collective-permute-start.7 = (f32[21,8,128]{2,1,0:T(8,128)S(1)}, f32[21,8,128]{2,1,0:T(8,128)S(1)}, u32[]{:S(2)}, u32[]{:S(2)}) collective-permute-start(f32[21,8,128]{2,1,0:T(8,128)S(1)} %get-tuple-element.23), channel_id=1, source_target_pairs={{4,8},{8,4},{5,9},{9,5},{6,10},{10,6},{7,11},{11,7},{20,24},{24,20... | collective-permute-start | bytes 258056 | tf_op jit(solution)/shard_map/ppermute | solution.py:549
  37.6 0.0 collective-permute-done.6.xa
  37.6 2.9 %collective-permute-done.7.xb = f32[21,8,128]{2,1,0:T(8,128)S(1)} collective-permute-done((f32[21,8,128]{2,1,0:T(8,128)S(1)}, f32[21,8,128]{2,1,0:T(8,128)S(1)}, u32[]{:S(2)}, u32[]{:S(2)}) %collective-permute-start.7) | collective-permute-done | bytes 86048 | tf_op jit(solution)/shard_map/ppermute | solution.py:549
  40.5 0.0 copy-done.2
  40.5 0.0 copy-done.6
  40.5 19.8 %shard_map.116 = (f32[16,32,256]{2,1,0:T(8,128)}, f32[16,32,256]{2,1,0:T(8,128)}) custom-call(f32[18,16,128]{2,1,0:T(8,128)S(1)} %get-tuple-element.21.c_in, f32[21,8,128]{2,1,0:T(8,128)S(1)} %collective-permute-done.6.xa, f32[21,8,128]{2,1,0:T(8,128)S(1)} %collective-permute-done.7.xb, f32[16,40,384]{2,1,0:T(8,128)S(1)} %get-tuple-element.24.b0, ...), custom_call_target="tpu_custom_call" | custom-call | tf_op jit(solution)/shard_map/pallas_call | solution.py:484
  (5 shorter events, 0.1 us)
Async XLA Ops:
  0.6 0.7 %copy-start.7 = (s32[512]{0:T(512)S(1)}, s32[512]{0:T(512)}, u32[]{:S(2)}) copy-start(s32[512]{0:T(512)} %param.14) | copy-start | bytes 6148
  1.3 0.7 %copy-start.8 = (f32[512]{0:T(512)S(1)}, f32[512]{0:T(512)}, u32[]{:S(2)}) copy-start(f32[512]{0:T(512)} %param.15) | copy-start | bytes 6148
  2.0 8.2 %collective-permute-start.2 = (f32[1,8,128]{2,1,0:T(8,128)S(1)}, f32[1,8,128]{2,1,0:T(8,128)S(1)}, u32[]{:S(2)}, u32[]{:S(2)}) collective-permute-start(f32[1,8,128]{2,1,0:T(8,128)S(1)} %maximum_bitcast_fusion), channel_id=1, source_target_pairs={{0,4},{4,0},{8,12},{12,8},{1,5},{5,1},{9,13},{13,9},{2,6},{6,2},{1... | collective-permute-start | bytes 12296 | tf_op jit(solution)/shard_map/ppermute | solution.py:512
  2.5 1.0 %copy-start = (f32[16,32,256]{2,1,0:T(8,128)S(1)}, f32[16,32,256]{2,1,0:T(8,128)}, u32[]{:S(2)}) copy-start(f32[16,32,256]{2,1,0:T(8,128)} %rs.3) | copy-start | bytes 1572868
  3.5 0.8 %copy-start.3 = (f32[32,256]{1,0:T(8,128)S(1)}, f32[32,256]{1,0:T(8,128)}, u32[]{:S(2)}) copy-start(f32[32,256]{1,0:T(8,128)} %kh.3) | copy-start | bytes 98308
  4.3 0.8 %copy-start.4 = (f32[32,256]{1,0:T(8,128)S(1)}, f32[32,256]{1,0:T(8,128)}, u32[]{:S(2)}) copy-start(f32[32,256]{1,0:T(8,128)} %kv.3) | copy-start | bytes 98308
  5.1 9.9 %collective-permute-start = (f32[27,8,256]{2,1,0:T(8,128)S(1)}, f32[27,8,256]{2,1,0:T(8,128)S(1)}, u32[]{:S(2)}, u32[]{:S(2)}) collective-permute-start(f32[27,8,256]{2,1,0:T(8,128)S(1)} %get-tuple-element.16), channel_id=1, source_target_pairs={{0,4},{4,0},{8,12},{12,8},{1,5},{5,1},{9,13},{13,9},{2,6},{6,2},{1... | collective-permute-start | bytes 663560 | tf_op jit(solution)/shard_map/ppermute | solution.py:517
  6.7 8.8 %collective-permute-start.1 = (f32[27,8,256]{2,1,0:T(8,128)S(1)}, f32[27,8,256]{2,1,0:T(8,128)S(1)}, u32[]{:S(2)}, u32[]{:S(2)}) collective-permute-start(f32[27,8,256]{2,1,0:T(8,128)S(1)} %get-tuple-element.17), channel_id=1, source_target_pairs={{4,8},{8,4},{5,9},{9,5},{6,10},{10,6},{7,11},{11,7},{20,24},{24,20... | collective-permute-start | bytes 663560 | tf_op jit(solution)/shard_map/ppermute | solution.py:518
  10.2 4.7 %collective-permute-start.3 = (f32[2,8,128]{2,1,0:T(8,128)S(1)}, f32[2,8,128]{2,1,0:T(8,128)S(1)}, u32[]{:S(2)}, u32[]{:S(2)}) collective-permute-start(f32[2,8,128]{2,1,0:T(8,128)S(1)} %pad_maximum_fusion.1), channel_id=1, source_target_pairs={{0,8},{4,12},{8,0},{12,4},{1,9},{5,13},{9,1},{13,5},{2,10},{6,14},... | collective-permute-start | bytes 24584 | tf_op jit(solution)/shard_map/ppermute | solution.py:512
  14.9 8.6 %copy-start.1 = (bf16[384,256]{1,0:T(8,128)(2,1)S(1)}, bf16[384,256]{1,0:T(8,128)(2,1)}, u32[]{:S(2)}) copy-start(bf16[384,256]{1,0:T(8,128)(2,1)} %constant.10.clone.c1) | copy-start | bytes 589828
  15.0 8.6 %copy-start.5 = (bf16[256,128]{1,0:T(8,128)(2,1)S(1)}, bf16[256,128]{1,0:T(8,128)(2,1)}, u32[]{:S(2)}) copy-start(bf16[256,128]{1,0:T(8,128)(2,1)} %constant.11.clone.c2) | copy-start | bytes 196612
  16.8 2.6 %collective-permute-start.4 = (f32[6,56,128]{2,1,0:T(8,128)S(1)}, f32[6,56,128]{2,1,0:T(8,128)S(1)}, u32[]{:S(2)}, u32[]{:S(2)}) collective-permute-start(f32[6,56,128]{2,1,0:T(8,128)S(1)} %get-tuple-element.19), channel_id=1, source_target_pairs={{0,1},{1,0},{2,3},{3,2},{4,5},{5,4},{6,7},{7,6},{8,9},{9,8},{10,11... | collective-permute-start | bytes 516104 | tf_op jit(solution)/shard_map/ppermute | solution.py:525
  16.8 6.7 %collective-permute-start.5 = (f32[6,56,128]{2,1,0:T(8,128)S(1)}, f32[6,56,128]{2,1,0:T(8,128)S(1)}, u32[]{:S(2)}, u32[]{:S(2)}) collective-permute-start(f32[6,56,128]{2,1,0:T(8,128)S(1)} %get-tuple-element.20), channel_id=1, source_target_pairs={{1,2},{2,1},{5,6},{6,5},{9,10},{10,9},{13,14},{14,13},{17,18},{18,... | collective-permute-start | bytes 516104 | tf_op jit(solution)/shard_map/ppermute | solution.py:526
  23.6 16.9 %copy-start.2 = (bf16[256,384]{1,0:T(8,128)(2,1)S(1)}, bf16[256,384]{1,0:T(8,128)(2,1)}, u32[]{:S(2)}) copy-start(bf16[256,384]{1,0:T(8,128)(2,1)} %constant.12.clone.p1) | copy-start | bytes 589828
  23.6 16.9 %copy-start.6 = (bf16[128,256]{1,0:T(8,128)(2,1)S(1)}, bf16[128,256]{1,0:T(8,128)(2,1)}, u32[]{:S(2)}) copy-start(bf16[128,256]{1,0:T(8,128)(2,1)} %constant.13.clone.p2) | copy-start | bytes 196612
  32.4 5.1 %collective-permute-start.6 = (f32[21,8,128]{2,1,0:T(8,128)S(1)}, f32[21,8,128]{2,1,0:T(8,128)S(1)}, u32[]{:S(2)}, u32[]{:S(2)}) collective-permute-start(f32[21,8,128]{2,1,0:T(8,128)S(1)} %get-tuple-element.22), channel_id=1, source_target_pairs={{0,4},{4,0},{8,12},{12,8},{1,5},{5,1},{9,13},{13,9},{2,6},{6,2},{1... | collective-permute-start | bytes 258056 | tf_op jit(solution)/shard_map/ppermute | solution.py:548
  34.1 6.4 %collective-permute-start.7 = (f32[21,8,128]{2,1,0:T(8,128)S(1)}, f32[21,8,128]{2,1,0:T(8,128)S(1)}, u32[]{:S(2)}, u32[]{:S(2)}) collective-permute-start(f32[21,8,128]{2,1,0:T(8,128)S(1)} %get-tuple-element.23), channel_id=1, source_target_pairs={{4,8},{8,4},{5,9},{9,5},{6,10},{10,6},{7,11},{11,7},{20,24},{24,20... | collective-permute-start | bytes 258056 | tf_op jit(solution)/shard_map/ppermute | solution.py:549
where the time goes:
time: 60.7 us; the launch traced here: 60.3 us
  Pallas kernels  30 us (49%)
  starting transfers between devices  13.4 us (22%)
  waiting for transfers between devices  12.2 us (20%)
  local copies, waits for them, and re-layouts  3.25 us (5%)
  between operations  0.75 us (1%)
  other arithmetic  0.71 us (1%)
    pallas_call x4, Pallas kernels, call(): pl.pallas_call(kernel, out_shape=[f32(s) for s in outs], in_specs=[VM] *...  30 us
    ppermute x2, waiting for transfers between devices, body(): panels = jnp.concatenate([panels, lax.ppermute(panels, 'tile', swap)], 0)  4.65 us
    ppermute x1, waiting for transfers between devices, body(): strip = lax.ppermute(strip, y_axes, edge_pairs(y_count, True))  4.18 us
    ppermute x1, starting transfers between devices, body(): b = lax.ppermute(b, 'tile', edge_pairs(tiles, True))  3.47 us
    ppermute x1, starting transfers between devices, body(): b2 = lax.ppermute(b2, 'tile', edge_pairs(tiles, True))  3.45 us
    unnamed x18, local copies, waits for them, and re-layouts  3.25 us
    ppermute x1, waiting for transfers between devices, body(): b2 = lax.ppermute(b2, 'tile', edge_pairs(tiles, True))  2.9 us
    ppermute x1, starting transfers between devices, body(): strip = lax.ppermute(strip, y_axes, edge_pairs(y_count, True))  2.53 us
  transfers between devices with their start and end apart: 8, of which 4 were waited for; matrix products, arithmetic and copies ran while one was open for 0% of the time, Pallas kernels for 0%

commit v1 on v0

--- a/solution.py
+++ b/solution.py
@@ -11,6 +11,7 @@
 HX = 12
 HX2 = 9
 HY = 42
+LIMIT = 512
 SLABS = 3
 
 
@@ -69,6 +70,10 @@
         b_ref[i] = w * kv
 
 
+def loop(depth, fn, vregs):
+    lax.fori_loop(0, depth, fn, 0, unroll=max(1, min(depth, LIMIT // vregs)))
+
+
 def sweep(src, dst, wb, a_ref, b_ref, depth):
     def layer(z, c):
         i = jnp.minimum(z, 1)
@@ -81,7 +86,7 @@
         )
         return c
 
-    lax.fori_loop(0, depth, layer, 0)
+    loop(depth, layer, src.shape[1] * src.shape[2] // 1024)
 
 
 def residual_of(src, z, b, kh, kv, scale):
@@ -266,7 +271,7 @@
         u0[z + 1] = w0[jnp.minimum(z, 1)] * b0[z]
         return c
 
-    lax.fori_loop(0, depth, first, 0)
+    loop(depth, first, 21)
     sweep(u0, u0n, u0.at[pl.ds(1, depth)], al0, be0, depth)
 
     low, top = 8, span - 8
@@ -286,7 +291,7 @@
         u_out[z] = u0n[z + 1][low:top]
         return c
 
-    lax.fori_loop(0, depth, rest, 0)
+    loop(depth, rest, 21)
 
     def coarse_rows(ref, l, n):
         return jnp.concatenate(
@@ -319,7 +324,7 @@
         u1[z + 1] = w1[jnp.minimum(z, 1)] * b1_out[z]
         return c
 
-    lax.fori_loop(0, depth, first1, 0)
+    loop(depth, first1, 8)
     sweep(u1, u1n, u1.at[pl.ds(1, depth)], al1, be1, depth)
 
     def rest1(z, c):
@@ -327,7 +332,7 @@
         u1_out[z] = u1n[z + 1]
         return c
 
-    lax.fori_loop(0, depth, rest1, 0)
+    loop(depth, rest1, 8)
     blocks_out(r1, depth, kh1)
     blocks_out(r1, depth + 1, kv1)
     span2 = span1 // 2
@@ -418,7 +423,7 @@
         u2[z + 1] = v
         return c
 
-    lax.fori_loop(0, depth, first2, 0)
+    loop(depth, first2, 4)
     src, dst = u2, u2n
     for _ in range(COARSE - 1):
         sweep(src, dst, wb2, al2, be2, depth)
@@ -442,7 +447,7 @@
         wb1[z] = w1[jnp.minimum(z, 1)] * b1[z]
         return c
 
-    lax.fori_loop(0, depth, first1, 0)
+    loop(depth, first1, 8)
     sweep(f1, f1n, wb1, al1, be1, depth)
     sweep(f1n, f1, wb1, al1, be1, depth)
 
@@ -463,7 +468,7 @@
         wb0[z] = w0[jnp.minimum(z, 1)] * b0[z]
         return c
 
-    lax.fori_loop(0, depth, first0, 0)
+    loop(depth, first0, 15)
     sweep(f0, f0n, wb0, al0, be0, depth)
     sweep(f0n, f0, wb0, al0, be0, depth)
 
@@ -473,7 +478,7 @@
         potential[z] = f0[z + 1][above : above + rows, 0:cols]
         return c
 
-    lax.fori_loop(0, depth, last, 0)
+    loop(depth, last, 15)
 
 
 VM = pl.BlockSpec(memory_space=pltpu.VMEM)

time: 60.7 us -> 41 us (0.68)
  Pallas kernels: 30 us -> 10.3 us
    pallas_call x4, Pallas kernels: 30 us -> 10.3 us  [call(): pl.pallas_call(kernel, out_shape=[f32(s) for s in outs], in_specs=[VM] *...]
where the time goes in v1:
time: 41 us; the launch traced here: 40.6 us
  starting transfers between devices  13.4 us (33%)
  waiting for transfers between devices  12.2 us (30%)
  Pallas kernels  10.3 us (25%)
  local copies, waits for them, and re-layouts  3.25 us (8%)
  between operations  0.75 us (2%)
  other arithmetic  0.71 us (2%)
    pallas_call x4, Pallas kernels, call(): pl.pallas_call(kernel, out_shape=[f32(s) for s in outs], in_specs=[VM] *...  10.3 us
    ppermute x2, waiting for transfers between devices, body(): panels = jnp.concatenate([panels, lax.ppermute(panels, 'tile', swap)], 0)  4.65 us
    ppermute x1, waiting for transfers between devices, body(): strip = lax.ppermute(strip, y_axes, edge_pairs(y_count, True))  4.18 us
    ppermute x1, starting transfers between devices, body(): b = lax.ppermute(b, 'tile', edge_pairs(tiles, True))  3.47 us
    ppermute x1, starting transfers between devices, body(): b2 = lax.ppermute(b2, 'tile', edge_pairs(tiles, True))  3.46 us
    unnamed x18, local copies, waits for them, and re-layouts  3.25 us
    ppermute x1, waiting for transfers between devices, body(): b2 = lax.ppermute(b2, 'tile', edge_pairs(tiles, True))  2.89 us
    ppermute x1, starting transfers between devices, body(): strip = lax.ppermute(strip, y_axes, edge_pairs(y_count, True))  2.53 us
  transfers between devices with their start and end apart: 8, of which 4 were waited for; matrix products, arithmetic and copies ran while one was open for 0% of the time, Pallas kernels for 0%

profile of v1, /device:TPU:10, one launch (start us, length us, event | category | flops | bytes accessed | tf_op | source)
XLA Modules:
  0.0 40.6 jit_solution(15817327088853230012)
XLA Ops:
  0.6 0.0 copy-start.7
  0.6 0.7 %broadcast_multiply_fusion = s32[512,1]{0,1:T(1,128)S(1)} fusion(s32[512,1]{0,1:T(1,128)} %param.13), kind=kLoop, calls=%fused_computation.4 | loop fusion | flops 512 | bytes 4096 | tf_op jit(solution)/shard_map/mul | solution.py:512
  1.3 0.0 copy-done.7
  1.3 0.0 copy-start.8
  1.3 0.7 %copy-done.8 = f32[512]{0:T(512)S(1)} copy-done((f32[512]{0:T(512)S(1)}, f32[512]{0:T(512)}, u32[]{:S(2)}) %copy-start.8) | copy-done | bytes 2072
  2.0 0.4 %collective-permute-start.2 = (f32[1,8,128]{2,1,0:T(8,128)S(1)}, f32[1,8,128]{2,1,0:T(8,128)S(1)}, u32[]{:S(2)}, u32[]{:S(2)}) collective-permute-start(f32[1,8,128]{2,1,0:T(8,128)S(1)} %maximum_bitcast_fusion), channel_id=1, source_target_pairs={{0,4},{4,0},{8,12},{12,8},{1,5},{5,1},{9,13},{13,9},{2,6},{6,2},{1... | collective-permute-start | bytes 12296 | tf_op jit(solution)/shard_map/ppermute | solution.py:517
  2.5 0.0 copy-start
  2.5 1.0 %copy-done = f32[16,32,256]{2,1,0:T(8,128)S(1)} copy-done((f32[16,32,256]{2,1,0:T(8,128)S(1)}, f32[16,32,256]{2,1,0:T(8,128)}, u32[]{:S(2)}) %copy-start) | copy-done | bytes 524312
  3.5 0.0 copy-start.3
  3.5 0.8 %copy-done.3 = f32[32,256]{1,0:T(8,128)S(1)} copy-done((f32[32,256]{1,0:T(8,128)S(1)}, f32[32,256]{1,0:T(8,128)}, u32[]{:S(2)}) %copy-start.3) | copy-done | bytes 32792
  4.3 0.0 copy-start.4
  4.3 0.8 %copy-done.4 = f32[32,256]{1,0:T(8,128)S(1)} copy-done((f32[32,256]{1,0:T(8,128)S(1)}, f32[32,256]{1,0:T(8,128)}, u32[]{:S(2)}) %copy-start.4) | copy-done | bytes 32792
  5.1 1.6 %collective-permute-start = (f32[27,8,256]{2,1,0:T(8,128)S(1)}, f32[27,8,256]{2,1,0:T(8,128)S(1)}, u32[]{:S(2)}, u32[]{:S(2)}) collective-permute-start(f32[27,8,256]{2,1,0:T(8,128)S(1)} %get-tuple-element.16), channel_id=1, source_target_pairs={{0,4},{4,0},{8,12},{12,8},{1,5},{5,1},{9,13},{13,9},{2,6},{6,2},{1... | collective-permute-start | bytes 663560 | tf_op jit(solution)/shard_map/ppermute | solution.py:522
  6.7 3.5 %collective-permute-start.1 = (f32[27,8,256]{2,1,0:T(8,128)S(1)}, f32[27,8,256]{2,1,0:T(8,128)S(1)}, u32[]{:S(2)}, u32[]{:S(2)}) collective-permute-start(f32[27,8,256]{2,1,0:T(8,128)S(1)} %get-tuple-element.17), channel_id=1, source_target_pairs={{4,8},{8,4},{5,9},{9,5},{6,10},{10,6},{7,11},{11,7},{20,24},{24,20... | collective-permute-start | bytes 663560 | tf_op jit(solution)/shard_map/ppermute | solution.py:523
  10.2 0.0 collective-permute-done.2
  10.2 0.1 collective-permute-start.3
  10.3 4.6 %collective-permute-done.3 = f32[2,8,128]{2,1,0:T(8,128)S(1)} collective-permute-done((f32[2,8,128]{2,1,0:T(8,128)S(1)}, f32[2,8,128]{2,1,0:T(8,128)S(1)}, u32[]{:S(2)}, u32[]{:S(2)}) %collective-permute-start.3) | collective-permute-done | bytes 8224 | tf_op jit(solution)/shard_map/ppermute | solution.py:517
  14.9 0.0 copy-start.1
  15.0 0.0 copy-start.5
  15.0 0.0 collective-permute-done.xa
  15.0 0.5 %collective-permute-done.1.xb = f32[27,8,256]{2,1,0:T(8,128)S(1)} collective-permute-done((f32[27,8,256]{2,1,0:T(8,128)S(1)}, f32[27,8,256]{2,1,0:T(8,128)S(1)}, u32[]{:S(2)}, u32[]{:S(2)}) %collective-permute-start.1) | collective-permute-done | bytes 221216 | tf_op jit(solution)/shard_map/ppermute | solution.py:523
  15.5 1.3 %shard_map.114 = (f32[18,56,256]{2,1,0:T(8,128)S(1)}, f32[6,56,128]{2,1,0:T(8,128)S(1)}, f32[6,56,128]{2,1,0:T(8,128)S(1)}) custom-call(f32[16,32,256]{2,1,0:T(8,128)S(1)} %copy-done, f32[32,256]{1,0:T(8,128)S(1)} %copy-done.3, f32[32,256]{1,0:T(8,128)S(1)} %copy-done.4, f32[27,8,256]{2,1,0:T(8,128)S(1)} %collective-permute-done.xa, ...), custom_call_target="tpu_custom_call" | custom-call | tf_op jit(solution)/shard_map/pallas_call | solution.py:489
  16.8 0.1 collective-permute-start.4
  16.8 2.5 %collective-permute-start.5 = (f32[6,56,128]{2,1,0:T(8,128)S(1)}, f32[6,56,128]{2,1,0:T(8,128)S(1)}, u32[]{:S(2)}, u32[]{:S(2)}) collective-permute-start(f32[6,56,128]{2,1,0:T(8,128)S(1)} %get-tuple-element.20), channel_id=1, source_target_pairs={{1,2},{2,1},{5,6},{6,5},{9,10},{10,9},{13,14},{14,13},{17,18},{18,... | collective-permute-start | bytes 516104 | tf_op jit(solution)/shard_map/ppermute | solution.py:531
  19.4 0.0 collective-permute-done.4.ysub
  19.4 4.2 %collective-permute-done.5.ystrip = f32[6,56,128]{2,1,0:T(8,128)S(1)} collective-permute-done((f32[6,56,128]{2,1,0:T(8,128)S(1)}, f32[6,56,128]{2,1,0:T(8,128)S(1)}, u32[]{:S(2)}, u32[]{:S(2)}) %collective-permute-start.5) | collective-permute-done | bytes 172064 | tf_op jit(solution)/shard_map/ppermute | solution.py:531
  23.6 0.0 copy-done.1
  23.6 0.0 copy-done.5
  23.6 0.0 copy-start.2
  23.6 0.0 copy-start.6
  23.6 3.9 %shard_map.115 = (f32[16,40,384]{2,1,0:T(8,128)S(1)}, f32[2,40,384]{2,1,0:T(8,128)S(1)}, f32[16,40,384]{2,1,0:T(8,128)S(1)}, f32[2,32,256]{2,1,0:T(8,128)S(1)}, ...) custom-call(f32[18,56,256]{2,1,0:T(8,128)S(1)} %get-tuple-element.18, ...), custom_call_target="tpu_custom_call" | custom-call | tf_op jit(solution)/shard_map/pallas_call | solution.py:489
  27.5 1.7 %collective-permute-start.6 = (f32[21,8,128]{2,1,0:T(8,128)S(1)}, f32[21,8,128]{2,1,0:T(8,128)S(1)}, u32[]{:S(2)}, u32[]{:S(2)}) collective-permute-start(f32[21,8,128]{2,1,0:T(8,128)S(1)} %get-tuple-element.22), channel_id=1, source_target_pairs={{0,4},{4,0},{8,12},{12,8},{1,5},{5,1},{9,13},{13,9},{2,6},{6,2},{1... | collective-permute-start | bytes 258056 | tf_op jit(solution)/shard_map/ppermute | solution.py:553
  29.2 3.5 %collective-permute-start.7 = (f32[21,8,128]{2,1,0:T(8,128)S(1)}, f32[21,8,128]{2,1,0:T(8,128)S(1)}, u32[]{:S(2)}, u32[]{:S(2)}) collective-permute-start(f32[21,8,128]{2,1,0:T(8,128)S(1)} %get-tuple-element.23), channel_id=1, source_target_pairs={{4,8},{8,4},{5,9},{9,5},{6,10},{10,6},{7,11},{11,7},{20,24},{24,20... | collective-permute-start | bytes 258056 | tf_op jit(solution)/shard_map/ppermute | solution.py:554
  32.7 0.0 collective-permute-done.6.xa
  32.7 2.9 %collective-permute-done.7.xb = f32[21,8,128]{2,1,0:T(8,128)S(1)} collective-permute-done((f32[21,8,128]{2,1,0:T(8,128)S(1)}, f32[21,8,128]{2,1,0:T(8,128)S(1)}, u32[]{:S(2)}, u32[]{:S(2)}) %collective-permute-start.7) | collective-permute-done | bytes 86048 | tf_op jit(solution)/shard_map/ppermute | solution.py:554
  35.6 0.0 copy-done.2
  35.6 0.0 copy-done.6
  35.6 5.0 %shard_map.116 = (f32[16,32,256]{2,1,0:T(8,128)}, f32[16,32,256]{2,1,0:T(8,128)}) custom-call(f32[18,16,128]{2,1,0:T(8,128)S(1)} %get-tuple-element.21.c_in, f32[21,8,128]{2,1,0:T(8,128)S(1)} %collective-permute-done.6.xa, f32[21,8,128]{2,1,0:T(8,128)S(1)} %collective-permute-done.7.xb, f32[16,40,384]{2,1,0:T(8,128)S(1)} %get-tuple-element.24.b0, ...), custom_call_target="tpu_custom_call" | custom-call | tf_op jit(solution)/shard_map/pallas_call | solution.py:489
  (5 shorter events, 0.1 us)
Async XLA Ops:
  0.6 0.7 %copy-start.7 = (s32[512]{0:T(512)S(1)}, s32[512]{0:T(512)}, u32[]{:S(2)}) copy-start(s32[512]{0:T(512)} %param.14) | copy-start | bytes 6148
  1.3 0.7 %copy-start.8 = (f32[512]{0:T(512)S(1)}, f32[512]{0:T(512)}, u32[]{:S(2)}) copy-start(f32[512]{0:T(512)} %param.15) | copy-start | bytes 6148
  2.0 8.2 %collective-permute-start.2 = (f32[1,8,128]{2,1,0:T(8,128)S(1)}, f32[1,8,128]{2,1,0:T(8,128)S(1)}, u32[]{:S(2)}, u32[]{:S(2)}) collective-permute-start(f32[1,8,128]{2,1,0:T(8,128)S(1)} %maximum_bitcast_fusion), channel_id=1, source_target_pairs={{0,4},{4,0},{8,12},{12,8},{1,5},{5,1},{9,13},{13,9},{2,6},{6,2},{1... | collective-permute-start | bytes 12296 | tf_op jit(solution)/shard_map/ppermute | solution.py:517
  2.5 1.0 %copy-start = (f32[16,32,256]{2,1,0:T(8,128)S(1)}, f32[16,32,256]{2,1,0:T(8,128)}, u32[]{:S(2)}) copy-start(f32[16,32,256]{2,1,0:T(8,128)} %rs.3) | copy-start | bytes 1572868
  3.5 0.8 %copy-start.3 = (f32[32,256]{1,0:T(8,128)S(1)}, f32[32,256]{1,0:T(8,128)}, u32[]{:S(2)}) copy-start(f32[32,256]{1,0:T(8,128)} %kh.3) | copy-start | bytes 98308
  4.3 0.8 %copy-start.4 = (f32[32,256]{1,0:T(8,128)S(1)}, f32[32,256]{1,0:T(8,128)}, u32[]{:S(2)}) copy-start(f32[32,256]{1,0:T(8,128)} %kv.3) | copy-start | bytes 98308
  5.1 9.9 %collective-permute-start = (f32[27,8,256]{2,1,0:T(8,128)S(1)}, f32[27,8,256]{2,1,0:T(8,128)S(1)}, u32[]{:S(2)}, u32[]{:S(2)}) collective-permute-start(f32[27,8,256]{2,1,0:T(8,128)S(1)} %get-tuple-element.16), channel_id=1, source_target_pairs={{0,4},{4,0},{8,12},{12,8},{1,5},{5,1},{9,13},{13,9},{2,6},{6,2},{1... | collective-permute-start | bytes 663560 | tf_op jit(solution)/shard_map/ppermute | solution.py:522
  6.7 8.8 %collective-permute-start.1 = (f32[27,8,256]{2,1,0:T(8,128)S(1)}, f32[27,8,256]{2,1,0:T(8,128)S(1)}, u32[]{:S(2)}, u32[]{:S(2)}) collective-permute-start(f32[27,8,256]{2,1,0:T(8,128)S(1)} %get-tuple-element.17), channel_id=1, source_target_pairs={{4,8},{8,4},{5,9},{9,5},{6,10},{10,6},{7,11},{11,7},{20,24},{24,20... | collective-permute-start | bytes 663560 | tf_op jit(solution)/shard_map/ppermute | solution.py:523
  10.2 4.7 %collective-permute-start.3 = (f32[2,8,128]{2,1,0:T(8,128)S(1)}, f32[2,8,128]{2,1,0:T(8,128)S(1)}, u32[]{:S(2)}, u32[]{:S(2)}) collective-permute-start(f32[2,8,128]{2,1,0:T(8,128)S(1)} %pad_maximum_fusion.1), channel_id=1, source_target_pairs={{0,8},{4,12},{8,0},{12,4},{1,9},{5,13},{9,1},{13,5},{2,10},{6,14},... | collective-permute-start | bytes 24584 | tf_op jit(solution)/shard_map/ppermute | solution.py:517
  14.9 8.6 %copy-start.1 = (bf16[384,256]{1,0:T(8,128)(2,1)S(1)}, bf16[384,256]{1,0:T(8,128)(2,1)}, u32[]{:S(2)}) copy-start(bf16[384,256]{1,0:T(8,128)(2,1)} %constant.10.clone.c1) | copy-start | bytes 589828
  15.0 8.6 %copy-start.5 = (bf16[256,128]{1,0:T(8,128)(2,1)S(1)}, bf16[256,128]{1,0:T(8,128)(2,1)}, u32[]{:S(2)}) copy-start(bf16[256,128]{1,0:T(8,128)(2,1)} %constant.11.clone.c2) | copy-start | bytes 196612
  16.8 2.6 %collective-permute-start.4 = (f32[6,56,128]{2,1,0:T(8,128)S(1)}, f32[6,56,128]{2,1,0:T(8,128)S(1)}, u32[]{:S(2)}, u32[]{:S(2)}) collective-permute-start(f32[6,56,128]{2,1,0:T(8,128)S(1)} %get-tuple-element.19), channel_id=1, source_target_pairs={{0,1},{1,0},{2,3},{3,2},{4,5},{5,4},{6,7},{7,6},{8,9},{9,8},{10,11... | collective-permute-start | bytes 516104 | tf_op jit(solution)/shard_map/ppermute | solution.py:530
  16.8 6.7 %collective-permute-start.5 = (f32[6,56,128]{2,1,0:T(8,128)S(1)}, f32[6,56,128]{2,1,0:T(8,128)S(1)}, u32[]{:S(2)}, u32[]{:S(2)}) collective-permute-start(f32[6,56,128]{2,1,0:T(8,128)S(1)} %get-tuple-element.20), channel_id=1, source_target_pairs={{1,2},{2,1},{5,6},{6,5},{9,10},{10,9},{13,14},{14,13},{17,18},{18,... | collective-permute-start | bytes 516104 | tf_op jit(solution)/shard_map/ppermute | solution.py:531
  23.6 12.0 %copy-start.2 = (bf16[256,384]{1,0:T(8,128)(2,1)S(1)}, bf16[256,384]{1,0:T(8,128)(2,1)}, u32[]{:S(2)}) copy-start(bf16[256,384]{1,0:T(8,128)(2,1)} %constant.12.clone.p1) | copy-start | bytes 589828
  23.6 12.0 %copy-start.6 = (bf16[128,256]{1,0:T(8,128)(2,1)S(1)}, bf16[128,256]{1,0:T(8,128)(2,1)}, u32[]{:S(2)}) copy-start(bf16[128,256]{1,0:T(8,128)(2,1)} %constant.13.clone.p2) | copy-start | bytes 196612
  27.5 5.1 %collective-permute-start.6 = (f32[21,8,128]{2,1,0:T(8,128)S(1)}, f32[21,8,128]{2,1,0:T(8,128)S(1)}, u32[]{:S(2)}, u32[]{:S(2)}) collective-permute-start(f32[21,8,128]{2,1,0:T(8,128)S(1)} %get-tuple-element.22), channel_id=1, source_target_pairs={{0,4},{4,0},{8,12},{12,8},{1,5},{5,1},{9,13},{13,9},{2,6},{6,2},{1... | collective-permute-start | bytes 258056 | tf_op jit(solution)/shard_map/ppermute | solution.py:553
  29.2 6.4 %collective-permute-start.7 = (f32[21,8,128]{2,1,0:T(8,128)S(1)}, f32[21,8,128]{2,1,0:T(8,128)S(1)}, u32[]{:S(2)}, u32[]{:S(2)}) collective-permute-start(f32[21,8,128]{2,1,0:T(8,128)S(1)} %get-tuple-element.23), channel_id=1, source_target_pairs={{4,8},{8,4},{5,9},{9,5},{6,10},{10,6},{7,11},{11,7},{20,24},{24,20... | collective-permute-start | bytes 258056 | tf_op jit(solution)/shard_map/ppermute | solution.py:554

commit v2 on v1

--- a/solution.py
+++ b/solution.py
@@ -41,13 +41,16 @@
     return (lanes[:, None] == np.arange(width)[None, :]).astype(np.float32)
 
 
+def split(x, parts):
+    out = []
+    for _ in range(parts):
+        out.append(x.astype(jnp.bfloat16))
+        x = x - out[-1].astype(jnp.float32)
+    return out
+
+
 def exact_dot(left, right):
-    high = left.astype(jnp.bfloat16)
-    rest = left - high.astype(jnp.float32)
-    mid = rest.astype(jnp.bfloat16)
-    low = (rest - mid.astype(jnp.float32)).astype(jnp.bfloat16)
-    dot = lambda part: jnp.dot(part, right, preferred_element_type=jnp.float32)
-    return dot(high) + dot(mid) + dot(low)
+    return sum(jnp.dot(part, right, preferred_element_type=jnp.float32) for part in split(left, 2))
 
 
 def neighbours(u):
@@ -111,27 +114,39 @@
             ref[l, j, pl.ds(s, n, stride=2), :] = part[:, 128 * j : 128 * (j + 1)]
 
 
-def pack_rows_kernel(rs, kh, kv, a_out, b_out):
-    depth, rows, _ = rs.shape
-    even = lax.axis_index("tile") % 2 == 0
-
-    def layer(l):
-        return rs[l] if l < depth else (kh[...] if l == depth else kv[...])
-
+def load_kernel(rs, kh, kv, owner, cell, pressure, x, panels, a_out, b_out, ints, sems):
+    depth, rows, cols = rs.shape
     count = depth + 2
     half = count // 2
+    even = lax.axis_index("tile") % 2 == 0
+    copies = [
+        pltpu.make_async_copy(src, dst, sems.at[i])
+        for i, (src, dst) in enumerate(
+            (
+                (owner, ints.at[0]),
+                (cell, ints.at[1]),
+                (pressure, panels.at[0, pl.ds(4, 4)]),
+                (rs, x.at[pl.ds(0, depth)]),
+                (kh, x.at[depth]),
+                (kv, x.at[depth + 1]),
+            )
+        )
+    ]
+    for copy in copies:
+        copy.start()
+    for copy in copies:
+        copy.wait()
+    panels[0, 0:4, :] = (ints[0] * (rows * cols) + ints[1]).astype(jnp.float32)
 
     def first(out):
         for l in range(count):
-            x = layer(l)
-            out[l] = x[0:8]
-            out[count + l % half, 4 * (l // half) : 4 * (l // half) + 4, :] = x[8:HX]
+            out[l] = x[l, 0:8, :]
+            out[count + l % half, 4 * (l // half) : 4 * (l // half) + 4, :] = x[l, 8:HX, :]
 
     def last(out):
         for l in range(count):
-            x = layer(l)
-            out[l] = x[rows - 8 : rows]
-            out[count + l % half, 4 * (l // half) : 4 * (l // half) + 4, :] = x[rows - HX : rows - 8]
+            out[l] = x[l, rows - 8 : rows, :]
+            out[count + l % half, 4 * (l // half) : 4 * (l // half) + 4, :] = x[l, rows - HX : rows - 8, :]
 
     @pl.when(even)
     def _():
@@ -144,9 +159,9 @@
         last(b_out)
 
 
-def forcing_kernel(rs, kh, kv, xa, xb, panels, ext, sub_out, strip_out):
-    depth, rows, cols = rs.shape
-    count = depth + 2
+def forcing_kernel(x_own, xa, xb, panels, ext, sub_out, strip_out):
+    count, rows, cols = x_own.shape
+    depth = count - 2
     half = count // 2
     tile = lax.axis_index("tile")
     even = tile % 2 == 0
@@ -172,18 +187,16 @@
         upper(xa)
         lower(xb)
 
-    for l in range(depth):
-        ext[l, HX:high, :] = rs[l]
-    ext[depth, HX:high, :] = kh[...]
-    ext[depth + 1, HX:high, :] = kv[...]
+    for l in range(count):
+        ext[l, HX:high, :] = x_own[l]
 
     span = rows + 2 * HX
-    total = jnp.zeros((span, cols), jnp.float32)
     left, right = [], []
     for g in range(panels.shape[0]):
+        group = panels[g]
         for k in range(4):
-            code = panels[g, k : k + 1, :].astype(jnp.int32)
-            value = panels[g, 4 + k : 5 + k, :]
+            code = group[k : k + 1].astype(jnp.int32)
+            value = group[4 + k : 5 + k]
             row = code // cols - (tile * rows - HX)
             col = code % cols
             hit = row == lax.broadcasted_iota(jnp.int32, (span, 128), 0)
@@ -193,14 +206,10 @@
             )
     left = jnp.concatenate(left, 1)
     right = jnp.concatenate(right, 1)
-    high_part = left.astype(jnp.bfloat16)
-    rest = left - high_part.astype(jnp.float32)
-    mid_part = rest.astype(jnp.bfloat16)
-    low_part = (rest - mid_part.astype(jnp.float32)).astype(jnp.bfloat16)
-    for part in (high_part, mid_part, low_part):
-        total = total + lax.dot_general(
-            part, right, (((1,), (1,)), ((), ())), preferred_element_type=jnp.float32
-        )
+    parts = lax.dot_general(
+        jnp.concatenate(split(left, 3), 0), right, (((1,), (1,)), ((), ())), preferred_element_type=jnp.float32
+    )
+    total = parts[0:span] + parts[span : 2 * span] + parts[2 * span :]
     ext[depth - 1] = ext[depth - 1] + total
 
     y = lax.axis_index("strip") * lax.axis_size("sub") + lax.axis_index("sub")
@@ -509,23 +518,38 @@
     p1 = jnp.asarray(selection(one, cols).T, jnp.bfloat16)
     p2 = jnp.asarray(selection(two, cols // 2).T, jnp.bfloat16)
 
-    code = (panel_owner[:, 0] * (rows * cols) + panel_cell).astype(jnp.float32)
-    panels = jnp.concatenate([code.reshape(4, -1), panel_pressure.reshape(4, -1)], 0)[None]
-    step = 1
+    message = (count + count // 2, 8, cols)
+    f32 = lambda shape: jax.ShapeDtypeStruct(shape, jnp.float32)
+    x_own, panels, a, b = pl.pallas_call(
+        load_kernel,
+        out_shape=[f32((count, rows, cols)), f32((1, 8, 128)), f32(message), f32(message)],
+        in_specs=[pl.BlockSpec(memory_space=pltpu.HBM)] * 6,
+        out_specs=[VM] * 4,
+        scratch_shapes=[pltpu.VMEM((2, 4, 128), jnp.int32), pltpu.SemaphoreType.DMA((6,))],
+        compiler_params=pltpu.CompilerParams(vmem_limit_bytes=8 << 20),
+    )(
+        *[
+            pltpu.with_memory_space_constraint(x, pltpu.HBM)
+            for x in (
+                right_side, horiz_coef, vert_coef,
+                panel_owner.reshape(4, -1), panel_cell.reshape(4, -1), panel_pressure.reshape(4, -1),
+            )
+        ]
+    )
+    near = lax.ppermute(panels, "tile", [(i, i ^ 1) for i in range(tiles)])
+    a = lax.ppermute(a, "tile", edge_pairs(tiles, False))
+    b = lax.ppermute(b, "tile", edge_pairs(tiles, True))
+    panels = jnp.concatenate([panels, near], 0)
+    step = 2
     while step < tiles:
         swap = [(i, i ^ step) for i in range(tiles)]
         panels = jnp.concatenate([panels, lax.ppermute(panels, "tile", swap)], 0)
         step *= 2
 
-    message = (count + count // 2, 8, cols)
-    a, b = call(pack_rows_kernel, [message] * 2, [], right_side, horiz_coef, vert_coef)
-    a = lax.ppermute(a, "tile", edge_pairs(tiles, False))
-    b = lax.ppermute(b, "tile", edge_pairs(tiles, True))
-
     slabs = (count // SLABS, span, 128)
     ext, sub, strip = call(
         forcing_kernel, [(count, span, cols), slabs, slabs], [],
-        right_side, horiz_coef, vert_coef, a, b, panels,
+        x_own, a, b, panels,
     )
     sub = lax.ppermute(sub, y_axes, edge_pairs(y_count, False))
     strip = lax.ppermute(strip, y_axes, edge_pairs(y_count, True))

time: 41 us -> 36.9 us (0.90)
  local copies, waits for them, and re-layouts: 3.25 us -> 0.01 us
  other arithmetic: 0.71 us -> 0.01 us
  starting transfers between devices: 13.4 us -> 14 us
  waiting for transfers between devices: 12.2 us -> 11.6 us
    unnamed x18 -> x8, local copies, waits for them, and re-layouts: 3.25 us -> 0.01 us
    pallas_call x0 -> x1, Pallas kernels: none -> 1.19 us  [body(): pl.pallas_call(load_kernel, out_shape=[f32((count, rows, cols)), f32((1,...]
    pallas_call x4 -> x3, Pallas kernels: 10.3 us -> 9.11 us  [call(): pl.pallas_call(kernel, out_shape=[f32(s) for s in outs], in_specs=[VM] *...]
    mul x1 -> x0, other arithmetic: 0.69 us -> none  [body(): code = (panel_owner[:, 0] * (rows * cols) + panel_cell).astype(jnp.float32)]
    ppermute x2 -> x1, waiting for transfers between devices: 4.65 us -> 4.01 us  [body(): panels = jnp.concatenate([panels, lax.ppermute(panels, 'tile', swap)], 0)]
    ppermute x0 -> x1, starting transfers between devices: none -> 0.51 us  [body(): near = lax.ppermute(panels, 'tile', [(i, i ^ 1) for i in range(tiles)])]
where the time goes in v2:
time: 36.9 us; the launch traced here: 36.7 us
  starting transfers between devices  14 us (38%)
  waiting for transfers between devices  11.6 us (31%)
  Pallas kernels  10.3 us (28%)
  between operations  0.73 us (2%)
    pallas_call x3, Pallas kernels, call(): pl.pallas_call(kernel, out_shape=[f32(s) for s in outs], in_specs=[VM] *...  9.11 us
    ppermute x1, waiting for transfers between devices, body(): strip = lax.ppermute(strip, y_axes, edge_pairs(y_count, True))  4.18 us
    ppermute x1, waiting for transfers between devices, body(): panels = jnp.concatenate([panels, lax.ppermute(panels, 'tile', swap)], 0)  4.01 us
    ppermute x1, starting transfers between devices, body(): b = lax.ppermute(b, 'tile', edge_pairs(tiles, True))  3.47 us
    ppermute x1, starting transfers between devices, body(): b2 = lax.ppermute(b2, 'tile', edge_pairs(tiles, True))  3.46 us
    ppermute x1, waiting for transfers between devices, body(): b2 = lax.ppermute(b2, 'tile', edge_pairs(tiles, True))  2.89 us
    ppermute x1, starting transfers between devices, body(): strip = lax.ppermute(strip, y_axes, edge_pairs(y_count, True))  2.53 us
    ppermute x1, starting transfers between devices, body(): a2 = lax.ppermute(a2, 'tile', edge_pairs(tiles, False))  1.68 us
  transfers between devices with their start and end apart: 8, of which 4 were waited for; matrix products, arithmetic and copies ran while one was open for 0% of the time, Pallas kernels for 0%

profile of v2, /device:TPU:10, one launch (start us, length us, event | category | flops | bytes accessed | tf_op | source)
XLA Modules:
  0.0 36.7 jit_solution(17772236033450498449)
XLA Ops:
  0.6 1.2 %shard_map.113 = (f32[18,32,256]{2,1,0:T(8,128)S(1)}, f32[1,8,128]{2,1,0:T(8,128)S(1)}, f32[27,8,256]{2,1,0:T(8,128)S(1)}, f32[27,8,256]{2,1,0:T(8,128)S(1)}) custom-call(f32[16,32,256]{2,1,0:T(8,128)} %rs.1, f32[32,256]{1,0:T(8,128)} %kh.1, f32[32,256]{1,0:T(8,128)} %kv.1, s32[4,128]{1,0:T(4,128)} %bitcast.3, s32[4,128]{1,0:T(4,128)} %bitcast.4, ...), custom_call_target="tpu_custom_call" | custom-call | tf_op jit(solution)/shard_map/pallas_call | solution.py:523
  1.8 0.5 %collective-permute-start.2 = (f32[1,8,128]{2,1,0:T(8,128)S(1)}, f32[1,8,128]{2,1,0:T(8,128)S(1)}, u32[]{:S(2)}, u32[]{:S(2)}) collective-permute-start(f32[1,8,128]{2,1,0:T(8,128)S(1)} %get-tuple-element.21), channel_id=1, source_target_pairs={{0,4},{4,0},{8,12},{12,8},{1,5},{5,1},{9,13},{13,9},{2,6},{6,2},{1... | collective-permute-start | bytes 12296 | tf_op jit(solution)/shard_map/ppermute | solution.py:539
  2.3 1.6 %collective-permute-start = (f32[27,8,256]{2,1,0:T(8,128)S(1)}, f32[27,8,256]{2,1,0:T(8,128)S(1)}, u32[]{:S(2)}, u32[]{:S(2)}) collective-permute-start(f32[27,8,256]{2,1,0:T(8,128)S(1)} %get-tuple-element.19), channel_id=1, source_target_pairs={{0,4},{4,0},{8,12},{12,8},{1,5},{5,1},{9,13},{13,9},{2,6},{6,2},{1... | collective-permute-start | bytes 663560 | tf_op jit(solution)/shard_map/ppermute | solution.py:540
  3.9 3.5 %collective-permute-start.1 = (f32[27,8,256]{2,1,0:T(8,128)S(1)}, f32[27,8,256]{2,1,0:T(8,128)S(1)}, u32[]{:S(2)}, u32[]{:S(2)}) collective-permute-start(f32[27,8,256]{2,1,0:T(8,128)S(1)} %get-tuple-element.20), channel_id=1, source_target_pairs={{4,8},{8,4},{5,9},{9,5},{6,10},{10,6},{7,11},{11,7},{20,24},{24,20... | collective-permute-start | bytes 663560 | tf_op jit(solution)/shard_map/ppermute | solution.py:541
  7.4 0.0 collective-permute-done.2
  7.4 0.7 %collective-permute-start.3 = (f32[2,8,128]{2,1,0:T(8,128)S(1)}, f32[2,8,128]{2,1,0:T(8,128)S(1)}, u32[]{:S(2)}, u32[]{:S(2)}) collective-permute-start(f32[2,8,128]{2,1,0:T(8,128)S(1)} %pad_maximum_fusion.1), channel_id=1, source_target_pairs={{0,8},{4,12},{8,0},{12,4},{1,9},{5,13},{9,1},{13,5},{2,10},{6,14},... | collective-permute-start | bytes 24584 | tf_op jit(solution)/shard_map/ppermute | solution.py:546
  8.1 4.0 %collective-permute-done.3 = f32[2,8,128]{2,1,0:T(8,128)S(1)} collective-permute-done((f32[2,8,128]{2,1,0:T(8,128)S(1)}, f32[2,8,128]{2,1,0:T(8,128)S(1)}, u32[]{:S(2)}, u32[]{:S(2)}) %collective-permute-start.3) | collective-permute-done | bytes 8224 | tf_op jit(solution)/shard_map/ppermute | solution.py:546
  12.1 0.0 collective-permute-done.xa
  12.2 0.5 %collective-permute-done.1.xb = f32[27,8,256]{2,1,0:T(8,128)S(1)} collective-permute-done((f32[27,8,256]{2,1,0:T(8,128)S(1)}, f32[27,8,256]{2,1,0:T(8,128)S(1)}, u32[]{:S(2)}, u32[]{:S(2)}) %collective-permute-start.1) | collective-permute-done | bytes 221216 | tf_op jit(solution)/shard_map/ppermute | solution.py:541
  12.7 0.0 copy-start
  12.7 0.0 copy-start.2
  12.7 0.8 %shard_map.114 = (f32[18,56,256]{2,1,0:T(8,128)S(1)}, f32[6,56,128]{2,1,0:T(8,128)S(1)}, f32[6,56,128]{2,1,0:T(8,128)S(1)}) custom-call(f32[18,32,256]{2,1,0:T(8,128)S(1)} %get-tuple-element.18.x_own, f32[27,8,256]{2,1,0:T(8,128)S(1)} %collective-permute-done.xa, f32[27,8,256]{2,1,0:T(8,128)S(1)} %collective-permute-done.1.xb, ...), custom_call_target="tpu_custom_call" | custom-call | tf_op jit(solution)/shard_map/pallas_call | solution.py:498
  13.4 0.1 collective-permute-start.4
  13.5 2.5 %collective-permute-start.5 = (f32[6,56,128]{2,1,0:T(8,128)S(1)}, f32[6,56,128]{2,1,0:T(8,128)S(1)}, u32[]{:S(2)}, u32[]{:S(2)}) collective-permute-start(f32[6,56,128]{2,1,0:T(8,128)S(1)} %get-tuple-element.24), channel_id=1, source_target_pairs={{1,2},{2,1},{5,6},{6,5},{9,10},{10,9},{13,14},{14,13},{17,18},{18,... | collective-permute-start | bytes 516104 | tf_op jit(solution)/shard_map/ppermute | solution.py:555
  16.1 0.0 collective-permute-done.4.ysub
  16.1 4.2 %collective-permute-done.5.ystrip = f32[6,56,128]{2,1,0:T(8,128)S(1)} collective-permute-done((f32[6,56,128]{2,1,0:T(8,128)S(1)}, f32[6,56,128]{2,1,0:T(8,128)S(1)}, u32[]{:S(2)}, u32[]{:S(2)}) %collective-permute-start.5) | collective-permute-done | bytes 172064 | tf_op jit(solution)/shard_map/ppermute | solution.py:555
  20.3 0.0 copy-done
  20.3 0.0 copy-done.2
  20.3 0.0 copy-start.1
  20.3 0.0 copy-start.3
  20.3 3.7 %shard_map.115 = (f32[16,40,384]{2,1,0:T(8,128)S(1)}, f32[2,40,384]{2,1,0:T(8,128)S(1)}, f32[16,40,384]{2,1,0:T(8,128)S(1)}, f32[2,32,256]{2,1,0:T(8,128)S(1)}, ...) custom-call(f32[18,56,256]{2,1,0:T(8,128)S(1)} %get-tuple-element.22, ...), custom_call_target="tpu_custom_call" | custom-call | tf_op jit(solution)/shard_map/pallas_call | solution.py:498
  24.0 1.7 %collective-permute-start.6 = (f32[21,8,128]{2,1,0:T(8,128)S(1)}, f32[21,8,128]{2,1,0:T(8,128)S(1)}, u32[]{:S(2)}, u32[]{:S(2)}) collective-permute-start(f32[21,8,128]{2,1,0:T(8,128)S(1)} %get-tuple-element.26), channel_id=1, source_target_pairs={{0,4},{4,0},{8,12},{12,8},{1,5},{5,1},{9,13},{13,9},{2,6},{6,2},{1... | collective-permute-start | bytes 258056 | tf_op jit(solution)/shard_map/ppermute | solution.py:577
  25.7 3.5 %collective-permute-start.7 = (f32[21,8,128]{2,1,0:T(8,128)S(1)}, f32[21,8,128]{2,1,0:T(8,128)S(1)}, u32[]{:S(2)}, u32[]{:S(2)}) collective-permute-start(f32[21,8,128]{2,1,0:T(8,128)S(1)} %get-tuple-element.27), channel_id=1, source_target_pairs={{4,8},{8,4},{5,9},{9,5},{6,10},{10,6},{7,11},{11,7},{20,24},{24,20... | collective-permute-start | bytes 258056 | tf_op jit(solution)/shard_map/ppermute | solution.py:578
  29.1 0.0 collective-permute-done.6.xa
  29.1 2.9 %collective-permute-done.7.xb = f32[21,8,128]{2,1,0:T(8,128)S(1)} collective-permute-done((f32[21,8,128]{2,1,0:T(8,128)S(1)}, f32[21,8,128]{2,1,0:T(8,128)S(1)}, u32[]{:S(2)}, u32[]{:S(2)}) %collective-permute-start.7) | collective-permute-done | bytes 86048 | tf_op jit(solution)/shard_map/ppermute | solution.py:578
  32.0 0.0 copy-done.1
  32.0 0.0 copy-done.3
  32.0 4.6 %shard_map.116 = (f32[16,32,256]{2,1,0:T(8,128)}, f32[16,32,256]{2,1,0:T(8,128)}) custom-call(f32[18,16,128]{2,1,0:T(8,128)S(1)} %get-tuple-element.25.c_in, f32[21,8,128]{2,1,0:T(8,128)S(1)} %collective-permute-done.6.xa, f32[21,8,128]{2,1,0:T(8,128)S(1)} %collective-permute-done.7.xb, f32[16,40,384]{2,1,0:T(8,128)S(1)} %get-tuple-element.28.b0, ...), custom_call_target="tpu_custom_call" | custom-call | tf_op jit(solution)/shard_map/pallas_call | solution.py:498
  (2 shorter events, 0.0 us)
Async XLA Ops:
  1.8 5.6 %collective-permute-start.2 = (f32[1,8,128]{2,1,0:T(8,128)S(1)}, f32[1,8,128]{2,1,0:T(8,128)S(1)}, u32[]{:S(2)}, u32[]{:S(2)}) collective-permute-start(f32[1,8,128]{2,1,0:T(8,128)S(1)} %get-tuple-element.21), channel_id=1, source_target_pairs={{0,4},{4,0},{8,12},{12,8},{1,5},{5,1},{9,13},{13,9},{2,6},{6,2},{1... | collective-permute-start | bytes 12296 | tf_op jit(solution)/shard_map/ppermute | solution.py:539
  2.3 9.8 %collective-permute-start = (f32[27,8,256]{2,1,0:T(8,128)S(1)}, f32[27,8,256]{2,1,0:T(8,128)S(1)}, u32[]{:S(2)}, u32[]{:S(2)}) collective-permute-start(f32[27,8,256]{2,1,0:T(8,128)S(1)} %get-tuple-element.19), channel_id=1, source_target_pairs={{0,4},{4,0},{8,12},{12,8},{1,5},{5,1},{9,13},{13,9},{2,6},{6,2},{1... | collective-permute-start | bytes 663560 | tf_op jit(solution)/shard_map/ppermute | solution.py:540
  3.9 8.8 %collective-permute-start.1 = (f32[27,8,256]{2,1,0:T(8,128)S(1)}, f32[27,8,256]{2,1,0:T(8,128)S(1)}, u32[]{:S(2)}, u32[]{:S(2)}) collective-permute-start(f32[27,8,256]{2,1,0:T(8,128)S(1)} %get-tuple-element.20), channel_id=1, source_target_pairs={{4,8},{8,4},{5,9},{9,5},{6,10},{10,6},{7,11},{11,7},{20,24},{24,20... | collective-permute-start | bytes 663560 | tf_op jit(solution)/shard_map/ppermute | solution.py:541
  7.4 4.7 %collective-permute-start.3 = (f32[2,8,128]{2,1,0:T(8,128)S(1)}, f32[2,8,128]{2,1,0:T(8,128)S(1)}, u32[]{:S(2)}, u32[]{:S(2)}) collective-permute-start(f32[2,8,128]{2,1,0:T(8,128)S(1)} %pad_maximum_fusion.1), channel_id=1, source_target_pairs={{0,8},{4,12},{8,0},{12,4},{1,9},{5,13},{9,1},{13,5},{2,10},{6,14},... | collective-permute-start | bytes 24584 | tf_op jit(solution)/shard_map/ppermute | solution.py:546
  12.7 7.6 %copy-start = (bf16[384,256]{1,0:T(8,128)(2,1)S(1)}, bf16[384,256]{1,0:T(8,128)(2,1)}, u32[]{:S(2)}) copy-start(bf16[384,256]{1,0:T(8,128)(2,1)} %constant.8.clone.c1) | copy-start | bytes 589828
  12.7 7.6 %copy-start.2 = (bf16[256,128]{1,0:T(8,128)(2,1)S(1)}, bf16[256,128]{1,0:T(8,128)(2,1)}, u32[]{:S(2)}) copy-start(bf16[256,128]{1,0:T(8,128)(2,1)} %constant.9.clone.c2) | copy-start | bytes 196612
  13.4 2.6 %collective-permute-start.4 = (f32[6,56,128]{2,1,0:T(8,128)S(1)}, f32[6,56,128]{2,1,0:T(8,128)S(1)}, u32[]{:S(2)}, u32[]{:S(2)}) collective-permute-start(f32[6,56,128]{2,1,0:T(8,128)S(1)} %get-tuple-element.23), channel_id=1, source_target_pairs={{0,1},{1,0},{2,3},{3,2},{4,5},{5,4},{6,7},{7,6},{8,9},{9,8},{10,11... | collective-permute-start | bytes 516104 | tf_op jit(solution)/shard_map/ppermute | solution.py:554
  13.5 6.7 %collective-permute-start.5 = (f32[6,56,128]{2,1,0:T(8,128)S(1)}, f32[6,56,128]{2,1,0:T(8,128)S(1)}, u32[]{:S(2)}, u32[]{:S(2)}) collective-permute-start(f32[6,56,128]{2,1,0:T(8,128)S(1)} %get-tuple-element.24), channel_id=1, source_target_pairs={{1,2},{2,1},{5,6},{6,5},{9,10},{10,9},{13,14},{14,13},{17,18},{18,... | collective-permute-start | bytes 516104 | tf_op jit(solution)/shard_map/ppermute | solution.py:555
  20.3 11.8 %copy-start.1 = (bf16[256,384]{1,0:T(8,128)(2,1)S(1)}, bf16[256,384]{1,0:T(8,128)(2,1)}, u32[]{:S(2)}) copy-start(bf16[256,384]{1,0:T(8,128)(2,1)} %constant.10.clone.p1) | copy-start | bytes 589828
  20.3 11.8 %copy-start.3 = (bf16[128,256]{1,0:T(8,128)(2,1)S(1)}, bf16[128,256]{1,0:T(8,128)(2,1)}, u32[]{:S(2)}) copy-start(bf16[128,256]{1,0:T(8,128)(2,1)} %constant.11.clone.p2) | copy-start | bytes 196612
  24.0 5.1 %collective-permute-start.6 = (f32[21,8,128]{2,1,0:T(8,128)S(1)}, f32[21,8,128]{2,1,0:T(8,128)S(1)}, u32[]{:S(2)}, u32[]{:S(2)}) collective-permute-start(f32[21,8,128]{2,1,0:T(8,128)S(1)} %get-tuple-element.26), channel_id=1, source_target_pairs={{0,4},{4,0},{8,12},{12,8},{1,5},{5,1},{9,13},{13,9},{2,6},{6,2},{1... | collective-permute-start | bytes 258056 | tf_op jit(solution)/shard_map/ppermute | solution.py:577
  25.7 6.4 %collective-permute-start.7 = (f32[21,8,128]{2,1,0:T(8,128)S(1)}, f32[21,8,128]{2,1,0:T(8,128)S(1)}, u32[]{:S(2)}, u32[]{:S(2)}) collective-permute-start(f32[21,8,128]{2,1,0:T(8,128)S(1)} %get-tuple-element.27), channel_id=1, source_target_pairs={{4,8},{8,4},{5,9},{9,5},{6,10},{10,6},{7,11},{11,7},{20,24},{24,20... | collective-permute-start | bytes 258056 | tf_op jit(solution)/shard_map/ppermute | solution.py:578

commit v3 on v2

--- a/solution.py
+++ b/solution.py
@@ -15,11 +15,20 @@
 SLABS = 3
 
 
-def edge_pairs(count, odd):
-    out = []
-    for i in range(1 if odd else 0, count - 1, 2):
-        out += [(i, i + 1), (i + 1, i)]
-    return out
+def neighbour_swap(x, axis, odd, spare):
+    axis = axis if isinstance(axis, tuple) else (axis,)
+    count = lax.axis_size(axis)
+    twins = lax.axis_size(spare)
+    leading = spare == "group"
+    place = lambda i, twin: twin * count + i if leading else i * twins + twin
+    pairs = []
+    for twin in range(twins):
+        for i in range(count):
+            j, other = (i + 1 if i % 2 == odd else i - 1), twin
+            if not 0 <= j < count:
+                j, other = i, twin ^ 1
+            pairs.append((place(i, twin), place(j, other)))
+    return lax.ppermute(x, (spare,) + axis if leading else axis + (spare,), pairs)
 
 
 def lane_maps(cols):
@@ -537,8 +546,8 @@
         ]
     )
     near = lax.ppermute(panels, "tile", [(i, i ^ 1) for i in range(tiles)])
-    a = lax.ppermute(a, "tile", edge_pairs(tiles, False))
-    b = lax.ppermute(b, "tile", edge_pairs(tiles, True))
+    a = neighbour_swap(a, "tile", 0, "sub")
+    b = neighbour_swap(b, "tile", 1, "sub")
     panels = jnp.concatenate([panels, near], 0)
     step = 2
     while step < tiles:
@@ -551,8 +560,8 @@
         forcing_kernel, [(count, span, cols), slabs, slabs], [],
         x_own, a, b, panels,
     )
-    sub = lax.ppermute(sub, y_axes, edge_pairs(y_count, False))
-    strip = lax.ppermute(strip, y_axes, edge_pairs(y_count, True))
+    sub = neighbour_swap(sub, y_axes, 0, "group")
+    strip = neighbour_swap(strip, y_axes, 1, "group")
 
     lanes = cols + 128
     small = span - 16
@@ -574,8 +583,8 @@
         ],
         ext, sub, strip, c1, c2,
     )
-    a2 = lax.ppermute(a2, "tile", edge_pairs(tiles, False))
-    b2 = lax.ppermute(b2, "tile", edge_pairs(tiles, True))
+    a2 = neighbour_swap(a2, "tile", 0, "sub")
+    b2 = neighbour_swap(b2, "tile", 1, "sub")
 
     wide2 = 32
     pair2, pair0 = (2, wide2, cols // 2), (2, small, lanes)

time: 36.9 us -> 32.8 us (0.89)
  the two profiles are of different devices: /device:TPU:10 before, /device:TPU:0 now
where the time goes in v3:
time: 32.8 us; the launch traced here: 32.7 us
  waiting for transfers between devices  12.3 us (38%)
  Pallas kernels  10.3 us (31%)
  starting transfers between devices  9.24 us (28%)
  between operations  0.7 us (2%)
    pallas_call x3, Pallas kernels, call(): pl.pallas_call(kernel, out_shape=[f32(s) for s in outs], in_specs=[VM] *...  9.16 us
    ppermute x6, waiting for transfers between devices, neighbour_swap(): lax.ppermute(x, (spare,) + axis if leading else axis + (spare,), pairs)  7.13 us
    ppermute x1, waiting for transfers between devices, body(): panels = jnp.concatenate([panels, lax.ppermute(panels, 'tile', swap)], 0)  3.71 us
    ppermute x6, starting transfers between devices, neighbour_swap(): lax.ppermute(x, (spare,) + axis if leading else axis + (spare,), pairs)  3.12 us
    ppermute x1, starting transfers between devices, body(): near = lax.ppermute(panels, 'tile', [(i, i ^ 1) for i in range(tiles)])  3.09 us
    ppermute x1, starting transfers between devices, body(): panels = jnp.concatenate([panels, lax.ppermute(panels, 'tile', swap)], 0)  3.03 us
    ppermute x1, waiting for transfers between devices, body(): near = lax.ppermute(panels, 'tile', [(i, i ^ 1) for i in range(tiles)])  1.5 us
    pallas_call x1, Pallas kernels, body(): pl.pallas_call(load_kernel, out_shape=[f32((count, rows, cols)), f32((1,...  1.19 us
  transfers between devices with their start and end apart: 8, of which 4 were waited for; matrix products, arithmetic and copies ran while one was open for 0% of the time, Pallas kernels for 0%

profile of v3, /device:TPU:0, one launch (start us, length us, event | category | flops | bytes accessed | tf_op | source)
XLA Modules:
  0.0 32.7 jit_solution(12222594050013994692)
XLA Ops:
  0.6 1.2 %shard_map.113 = (f32[18,32,256]{2,1,0:T(8,128)S(1)}, f32[1,8,128]{2,1,0:T(8,128)S(1)}, f32[27,8,256]{2,1,0:T(8,128)S(1)}, f32[27,8,256]{2,1,0:T(8,128)S(1)}) custom-call(f32[16,32,256]{2,1,0:T(8,128)} %rs.1, f32[32,256]{1,0:T(8,128)} %kh.1, f32[32,256]{1,0:T(8,128)} %kv.1, s32[4,128]{1,0:T(4,128)} %bitcast.3, s32[4,128]{1,0:T(4,128)} %bitcast.4, ...), custom_call_target="tpu_custom_call" | custom-call | tf_op jit(solution)/shard_map/pallas_call | solution.py:532
  1.8 3.1 %collective-permute-start.2 = (f32[1,8,128]{2,1,0:T(8,128)S(1)}, f32[1,8,128]{2,1,0:T(8,128)S(1)}, u32[]{:S(2)}, u32[]{:S(2)}) collective-permute-start(f32[1,8,128]{2,1,0:T(8,128)S(1)} %get-tuple-element.21), channel_id=1, source_target_pairs={{0,4},{4,0},{8,12},{12,8},{1,5},{5,1},{9,13},{13,9},{2,6},{6,2},{1... | collective-permute-start | bytes 12296 | tf_op jit(solution)/shard_map/ppermute | solution.py:548
  4.9 0.1 collective-permute-start
  5.0 0.0 collective-permute-start.1
  5.0 1.5 %collective-permute-done.2 = f32[1,8,128]{2,1,0:T(8,128)S(1)} collective-permute-done((f32[1,8,128]{2,1,0:T(8,128)S(1)}, f32[1,8,128]{2,1,0:T(8,128)S(1)}, u32[]{:S(2)}, u32[]{:S(2)}) %collective-permute-start.2) | collective-permute-done | bytes 4128 | tf_op jit(solution)/shard_map/ppermute | solution.py:548
  6.5 3.0 %collective-permute-start.3 = (f32[2,8,128]{2,1,0:T(8,128)S(1)}, f32[2,8,128]{2,1,0:T(8,128)S(1)}, u32[]{:S(2)}, u32[]{:S(2)}) collective-permute-start(f32[2,8,128]{2,1,0:T(8,128)S(1)} %pad_maximum_fusion.1), channel_id=1, source_target_pairs={{0,8},{4,12},{8,0},{12,4},{1,9},{5,13},{9,1},{13,5},{2,10},{6,14},... | collective-permute-start | bytes 24584 | tf_op jit(solution)/shard_map/ppermute | solution.py:555
  9.5 3.7 %collective-permute-done.3 = f32[2,8,128]{2,1,0:T(8,128)S(1)} collective-permute-done((f32[2,8,128]{2,1,0:T(8,128)S(1)}, f32[2,8,128]{2,1,0:T(8,128)S(1)}, u32[]{:S(2)}, u32[]{:S(2)}) %collective-permute-start.3) | collective-permute-done | bytes 8224 | tf_op jit(solution)/shard_map/ppermute | solution.py:555
  13.3 0.0 collective-permute-done.xa
  13.3 0.0 collective-permute-done.1.xb
  13.3 0.0 copy-start
  13.3 0.0 copy-start.2
  13.3 0.8 %shard_map.114 = (f32[18,56,256]{2,1,0:T(8,128)S(1)}, f32[6,56,128]{2,1,0:T(8,128)S(1)}, f32[6,56,128]{2,1,0:T(8,128)S(1)}) custom-call(f32[18,32,256]{2,1,0:T(8,128)S(1)} %get-tuple-element.18.x_own, f32[27,8,256]{2,1,0:T(8,128)S(1)} %collective-permute-done.xa, f32[27,8,256]{2,1,0:T(8,128)S(1)} %collective-permute-done.1.xb, ...), custom_call_target="tpu_custom_call" | custom-call | tf_op jit(solution)/shard_map/pallas_call | solution.py:507
  14.1 0.1 collective-permute-start.4
  14.2 1.6 %collective-permute-start.5 = (f32[6,56,128]{2,1,0:T(8,128)S(1)}, f32[6,56,128]{2,1,0:T(8,128)S(1)}, u32[]{:S(2)}, u32[]{:S(2)}) collective-permute-start(f32[6,56,128]{2,1,0:T(8,128)S(1)} %get-tuple-element.24), channel_id=1, source_target_pairs={{0,16},{1,2},{2,1},{3,19},{16,0},{17,18},{18,17},{19,3},{4,20},{5,... | collective-permute-start | bytes 516104 | tf_op jit(solution)/shard_map/ppermute | solution.py:31
  15.7 0.0 collective-permute-done.4.ysub
  15.7 3.9 %collective-permute-done.5.ystrip = f32[6,56,128]{2,1,0:T(8,128)S(1)} collective-permute-done((f32[6,56,128]{2,1,0:T(8,128)S(1)}, f32[6,56,128]{2,1,0:T(8,128)S(1)}, u32[]{:S(2)}, u32[]{:S(2)}) %collective-permute-start.5) | collective-permute-done | bytes 172064 | tf_op jit(solution)/shard_map/ppermute | solution.py:31
  19.6 0.0 copy-done
  19.6 0.0 copy-done.2
  19.6 0.0 copy-start.1
  19.6 0.0 copy-start.3
  19.6 3.7 %shard_map.115 = (f32[16,40,384]{2,1,0:T(8,128)S(1)}, f32[2,40,384]{2,1,0:T(8,128)S(1)}, f32[16,40,384]{2,1,0:T(8,128)S(1)}, f32[2,32,256]{2,1,0:T(8,128)S(1)}, ...) custom-call(f32[18,56,256]{2,1,0:T(8,128)S(1)} %get-tuple-element.22, ...), custom_call_target="tpu_custom_call" | custom-call | tf_op jit(solution)/shard_map/pallas_call | solution.py:507
  23.4 1.4 %collective-permute-start.6 = (f32[21,8,128]{2,1,0:T(8,128)S(1)}, f32[21,8,128]{2,1,0:T(8,128)S(1)}, u32[]{:S(2)}, u32[]{:S(2)}) collective-permute-start(f32[21,8,128]{2,1,0:T(8,128)S(1)} %get-tuple-element.26), channel_id=1, source_target_pairs={{0,4},{4,0},{8,12},{12,8},{1,5},{5,1},{9,13},{13,9},{2,6},{6,2},{1... | collective-permute-start | bytes 258056 | tf_op jit(solution)/shard_map/ppermute | solution.py:31
  24.7 0.0 collective-permute-start.7
  24.8 3.2 %collective-permute-done.6.xa = f32[21,8,128]{2,1,0:T(8,128)S(1)} collective-permute-done((f32[21,8,128]{2,1,0:T(8,128)S(1)}, f32[21,8,128]{2,1,0:T(8,128)S(1)}, u32[]{:S(2)}, u32[]{:S(2)}) %collective-permute-start.6) | collective-permute-done | bytes 86048 | tf_op jit(solution)/shard_map/ppermute | solution.py:31
  28.0 0.0 collective-permute-done.7.xb
  28.0 0.0 copy-done.1
  28.0 0.0 copy-done.3
  28.0 4.7 %shard_map.116 = (f32[16,32,256]{2,1,0:T(8,128)}, f32[16,32,256]{2,1,0:T(8,128)}) custom-call(f32[18,16,128]{2,1,0:T(8,128)S(1)} %get-tuple-element.25.c_in, f32[21,8,128]{2,1,0:T(8,128)S(1)} %collective-permute-done.6.xa, f32[21,8,128]{2,1,0:T(8,128)S(1)} %collective-permute-done.7.xb, f32[16,40,384]{2,1,0:T(8,128)S(1)} %get-tuple-element.28.b0, ...), custom_call_target="tpu_custom_call" | custom-call | tf_op jit(solution)/shard_map/pallas_call | solution.py:507
  (2 shorter events, 0.0 us)
Async XLA Ops:
  1.8 4.7 %collective-permute-start.2 = (f32[1,8,128]{2,1,0:T(8,128)S(1)}, f32[1,8,128]{2,1,0:T(8,128)S(1)}, u32[]{:S(2)}, u32[]{:S(2)}) collective-permute-start(f32[1,8,128]{2,1,0:T(8,128)S(1)} %get-tuple-element.21), channel_id=1, source_target_pairs={{0,4},{4,0},{8,12},{12,8},{1,5},{5,1},{9,13},{13,9},{2,6},{6,2},{1... | collective-permute-start | bytes 12296 | tf_op jit(solution)/shard_map/ppermute | solution.py:548
  4.9 8.3 %collective-permute-start = (f32[27,8,256]{2,1,0:T(8,128)S(1)}, f32[27,8,256]{2,1,0:T(8,128)S(1)}, u32[]{:S(2)}, u32[]{:S(2)}) collective-permute-start(f32[27,8,256]{2,1,0:T(8,128)S(1)} %get-tuple-element.19), channel_id=1, source_target_pairs={{0,4},{4,0},{8,12},{12,8},{1,5},{5,1},{9,13},{13,9},{2,6},{6,2},{1... | collective-permute-start | bytes 663560 | tf_op jit(solution)/shard_map/ppermute | solution.py:31
  5.0 8.3 %collective-permute-start.1 = (f32[27,8,256]{2,1,0:T(8,128)S(1)}, f32[27,8,256]{2,1,0:T(8,128)S(1)}, u32[]{:S(2)}, u32[]{:S(2)}) collective-permute-start(f32[27,8,256]{2,1,0:T(8,128)S(1)} %get-tuple-element.20), channel_id=1, source_target_pairs={{0,1},{4,8},{8,4},{12,13},{1,0},{5,9},{9,5},{13,12},{2,3},{6,10},{... | collective-permute-start | bytes 663560 | tf_op jit(solution)/shard_map/ppermute | solution.py:31
  6.5 6.7 %collective-permute-start.3 = (f32[2,8,128]{2,1,0:T(8,128)S(1)}, f32[2,8,128]{2,1,0:T(8,128)S(1)}, u32[]{:S(2)}, u32[]{:S(2)}) collective-permute-start(f32[2,8,128]{2,1,0:T(8,128)S(1)} %pad_maximum_fusion.1), channel_id=1, source_target_pairs={{0,8},{4,12},{8,0},{12,4},{1,9},{5,13},{9,1},{13,5},{2,10},{6,14},... | collective-permute-start | bytes 24584 | tf_op jit(solution)/shard_map/ppermute | solution.py:555
  13.3 6.4 %copy-start = (bf16[384,256]{1,0:T(8,128)(2,1)S(1)}, bf16[384,256]{1,0:T(8,128)(2,1)}, u32[]{:S(2)}) copy-start(bf16[384,256]{1,0:T(8,128)(2,1)} %constant.8.clone.c1) | copy-start | bytes 589828
  13.3 6.4 %copy-start.2 = (bf16[256,128]{1,0:T(8,128)(2,1)S(1)}, bf16[256,128]{1,0:T(8,128)(2,1)}, u32[]{:S(2)}) copy-start(bf16[256,128]{1,0:T(8,128)(2,1)} %constant.9.clone.c2) | copy-start | bytes 196612
  14.1 1.7 %collective-permute-start.4 = (f32[6,56,128]{2,1,0:T(8,128)S(1)}, f32[6,56,128]{2,1,0:T(8,128)S(1)}, u32[]{:S(2)}, u32[]{:S(2)}) collective-permute-start(f32[6,56,128]{2,1,0:T(8,128)S(1)} %get-tuple-element.23), channel_id=1, source_target_pairs={{0,1},{1,0},{2,3},{3,2},{16,17},{17,16},{18,19},{19,18},{4,5},{5,4... | collective-permute-start | bytes 516104 | tf_op jit(solution)/shard_map/ppermute | solution.py:31
  14.2 5.5 %collective-permute-start.5 = (f32[6,56,128]{2,1,0:T(8,128)S(1)}, f32[6,56,128]{2,1,0:T(8,128)S(1)}, u32[]{:S(2)}, u32[]{:S(2)}) collective-permute-start(f32[6,56,128]{2,1,0:T(8,128)S(1)} %get-tuple-element.24), channel_id=1, source_target_pairs={{0,16},{1,2},{2,1},{3,19},{16,0},{17,18},{18,17},{19,3},{4,20},{5,... | collective-permute-start | bytes 516104 | tf_op jit(solution)/shard_map/ppermute | solution.py:31
  19.6 8.4 %copy-start.1 = (bf16[256,384]{1,0:T(8,128)(2,1)S(1)}, bf16[256,384]{1,0:T(8,128)(2,1)}, u32[]{:S(2)}) copy-start(bf16[256,384]{1,0:T(8,128)(2,1)} %constant.10.clone.p1) | copy-start | bytes 589828
  19.6 8.4 %copy-start.3 = (bf16[128,256]{1,0:T(8,128)(2,1)S(1)}, bf16[128,256]{1,0:T(8,128)(2,1)}, u32[]{:S(2)}) copy-start(bf16[128,256]{1,0:T(8,128)(2,1)} %constant.11.clone.p2) | copy-start | bytes 196612
  23.4 4.6 %collective-permute-start.6 = (f32[21,8,128]{2,1,0:T(8,128)S(1)}, f32[21,8,128]{2,1,0:T(8,128)S(1)}, u32[]{:S(2)}, u32[]{:S(2)}) collective-permute-start(f32[21,8,128]{2,1,0:T(8,128)S(1)} %get-tuple-element.26), channel_id=1, source_target_pairs={{0,4},{4,0},{8,12},{12,8},{1,5},{5,1},{9,13},{13,9},{2,6},{6,2},{1... | collective-permute-start | bytes 258056 | tf_op jit(solution)/shard_map/ppermute | solution.py:31
  24.7 3.2 %collective-permute-start.7 = (f32[21,8,128]{2,1,0:T(8,128)S(1)}, f32[21,8,128]{2,1,0:T(8,128)S(1)}, u32[]{:S(2)}, u32[]{:S(2)}) collective-permute-start(f32[21,8,128]{2,1,0:T(8,128)S(1)} %get-tuple-element.27), channel_id=1, source_target_pairs={{0,1},{4,8},{8,4},{12,13},{1,0},{5,9},{9,5},{13,12},{2,3},{6,10},{... | collective-permute-start | bytes 258056 | tf_op jit(solution)/shard_map/ppermute | solution.py:31

commit v4 on v3

--- a/solution.py
+++ b/solution.py
@@ -13,6 +13,7 @@
 HY = 42
 LIMIT = 512
 SLABS = 3
+EDGE = 16
 
 
 def neighbour_swap(x, axis, odd, spare):
@@ -32,18 +33,26 @@
 
 
 def lane_maps(cols):
-    one = -np.ones(cols + 128, np.int64)
-    half = cols // 2
-    one[:cols] = np.arange(cols) // 2
-    one[cols : cols + HY] = half + np.arange(HY) // 2
-    one[cols + 128 - HY :] = 2 * half - HY // 2 + np.arange(HY) // 2
-    h1 = HY // 2
-    two = -np.ones(2 * half, np.int64)
-    quarter = half // 2
-    two[:half] = np.arange(half) // 2
-    two[half : half + h1 - 1] = quarter + np.arange(h1 - 1) // 2
-    two[2 * half - h1 + 1 :] = 2 * quarter - (h1 - 1) // 2 + np.arange(h1 - 1) // 2
-    return one, two
+    half, quarter, h1, h2 = cols // 2, cols // 4, HY // 2, HY // 4
+    wide1 = -np.ones(cols + 128, np.int64)
+    wide1[:cols] = np.arange(cols) // 2
+    wide1[cols : cols + HY] = half + np.arange(HY) // 2
+    wide1[cols + 128 - HY :] = 2 * half - h1 + np.arange(HY) // 2
+    wide2 = -np.ones(2 * half, np.int64)
+    wide2[:half] = np.arange(half) // 2
+    wide2[half : half + 2 * h2] = quarter + np.arange(2 * h2) // 2
+    wide2[2 * half - 2 * h2 :] = 2 * quarter - h2 + np.arange(2 * h2) // 2
+    inner2 = -np.ones(half, np.int64)
+    inner2[4 : half - 4] = np.arange(4, half - 4) // 2
+    edge1 = -np.ones(128, np.int64)
+    edge1[: 2 * HY + EDGE] = np.arange(2 * HY + EDGE) // 2
+    edge1[128 - EDGE :] = 128 - EDGE // 2 + np.arange(EDGE) // 2
+    edge2 = -np.ones(128, np.int64)
+    edge2[: 2 * h2] = quarter + np.arange(2 * h2) // 2
+    edge2[2 * h1 - 2 * h2 : 2 * h1] = 2 * quarter - h2 + np.arange(2 * h2) // 2
+    edge2[2 * h1 : 2 * h1 + 4] = np.arange(4) // 2
+    edge2[124:] = quarter - 2 + np.arange(4) // 2
+    return wide1, wide2, inner2, edge1, edge2
 
 
 def selection(lanes, width):
@@ -101,10 +110,12 @@
     loop(depth, layer, src.shape[1] * src.shape[2] // 1024)
 
 
-def residual_of(src, z, b, kh, kv, scale):
+def residual_of(src, z, b, kh, kv, scale, lanes=None):
     layers = jnp.where(z == 0, 1.0, 2.0)
     u = src[z + 1]
-    return b + (scale * kh) * (neighbours(u) - 4.0 * u) + kv * (src[z] + src[z + 2] - layers * u)
+    around = neighbours(u)[:, :lanes]
+    u = u[:, :lanes]
+    return b + (scale * kh) * (around - 4.0 * u) + kv * (src[z, :, :lanes] + src[z + 2, :, :lanes] - layers * u)
 
 
 def blocks_out(ref, l, x):
@@ -243,124 +254,140 @@
         strip_out[g] = jnp.where(y_even, to_left, to_right)
 
 
-def down_kernel(
-    ext, ysub, ystrip, c1, c2,
-    b_out, k_out, u_out, k1_out, b1_out, u1_out, c_out, a_msg, b_msg,
-    b0, u0, u0n, r0, w0, al0, be0, w1, al1, be1, u1, u1n, r1,
+def row_inside(shape, rows, above):
+    row = lax.axis_index("tile") * rows - above + lax.broadcasted_iota(jnp.int32, shape, 0)
+    return (row >= 0) & (row < lax.axis_size("tile") * rows)
+
+
+def y_sides():
+    y = lax.axis_index("strip") * lax.axis_size("sub") + lax.axis_index("sub")
+    return y > 0, y < lax.axis_size("strip") * lax.axis_size("sub") - 1, y % 2 == 0
+
+
+def wide_inside(shape, rows, above, own, halo):
+    has_left, has_right, _ = y_sides()
+    column = lax.broadcasted_iota(jnp.int32, shape, 1)
+    right = (column >= own) & (column < own + halo) & has_right
+    left = (column >= shape[1] - halo) & has_left
+    return row_inside(shape, rows, above) & ((column < own) | right | left)
+
+
+def edge_inside(shape, rows, above, halo, edge):
+    has_left, has_right, _ = y_sides()
+    column = lax.broadcasted_iota(jnp.int32, shape, 1)
+    right = (column < halo) & has_right
+    left = (column >= halo) & (column < 2 * halo) & has_left
+    own = ((column >= 2 * halo) & (column < 2 * halo + edge)) | (column >= 128 - edge)
+    return row_inside(shape, rows, above) & (own | right | left)
+
+
+def zero_ends(*refs):
+    for ref in refs:
+        ref[0] = jnp.zeros(ref.shape[1:], jnp.float32)
+        ref[ref.shape[0] - 1] = jnp.zeros(ref.shape[1:], jnp.float32)
+
+
+def presmooth(source, kh, kv, scale, inside, w, al, be, u, un, depth):
+    weights(kh, kv, scale, inside, w, al, be)
+    zero_ends(u, un)
+
+    def first(z, c):
+        u[z + 1] = w[jnp.minimum(z, 1)] * source[z]
+        return c
+
+    loop(depth, first, u.shape[1] * u.shape[2] // 1024)
+    sweep(u, un, u.at[pl.ds(1, depth)], al, be, depth)
+
+
+def restrict(source, un, scale, r, depth, parts):
+    kh, kv = source[depth], source[depth + 1]
+    rows = kh.shape[0]
+    for l in range(depth + 2):
+        for j in range(r.shape[1]):
+            if r.shape[2] > rows:
+                r[l, j, rows:, :] = jnp.zeros((r.shape[2] - rows, 128), jnp.float32)
+    blocks_out(r, depth, kh)
+    blocks_out(r, depth + 1, kv)
+
+    def rest(z, c):
+        blocks_out(r, z, residual_of(un, z, source[z], source[depth], source[depth + 1], scale))
+        return c
+
+    loop(depth, rest, rows * kh.shape[1] // 1024)
+    n = r.shape[2] // 2
+    pairs = jnp.concatenate(
+        [
+            jnp.concatenate(
+                [r[l, j, pl.ds(0, n, stride=2), :] + r[l, j, pl.ds(1, n, stride=2), :] for j in range(r.shape[1])], 1
+            )
+            for l in range(depth + 2)
+        ],
+        0,
+    )
+    return exact_dot(pairs, parts).reshape(depth + 2, n, parts.shape[1])
+
+
+def inner_kernel(
+    ext, c1, c2, u_out, b1_out, u1_out, c_out,
+    w0, al0, be0, u0, u0n, r0, w1, al1, be1, u1, u1n, r1,
 ):
-    depth = ext.shape[0] - 2
-    span, cols = ext.shape[1], ext.shape[2]
+    depth, span, cols = ext.shape[0] - 2, ext.shape[1], ext.shape[2]
+    rows = span - 2 * HX
+    presmooth(
+        ext, ext[depth], ext[depth + 1], 1.0, row_inside((span, cols), rows, HX), w0, al0, be0, u0, u0n, depth
+    )
+    for z in range(depth):
+        u_out[z] = u0n[z + 1, 8 : span - 8, :]
+    b1_out[...] = restrict(ext, u0n, 1.0, r0, depth, c1[...])
+    span1, half = b1_out.shape[1], b1_out.shape[2]
+    presmooth(
+        b1_out, b1_out[depth], b1_out[depth + 1], 0.25, row_inside((span1, half), rows // 2, HX // 2),
+        w1, al1, be1, u1, u1n, depth,
+    )
+    u1_out[...] = u1n[pl.ds(1, depth)]
+    c_out[...] = restrict(b1_out, u1n, 0.25, r1, depth, c2[...])
+
+
+def edge_kernel(
+    ext, ysub, ystrip, c_inner, c1, c2,
+    b_out, u_out, b1_out, u1_out, c_out, a_msg, b_msg,
+    w0, al0, be0, u0, u0n, r0, w1, al1, be1, u1, u1n, r1,
+):
+    depth, span, cols = ext.shape[0] - 2, ext.shape[1], ext.shape[2]
+    rows = span - 2 * HX
     count = depth + 2
-    tiles = lax.axis_size("tile")
-    tile = lax.axis_index("tile")
-    y_count = lax.axis_size("strip") * lax.axis_size("sub")
-    y = lax.axis_index("strip") * lax.axis_size("sub") + lax.axis_index("sub")
-    y_even = y % 2 == 0
-    rows = span - 2 * HX
+    even = lax.axis_index("tile") % 2 == 0
+    _, _, y_even = y_sides()
     lane = lax.broadcasted_iota(jnp.int32, (span, 128), 1)
+
+    def rolled(x, shift):
+        return pltpu.roll(x, shift % 128, 1) if shift % 128 else x
 
     for g in range(count // SLABS):
         from_right = jnp.where(y_even, ysub[g], ystrip[g])
         from_left = jnp.where(y_even, ystrip[g], ysub[g])
         for k in range(SLABS):
             l = SLABS * g + k
-            right = pltpu.roll(from_right, 128 - HY * k, 1) if k else from_right
-            left = pltpu.roll(from_left, 128 - HY - HY * k, 1) if (128 - HY - HY * k) % 128 else from_left
-            b0[l, :, 0:cols] = ext[l]
-            b0[l, :, cols : cols + 128] = jnp.where(lane < HY, right, jnp.where(lane >= 128 - HY, left, 0.0))
-
-    def inside_of(shape, first_row, row_end, own, halo):
-        row = first_row + lax.broadcasted_iota(jnp.int32, shape, 0)
-        column = lax.broadcasted_iota(jnp.int32, shape, 1)
-        right = (column >= own) & (column < own + halo) & (y < y_count - 1)
-        left = (column >= shape[1] - halo) & (y > 0)
-        return (row >= 0) & (row < row_end) & ((column < own) | right | left)
-
-    lanes = cols + 128
-    kh, kv = b0[depth], b0[depth + 1]
-    weights(kh, kv, 1.0, inside_of((span, lanes), tile * rows - HX, tiles * rows, cols, HY), w0, al0, be0)
-    zero = jnp.zeros((span, lanes), jnp.float32)
-    u0[0] = zero
-    u0[depth + 1] = zero
-    u0n[0] = zero
-    u0n[depth + 1] = zero
-
-    def first(z, c):
-        u0[z + 1] = w0[jnp.minimum(z, 1)] * b0[z]
-        return c
-
-    loop(depth, first, 21)
-    sweep(u0, u0n, u0.at[pl.ds(1, depth)], al0, be0, depth)
-
-    low, top = 8, span - 8
-    pad = r0.shape[2] - span
-    for l in range(count):
-        for j in range(r0.shape[1]):
-            r0[l, j, span : span + pad, :] = jnp.zeros((pad, 128), jnp.float32)
-    blocks_out(r0, depth, kh)
-    blocks_out(r0, depth + 1, kv)
-    k_out[0] = kh[low:top]
-    k_out[1] = kv[low:top]
-
-    def rest(z, c):
-        b = b0[z]
-        blocks_out(r0, z, residual_of(u0n, z, b, b0[depth], b0[depth + 1], 1.0))
-        b_out[z] = b[low:top]
-        u_out[z] = u0n[z + 1][low:top]
-        return c
-
-    loop(depth, rest, 21)
-
-    def coarse_rows(ref, l, n):
-        return jnp.concatenate(
-            [
-                ref[l, j, pl.ds(0, n, stride=2), :] + ref[l, j, pl.ds(1, n, stride=2), :]
-                for j in range(ref.shape[1])
-            ],
-            1,
-        )
-
-    span1 = r0.shape[2] // 2
-    half = cols
-    pairs = jnp.concatenate([coarse_rows(r0, l, span1) for l in range(count)], 0)
-    b1 = exact_dot(pairs, c1[...]).reshape(count, span1, half)
-    b1_out[...] = b1[0:depth]
-    k1_out[...] = b1[depth:]
-    kh1, kv1 = k1_out[0], k1_out[1]
-    weights(
-        kh1, kv1, 0.25,
-        inside_of((span1, half), tile * (rows // 2) - HX // 2, tiles * (rows // 2), cols // 2, HY // 2),
-        w1, al1, be1,
-    )
-    zero1 = jnp.zeros((span1, half), jnp.float32)
-    u1[0] = zero1
-    u1[depth + 1] = zero1
-    u1n[0] = zero1
-    u1n[depth + 1] = zero1
-
-    def first1(z, c):
-        u1[z + 1] = w1[jnp.minimum(z, 1)] * b1_out[z]
-        return c
-
-    loop(depth, first1, 8)
-    sweep(u1, u1n, u1.at[pl.ds(1, depth)], al1, be1, depth)
-
-    def rest1(z, c):
-        blocks_out(r1, z, residual_of(u1n, z, b1_out[z], k1_out[0], k1_out[1], 0.25))
-        u1_out[z] = u1n[z + 1]
-        return c
-
-    loop(depth, rest1, 8)
-    blocks_out(r1, depth, kh1)
-    blocks_out(r1, depth + 1, kv1)
-    span2 = span1 // 2
-    pairs = jnp.concatenate([coarse_rows(r1, l, span2) for l in range(count)], 0)
-    b2 = exact_dot(pairs, c2[...]).reshape(count, span2, cols // 2)
-    c_out[...] = b2
-
+            x = jnp.where(lane >= 128 - EDGE, ext[l, :, cols - 128 : cols], 0.0)
+            x = jnp.where((lane >= 2 * HY) & (lane < 2 * HY + EDGE), rolled(ext[l, :, 0:128], 2 * HY), x)
+            x = jnp.where((lane >= HY) & (lane < 2 * HY), rolled(from_left, HY - HY * k), x)
+            b_out[l] = jnp.where(lane < HY, rolled(from_right, -HY * k), x)
+    presmooth(
+        b_out, b_out[depth], b_out[depth + 1], 1.0, edge_inside((span, 128), rows, HX, HY, EDGE),
+        w0, al0, be0, u0, u0n, depth,
+    )
+    for z in range(depth):
+        u_out[z] = u0n[z + 1, 8 : span - 8, :]
+    b1_out[...] = restrict(b_out, u0n, 1.0, r0, depth, c1[...])
+    span1 = b1_out.shape[1]
+    presmooth(
+        b1_out, b1_out[depth], b1_out[depth + 1], 0.25,
+        edge_inside((span1, 128), rows // 2, HX // 2, HY // 2, EDGE // 2),
+        w1, al1, be1, u1, u1n, depth,
+    )
+    u1_out[...] = u1n[pl.ds(1, depth)]
+    c_out[...] = c_inner[...] + restrict(b1_out, u1n, 0.25, r1, depth, c2[...])
     own2 = HX // 4
-    rows2 = rows // 4
-    even = tile % 2 == 0
 
     def send(out, start):
         for l in range(count):
@@ -378,31 +405,59 @@
         send(b_msg, own2 - 1)
 
 
+def join_kernel(
+    ext, edge, u_in, u_edge, b1_in, b1_edge, u1_in, u1_edge,
+    k0, u0, wb0, al0, be0, u1, wb1, al1, be1, w0, w1,
+):
+    depth, small, cols = u_in.shape
+    span = ext.shape[1]
+    rows = span - 2 * HX
+
+    def joined(inner, strip, halo, edge, patch):
+        own = inner.shape[1]
+        lane = lax.broadcasted_iota(jnp.int32, strip.shape, 1)
+        turned = pltpu.roll(strip, 128 - 2 * halo, 1)
+        outer = jnp.where(lane < halo, strip, jnp.where(lane >= 128 - halo, turned, 0.0))
+        blocks = [inner[:, 128 * j : 128 * (j + 1)] for j in range(own // 128)]
+        blocks[0] = jnp.where(lane < patch, turned, blocks[0])
+        blocks[-1] = jnp.where(lane >= 128 - patch, strip, blocks[-1])
+        return jnp.concatenate(blocks + [outer], 1)
+
+    part0 = lambda inner, strip: joined(inner, strip, HY, EDGE, EDGE // 2)
+    part1 = lambda inner, strip: joined(inner, strip, HY // 2, EDGE // 2, EDGE // 4)
+    low, top = 8, span - 8
+    lanes = cols + 128
+    for i in (0, 1):
+        k0[i] = part0(ext[depth + i, low:top, :], edge[depth + i, low:top, :])
+    weights(
+        k0[0], k0[1], 1.0, wide_inside((small, lanes), rows, HX - low, cols, HY), w0, al0, be0,
+    )
+    span1, half = b1_in.shape[1], b1_in.shape[2]
+    kh1, kv1 = (part1(b1_in[depth + i], b1_edge[depth + i]) for i in (0, 1))
+    weights(
+        kh1, kv1, 0.25, wide_inside((span1, 2 * half), rows // 2, HX // 2, half, HY // 2), w1, al1, be1,
+    )
+    for z in range(depth):
+        i = min(z, 1)
+        u0[z] = part0(u_in[z], u_edge[z])
+        wb0[z] = w0[i] * part0(ext[z, low:top, :], edge[z, low:top, :])
+        u1[z] = part1(u1_in[z], u1_edge[z])
+        wb1[z] = w1[i] * part1(b1_in[z], b1_edge[z])
+
+
 def up_kernel(
-    c_in, xa, xb, b0, k0, u0, k1, b1, u1, p1, p2,
+    c_in, xa, xb, ext, k0, u0, wb0, al0, be0, u1, wb1, al1, be1, p1, p2,
     potential, residual,
-    b2, w2, al2, be2, wb2, u2, u2n, w1, al1, be1, wb1, f1, f1n, w0, al0, be0, wb0, f0, f0n, e1, e0,
+    b2, w2, al2, be2, wb2, u2, u2n, f1, f1n, f0, f0n, e1, e0, pot, res, sems,
 ):
     count = c_in.shape[0]
     depth = count - 2
-    cols = potential.shape[2]
-    rows = potential.shape[1]
+    rows, cols = potential.shape[1:]
     rows2 = rows // 4
-    tiles = lax.axis_size("tile")
-    tile = lax.axis_index("tile")
-    y_count = lax.axis_size("strip") * lax.axis_size("sub")
-    y = lax.axis_index("strip") * lax.axis_size("sub") + lax.axis_index("sub")
-    even = tile % 2 == 0
+    even = lax.axis_index("tile") % 2 == 0
     own2 = HX // 4
     span2 = b2.shape[1]
     end2 = rows2 + 2 * HX2
-
-    def inside_of(shape, first_row, row_end, own, halo):
-        row = first_row + lax.broadcasted_iota(jnp.int32, shape, 0)
-        column = lax.broadcasted_iota(jnp.int32, shape, 1)
-        right = (column >= own) & (column < own + halo) & (y < y_count - 1)
-        left = (column >= shape[1] - halo) & (y > 0)
-        return (row >= 0) & (row < row_end) & ((column < own) | right | left)
 
     def put(x, start):
         for l in range(count):
@@ -424,16 +479,9 @@
         b2[l, HX2 : HX2 + rows2, :] = c_in[l, own2 : own2 + rows2, :]
         b2[l, end2:span2, :] = jnp.zeros((span2 - end2, lanes2), jnp.float32)
     row = lax.broadcasted_iota(jnp.int32, (span2, lanes2), 0)
-    inside2 = inside_of((span2, lanes2), tile * rows2 - HX2, tiles * rows2, cols // 4, (HY - 2) // 4)
+    inside2 = wide_inside((span2, lanes2), rows2, HX2, cols // 4, HY // 4)
     weights(b2[depth], b2[depth + 1], 0.0625, inside2 & (row < end2), w2, al2, be2)
-
-    def zero_ends(ref):
-        z = jnp.zeros(ref.shape[1:], jnp.float32)
-        ref[0] = z
-        ref[depth + 1] = z
-
-    for ref in (u2, u2n, f1, f1n, f0, f0n):
-        zero_ends(ref)
+    zero_ends(u2, u2n, f1, f1n, f0, f0n)
 
     def first2(z, c):
         v = w2[jnp.minimum(z, 1)] * b2[z]
@@ -448,12 +496,6 @@
         src, dst = dst, src
 
     span1, lanes1 = u1.shape[1], u1.shape[2]
-    kh1, kv1 = k1[0], k1[1]
-    weights(
-        kh1, kv1, 0.25,
-        inside_of((span1, lanes1), tile * (rows // 2) - HX // 2, tiles * (rows // 2), cols // 2, HY // 2),
-        w1, al1, be1,
-    )
     off2 = HX2 - own2
     coarse = jnp.concatenate([src[z + 1][off2 : off2 + span1 // 2] for z in range(depth)], 0)
     fine = exact_dot(coarse, p2[...])
@@ -462,20 +504,14 @@
 
     def first1(z, c):
         f1[z + 1] = u1[z] + blocks_in(e1, z)
-        wb1[z] = w1[jnp.minimum(z, 1)] * b1[z]
         return c
 
     loop(depth, first1, 8)
     sweep(f1, f1n, wb1, al1, be1, depth)
     sweep(f1n, f1, wb1, al1, be1, depth)
 
-    span0, lanes0 = b0.shape[1], b0.shape[2]
+    span0, lanes0 = u0.shape[1], u0.shape[2]
     above = (span0 - rows) // 2
-    weights(
-        k0[0], k0[1], 1.0,
-        inside_of((span0, lanes0), tile * rows - above, tiles * rows, cols, HY),
-        w0, al0, be0,
-    )
     off1 = (HX - above) // 2
     fine = exact_dot(f1[pl.ds(1, depth)].reshape(depth * span1, lanes1), p1[...])
     for z in range(depth):
@@ -483,20 +519,31 @@
 
     def first0(z, c):
         f0[z + 1] = u0[z] + blocks_in(e0, z)
-        wb0[z] = w0[jnp.minimum(z, 1)] * b0[z]
         return c
 
     loop(depth, first0, 15)
     sweep(f0, f0n, wb0, al0, be0, depth)
     sweep(f0n, f0, wb0, al0, be0, depth)
 
-    def last(z, c):
-        r = residual_of(f0, z, b0[z], k0[0], k0[1], 1.0)
-        residual[z] = r[above : above + rows, 0:cols]
-        potential[z] = f0[z + 1][above : above + rows, 0:cols]
-        return c
-
-    loop(depth, last, 15)
+    copies = []
+
+    def ship(src, dst, first, n):
+        copy = pltpu.make_async_copy(src.at[pl.ds(first, n)], dst.at[pl.ds(first, n)], sems.at[len(copies)])
+        copy.start()
+        copies.append(copy)
+
+    for z in range(depth):
+        pot[z] = f0[z + 1, above : above + rows, 0:cols]
+    ship(pot, potential, 0, depth)
+    chunk = depth // 4
+    for z in range(depth):
+        b = ext[z, HX - above : HX - above + span0, :]
+        r = residual_of(f0, z, b, k0[0, :, 0:cols], k0[1, :, 0:cols], 1.0, cols)
+        res[z] = r[above : above + rows]
+        if z % chunk == chunk - 1:
+            ship(res, residual, z + 1 - chunk, chunk)
+    for copy in copies:
+        copy.wait()
 
 
 VM = pl.BlockSpec(memory_space=pltpu.VMEM)
@@ -510,7 +557,7 @@
         in_specs=[VM] * len(args),
         out_specs=[VM] * len(outs),
         scratch_shapes=[pltpu.VMEM(s, jnp.float32) for s in scratch],
-        compiler_params=pltpu.CompilerParams(vmem_limit_bytes=40 << 20),
+        compiler_params=pltpu.CompilerParams(vmem_limit_bytes=24 << 20),
     )(*args)
 
 
@@ -521,11 +568,12 @@
     y_count = lax.axis_size("strip") * lax.axis_size("sub")
     count = depth + 2
     span = rows + 2 * HX
-    one, two = lane_maps(cols)
-    c1 = jnp.asarray(0.25 * selection(one, cols), jnp.bfloat16)
-    c2 = jnp.asarray(0.25 * selection(two, cols // 2), jnp.bfloat16)
-    p1 = jnp.asarray(selection(one, cols).T, jnp.bfloat16)
-    p2 = jnp.asarray(selection(two, cols // 2).T, jnp.bfloat16)
+    wide1, wide2, inner2, edge1, edge2 = lane_maps(cols)
+    mean = lambda lanes, width: jnp.asarray(0.25 * selection(lanes, width), jnp.bfloat16)
+    spread = lambda lanes, width: jnp.asarray(selection(lanes, width).T, jnp.bfloat16)
+    c1_inner, c2_inner = mean(wide1[:cols], cols // 2), mean(inner2, cols // 2)
+    c1_edge, c2_edge = mean(edge1, 128), mean(edge2, cols // 2)
+    p1, p2 = spread(wide1, cols), spread(wide2, cols // 2)
 
     message = (count + count // 2, 8, cols)
     f32 = lambda shape: jax.ShapeDtypeStruct(shape, jnp.float32)
@@ -563,43 +611,65 @@
     sub = neighbour_swap(sub, y_axes, 0, "group")
     strip = neighbour_swap(strip, y_axes, 1, "group")
 
-    lanes = cols + 128
+    lanes, half = cols + 128, cols // 2
     small = span - 16
     span1 = (span + 8) // 2
     span2 = span1 // 2
-    message2 = (count + (count + 7) // 8, 8, cols // 2)
-    field = (depth + 2, span, lanes)
-    field1 = (depth + 2, span1, cols)
-    pair, pair1 = (2, span, lanes), (2, span1, cols)
-    b0, k0, u0, k1, b1, u1, c2_own, a2, b2 = call(
-        down_kernel,
+
+    def down_scratch(width, width1):
+        return (
+            [(2, span, width)] * 3 + [(depth + 2, span, width)] * 2 + [(count, width // 128, span + 8, 128)]
+            + [(2, span1, width1)] * 3 + [(depth + 2, span1, width1)] * 2 + [(count, width1 // 128, span1, 128)]
+        )
+
+    u_in, b1_in, u1_in, c_in = call(
+        inner_kernel,
+        [(depth, small, cols), (count, span1, half), (depth, span1, half), (count, span2, half)],
+        down_scratch(cols, half),
+        ext, c1_inner, c2_inner,
+    )
+    message2 = (count + (count + 7) // 8, 8, half)
+    edge, u_edge, b1_edge, u1_edge, c_own, a2, b2 = call(
+        edge_kernel,
         [
-            (depth, small, lanes), (2, small, lanes), (depth, small, lanes), (2, span1, cols),
-            (depth, span1, cols), (depth, span1, cols), (count, span2, cols // 2), message2, message2,
+            (count, span, 128), (depth, small, 128), (count, span1, 128), (depth, span1, 128),
+            (count, span2, half), message2, message2,
         ],
-        [
-            (count, span, lanes), field, field, (count, lanes // 128, span + 8, 128), pair, pair, pair,
-            pair1, pair1, pair1, field1, field1, (count, cols // 128, span1, 128),
-        ],
-        ext, sub, strip, c1, c2,
+        down_scratch(128, 128),
+        ext, sub, strip, c_in, c1_edge, c2_edge,
     )
     a2 = neighbour_swap(a2, "tile", 0, "sub")
     b2 = neighbour_swap(b2, "tile", 1, "sub")
 
+    pair0, field = (2, small, lanes), (depth, small, lanes)
+    pair1, field1 = (2, span1, cols), (depth, span1, cols)
+    state = call(
+        join_kernel,
+        [pair0, field, field, pair0, pair0, field1, field1, pair1, pair1],
+        [pair0, pair1],
+        ext, edge, u_in, u_edge, b1_in, b1_edge, u1_in, u1_edge,
+    )
+
     wide2 = 32
-    pair2, pair0 = (2, wide2, cols // 2), (2, small, lanes)
-    field2 = (depth + 2, wide2, cols // 2)
-    field0 = (depth + 2, small, lanes)
-    potential, residual = call(
-        up_kernel, [right_side.shape, right_side.shape],
-        [
-            (count, wide2, cols // 2), pair2, pair2, pair2, (depth, wide2, cols // 2), field2, field2,
-            pair1, pair1, pair1, (depth, span1, cols), field1, field1,
-            pair0, pair0, pair0, (depth, small, lanes), field0, field0,
-            (depth, cols // 128, span1, 128), (depth, lanes // 128, small, 128),
-        ],
-        c2_own, a2, b2, b0, k0, u0, k1, b1, u1, p1, p2,
-    )
+    field2 = (depth + 2, wide2, half)
+    own = right_side.shape
+    potential, residual = pl.pallas_call(
+        up_kernel,
+        out_shape=[f32(own), f32(own)],
+        in_specs=[VM] * (6 + len(state)),
+        out_specs=[pl.BlockSpec(memory_space=pltpu.HBM)] * 2,
+        scratch_shapes=[
+            pltpu.VMEM(shape, jnp.float32)
+            for shape in (
+                (count, wide2, half), (2, wide2, half), (2, wide2, half), (2, wide2, half), (depth, wide2, half),
+                field2, field2, (depth + 2, span1, cols), (depth + 2, span1, cols),
+                (depth + 2, small, lanes), (depth + 2, small, lanes),
+                (depth, cols // 128, span1, 128), (depth, lanes // 128, small, 128), own, own,
+            )
+        ]
+        + [pltpu.SemaphoreType.DMA((5,))],
+        compiler_params=pltpu.CompilerParams(vmem_limit_bytes=24 << 20),
+    )(c_own, a2, b2, ext, *state, p1, p2)
     return potential, residual
 
 

time: 32.8 us -> 30.8 us (0.939)
  waiting for transfers between devices: 12.3 us -> 9.59 us
  Pallas kernels: 10.3 us -> 11 us
    pallas_call x0 -> x1, Pallas kernels: none -> 4.61 us  [body(): pl.pallas_call(up_kernel, out_shape=[f32(own), f32(own)], in_specs=[VM] *...]
    pallas_call x3 -> x4, Pallas kernels: 9.16 us -> 5.24 us  [call(): pl.pallas_call(kernel, out_shape=[f32(s) for s in outs], in_specs=[VM] *...]
    ppermute x6, waiting for transfers between devices: 7.13 us -> 4.37 us  [neighbour_swap(): lax.ppermute(x, (spare,) + axis if leading else axis + (spare,), pairs)]
  transfers between devices with their start and end apart: 8 -> 8, of which waited for: 4 -> 4; matrix products, arithmetic and copies ran while one was open for 0% -> 0% of each run, Pallas kernels for 0% -> 9%
where the time goes in v4:
time: 30.8 us; the launch traced here: 30.6 us
  Pallas kernels  11 us (36%)
  waiting for transfers between devices  9.59 us (31%)
  starting transfers between devices  9.25 us (30%)
  between operations  0.73 us (2%)
    pallas_call x4, Pallas kernels, call(): pl.pallas_call(kernel, out_shape=[f32(s) for s in outs], in_specs=[VM] *...  5.24 us
    pallas_call x1, Pallas kernels, body(): pl.pallas_call(up_kernel, out_shape=[f32(own), f32(own)], in_specs=[VM] *...  4.61 us
    ppermute x6, waiting for transfers between devices, neighbour_swap(): lax.ppermute(x, (spare,) + axis if leading else axis + (spare,), pairs)  4.37 us
    ppermute x1, waiting for transfers between devices, body(): panels = jnp.concatenate([panels, lax.ppermute(panels, 'tile', swap)], 0)  3.71 us
    ppermute x6, starting transfers between devices, neighbour_swap(): lax.ppermute(x, (spare,) + axis if leading else axis + (spare,), pairs)  3.13 us
    ppermute x1, starting transfers between devices, body(): near = lax.ppermute(panels, 'tile', [(i, i ^ 1) for i in range(tiles)])  3.09 us
    ppermute x1, starting transfers between devices, body(): panels = jnp.concatenate([panels, lax.ppermute(panels, 'tile', swap)], 0)  3.03 us
    ppermute x1, waiting for transfers between devices, body(): near = lax.ppermute(panels, 'tile', [(i, i ^ 1) for i in range(tiles)])  1.5 us
  transfers between devices with their start and end apart: 8, of which 4 were waited for; matrix products, arithmetic and copies ran while one was open for 0% of the time, Pallas kernels for 9%

profile of v4, /device:TPU:0, one launch (start us, length us, event | category | flops | bytes accessed | tf_op | source)
XLA Modules:
  0.0 30.6 jit_solution(685046860964212711)
XLA Ops:
  0.6 1.2 %shard_map.131 = (f32[18,32,256]{2,1,0:T(8,128)S(1)}, f32[1,8,128]{2,1,0:T(8,128)S(1)}, f32[27,8,256]{2,1,0:T(8,128)S(1)}, f32[27,8,256]{2,1,0:T(8,128)S(1)}) custom-call(f32[16,32,256]{2,1,0:T(8,128)} %rs.1, f32[32,256]{1,0:T(8,128)} %kh.1, f32[32,256]{1,0:T(8,128)} %kv.1, s32[4,128]{1,0:T(4,128)} %bitcast.3, s32[4,128]{1,0:T(4,128)} %bitcast.4, ...), custom_call_target="tpu_custom_call" | custom-call | tf_op jit(solution)/shard_map/pallas_call | solution.py:580
  1.8 3.1 %collective-permute-start.2 = (f32[1,8,128]{2,1,0:T(8,128)S(1)}, f32[1,8,128]{2,1,0:T(8,128)S(1)}, u32[]{:S(2)}, u32[]{:S(2)}) collective-permute-start(f32[1,8,128]{2,1,0:T(8,128)S(1)} %get-tuple-element.32), channel_id=1, source_target_pairs={{0,4},{4,0},{8,12},{12,8},{1,5},{5,1},{9,13},{13,9},{2,6},{6,2},{1... | collective-permute-start | bytes 12296 | tf_op jit(solution)/shard_map/ppermute | solution.py:596
  4.9 0.1 collective-permute-start
  5.0 0.0 collective-permute-start.1
  5.0 1.5 %collective-permute-done.2 = f32[1,8,128]{2,1,0:T(8,128)S(1)} collective-permute-done((f32[1,8,128]{2,1,0:T(8,128)S(1)}, f32[1,8,128]{2,1,0:T(8,128)S(1)}, u32[]{:S(2)}, u32[]{:S(2)}) %collective-permute-start.2) | collective-permute-done | bytes 4128 | tf_op jit(solution)/shard_map/ppermute | solution.py:596
  6.5 3.0 %collective-permute-start.3 = (f32[2,8,128]{2,1,0:T(8,128)S(1)}, f32[2,8,128]{2,1,0:T(8,128)S(1)}, u32[]{:S(2)}, u32[]{:S(2)}) collective-permute-start(f32[2,8,128]{2,1,0:T(8,128)S(1)} %pad_maximum_fusion.1), channel_id=1, source_target_pairs={{0,8},{4,12},{8,0},{12,4},{1,9},{5,13},{9,1},{13,5},{2,10},{6,14},... | collective-permute-start | bytes 24584 | tf_op jit(solution)/shard_map/ppermute | solution.py:603
  9.5 3.7 %collective-permute-done.3 = f32[2,8,128]{2,1,0:T(8,128)S(1)} collective-permute-done((f32[2,8,128]{2,1,0:T(8,128)S(1)}, f32[2,8,128]{2,1,0:T(8,128)S(1)}, u32[]{:S(2)}, u32[]{:S(2)}) %collective-permute-start.3) | collective-permute-done | bytes 8224 | tf_op jit(solution)/shard_map/ppermute | solution.py:603
  13.3 0.0 collective-permute-done.xa
  13.3 0.0 collective-permute-done.1.xb
  13.3 0.0 copy-start.2
  13.3 0.0 copy-start.5
  13.3 0.8 %shard_map.132 = (f32[18,56,256]{2,1,0:T(8,128)S(1)}, f32[6,56,128]{2,1,0:T(8,128)S(1)}, f32[6,56,128]{2,1,0:T(8,128)S(1)}) custom-call(f32[18,32,256]{2,1,0:T(8,128)S(1)} %get-tuple-element.29.x_own, f32[27,8,256]{2,1,0:T(8,128)S(1)} %collective-permute-done.xa, f32[27,8,256]{2,1,0:T(8,128)S(1)} %collective-permute-done.1.xb, ...), custom_call_target="tpu_custom_call" | custom-call | tf_op jit(solution)/shard_map/pallas_call | solution.py:554
  14.1 0.1 collective-permute-start.4
  14.2 1.6 %collective-permute-start.5 = (f32[6,56,128]{2,1,0:T(8,128)S(1)}, f32[6,56,128]{2,1,0:T(8,128)S(1)}, u32[]{:S(2)}, u32[]{:S(2)}) collective-permute-start(f32[6,56,128]{2,1,0:T(8,128)S(1)} %get-tuple-element.35), channel_id=1, source_target_pairs={{0,16},{1,2},{2,1},{3,19},{16,0},{17,18},{18,17},{19,3},{4,20},{5,... | collective-permute-start | bytes 516104 | tf_op jit(solution)/shard_map/ppermute | solution.py:32
  15.7 0.0 copy-done.2
  15.7 0.0 copy-done.5
  15.7 0.0 copy-start.3
  15.7 0.0 copy-start.4
  15.8 2.1 %shard_map.133 = (f32[16,40,256]{2,1,0:T(8,128)S(1)}, f32[18,32,128]{2,1,0:T(8,128)S(1)}, f32[16,32,128]{2,1,0:T(8,128)S(1)}, f32[18,16,128]{2,1,0:T(8,128)S(1)}) custom-call(f32[18,56,256]{2,1,0:T(8,128)S(1)} %get-tuple-element.33.ext, bf16[256,128]{1,0:T(8,128)(2,1)S(1)} %copy-done.2, bf16[128,128]{1,0:T(8,128)(2,1)S(1)} %copy-done.5), custom_call_target="tpu_custom_call" | custom-call | tf_op jit(solution)/shard_map/pallas_call | solution.py:554
  17.8 0.0 collective-permute-done.4.ysub
  17.8 1.8 %collective-permute-done.5.ystrip = f32[6,56,128]{2,1,0:T(8,128)S(1)} collective-permute-done((f32[6,56,128]{2,1,0:T(8,128)S(1)}, f32[6,56,128]{2,1,0:T(8,128)S(1)}, u32[]{:S(2)}, u32[]{:S(2)}) %collective-permute-start.5) | collective-permute-done | bytes 172064 | tf_op jit(solution)/shard_map/ppermute | solution.py:32
  19.6 0.0 copy-done.3
  19.6 0.0 copy-done.4
  19.6 1.7 %shard_map.134 = (f32[18,56,128]{2,1,0:T(8,128)S(1)}, f32[16,40,128]{2,1,0:T(8,128)S(1)}, f32[18,32,128]{2,1,0:T(8,128)S(1)}, f32[16,32,128]{2,1,0:T(8,128)S(1)}...) custom-call(f32[18,56,256]{2,1,0:T(8,128)S(1)} %get-tuple-element.33.ext, ...), custom_call_target="tpu_custom_call" | custom-call | tf_op jit(solution)/shard_map/pallas_call | solution.py:554
  21.4 1.4 %collective-permute-start.6 = (f32[21,8,128]{2,1,0:T(8,128)S(1)}, f32[21,8,128]{2,1,0:T(8,128)S(1)}, u32[]{:S(2)}, u32[]{:S(2)}) collective-permute-start(f32[21,8,128]{2,1,0:T(8,128)S(1)} %get-tuple-element.38), channel_id=1, source_target_pairs={{0,4},{4,0},{8,12},{12,8},{1,5},{5,1},{9,13},{13,9},{2,6},{6,2},{1... | collective-permute-start | bytes 258056 | tf_op jit(solution)/shard_map/ppermute | solution.py:32
  22.8 0.0 collective-permute-start.7
  22.8 0.0 copy-start
  22.8 0.0 copy-start.1
  22.8 0.7 %shard_map.135 = (f32[2,40,384]{2,1,0:T(8,128)S(1)}, f32[16,40,384]{2,1,0:T(8,128)S(1)}, f32[16,40,384]{2,1,0:T(8,128)S(1)}, f32[2,40,384]{2,1,0:T(8,128)S(1)}, ...) custom-call(f32[18,56,256]{2,1,0:T(8,128)S(1)} %get-tuple-element.33, ...), custom_call_target="tpu_custom_call" | custom-call | tf_op jit(solution)/shard_map/pallas_call | solution.py:554
  23.5 2.6 %collective-permute-done.6.xa = f32[21,8,128]{2,1,0:T(8,128)S(1)} collective-permute-done((f32[21,8,128]{2,1,0:T(8,128)S(1)}, f32[21,8,128]{2,1,0:T(8,128)S(1)}, u32[]{:S(2)}, u32[]{:S(2)}) %collective-permute-start.6) | collective-permute-done | bytes 86048 | tf_op jit(solution)/shard_map/ppermute | solution.py:32
  26.0 0.0 collective-permute-done.7.xb
  26.0 0.0 copy-done
  26.0 0.0 copy-done.1
  26.0 4.6 %shard_map.136 = (f32[16,32,256]{2,1,0:T(8,128)}, f32[16,32,256]{2,1,0:T(8,128)}) custom-call(f32[18,16,128]{2,1,0:T(8,128)S(1)} %get-tuple-element.37.c_in, f32[21,8,128]{2,1,0:T(8,128)S(1)} %collective-permute-done.6.xa, f32[21,8,128]{2,1,0:T(8,128)S(1)} %collective-permute-done.7.xb, f32[18,56,256]{2,1,0:T(8,128)S(1)} %get-tuple-element.33.ext, ...), custom_call_target="tpu_custom_call" | custom-call | tf_op jit(solution)/shard_map/pallas_call | solution.py:656
  (2 shorter events, 0.0 us)
Async XLA Ops:
  1.8 4.7 %collective-permute-start.2 = (f32[1,8,128]{2,1,0:T(8,128)S(1)}, f32[1,8,128]{2,1,0:T(8,128)S(1)}, u32[]{:S(2)}, u32[]{:S(2)}) collective-permute-start(f32[1,8,128]{2,1,0:T(8,128)S(1)} %get-tuple-element.32), channel_id=1, source_target_pairs={{0,4},{4,0},{8,12},{12,8},{1,5},{5,1},{9,13},{13,9},{2,6},{6,2},{1... | collective-permute-start | bytes 12296 | tf_op jit(solution)/shard_map/ppermute | solution.py:596
  4.9 8.3 %collective-permute-start = (f32[27,8,256]{2,1,0:T(8,128)S(1)}, f32[27,8,256]{2,1,0:T(8,128)S(1)}, u32[]{:S(2)}, u32[]{:S(2)}) collective-permute-start(f32[27,8,256]{2,1,0:T(8,128)S(1)} %get-tuple-element.30), channel_id=1, source_target_pairs={{0,4},{4,0},{8,12},{12,8},{1,5},{5,1},{9,13},{13,9},{2,6},{6,2},{1... | collective-permute-start | bytes 663560 | tf_op jit(solution)/shard_map/ppermute | solution.py:32
  5.0 8.3 %collective-permute-start.1 = (f32[27,8,256]{2,1,0:T(8,128)S(1)}, f32[27,8,256]{2,1,0:T(8,128)S(1)}, u32[]{:S(2)}, u32[]{:S(2)}) collective-permute-start(f32[27,8,256]{2,1,0:T(8,128)S(1)} %get-tuple-element.31), channel_id=1, source_target_pairs={{0,1},{4,8},{8,4},{12,13},{1,0},{5,9},{9,5},{13,12},{2,3},{6,10},{... | collective-permute-start | bytes 663560 | tf_op jit(solution)/shard_map/ppermute | solution.py:32
  6.5 6.7 %collective-permute-start.3 = (f32[2,8,128]{2,1,0:T(8,128)S(1)}, f32[2,8,128]{2,1,0:T(8,128)S(1)}, u32[]{:S(2)}, u32[]{:S(2)}) collective-permute-start(f32[2,8,128]{2,1,0:T(8,128)S(1)} %pad_maximum_fusion.1), channel_id=1, source_target_pairs={{0,8},{4,12},{8,0},{12,4},{1,9},{5,13},{9,1},{13,5},{2,10},{6,14},... | collective-permute-start | bytes 24584 | tf_op jit(solution)/shard_map/ppermute | solution.py:603
  13.3 2.5 %copy-start.2 = (bf16[256,128]{1,0:T(8,128)(2,1)S(1)}, bf16[256,128]{1,0:T(8,128)(2,1)}, u32[]{:S(2)}) copy-start(bf16[256,128]{1,0:T(8,128)(2,1)} %constant.12.clone.c1) | copy-start | bytes 196612
  13.3 2.5 %copy-start.5 = (bf16[128,128]{1,0:T(8,128)(2,1)S(1)}, bf16[128,128]{1,0:T(8,128)(2,1)}, u32[]{:S(2)}) copy-start(bf16[128,128]{1,0:T(8,128)(2,1)} %constant.13.clone.c2) | copy-start | bytes 98308
  14.1 3.7 %collective-permute-start.4 = (f32[6,56,128]{2,1,0:T(8,128)S(1)}, f32[6,56,128]{2,1,0:T(8,128)S(1)}, u32[]{:S(2)}, u32[]{:S(2)}) collective-permute-start(f32[6,56,128]{2,1,0:T(8,128)S(1)} %get-tuple-element.34), channel_id=1, source_target_pairs={{0,1},{1,0},{2,3},{3,2},{16,17},{17,16},{18,19},{19,18},{4,5},{5,4... | collective-permute-start | bytes 516104 | tf_op jit(solution)/shard_map/ppermute | solution.py:32
  14.2 5.5 %collective-permute-start.5 = (f32[6,56,128]{2,1,0:T(8,128)S(1)}, f32[6,56,128]{2,1,0:T(8,128)S(1)}, u32[]{:S(2)}, u32[]{:S(2)}) collective-permute-start(f32[6,56,128]{2,1,0:T(8,128)S(1)} %get-tuple-element.35), channel_id=1, source_target_pairs={{0,16},{1,2},{2,1},{3,19},{16,0},{17,18},{18,17},{19,3},{4,20},{5,... | collective-permute-start | bytes 516104 | tf_op jit(solution)/shard_map/ppermute | solution.py:32
  15.7 3.9 %copy-start.3 = (bf16[128,128]{1,0:T(8,128)(2,1)S(1)}, bf16[128,128]{1,0:T(8,128)(2,1)}, u32[]{:S(2)}) copy-start(bf16[128,128]{1,0:T(8,128)(2,1)} %constant.15.clone.c2) | copy-start | bytes 98308
  15.7 3.9 %copy-start.4 = (bf16[128,128]{1,0:T(8,128)(2,1)S(1)}, bf16[128,128]{1,0:T(8,128)(2,1)}, u32[]{:S(2)}) copy-start(bf16[128,128]{1,0:T(8,128)(2,1)} %constant.14.clone.c1) | copy-start | bytes 98308
  21.4 4.6 %collective-permute-start.6 = (f32[21,8,128]{2,1,0:T(8,128)S(1)}, f32[21,8,128]{2,1,0:T(8,128)S(1)}, u32[]{:S(2)}, u32[]{:S(2)}) collective-permute-start(f32[21,8,128]{2,1,0:T(8,128)S(1)} %get-tuple-element.38), channel_id=1, source_target_pairs={{0,4},{4,0},{8,12},{12,8},{1,5},{5,1},{9,13},{13,9},{2,6},{6,2},{1... | collective-permute-start | bytes 258056 | tf_op jit(solution)/shard_map/ppermute | solution.py:32
  22.8 3.2 %collective-permute-start.7 = (f32[21,8,128]{2,1,0:T(8,128)S(1)}, f32[21,8,128]{2,1,0:T(8,128)S(1)}, u32[]{:S(2)}, u32[]{:S(2)}) collective-permute-start(f32[21,8,128]{2,1,0:T(8,128)S(1)} %get-tuple-element.39), channel_id=1, source_target_pairs={{0,1},{4,8},{8,4},{12,13},{1,0},{5,9},{9,5},{13,12},{2,3},{6,10},{... | collective-permute-start | bytes 258056 | tf_op jit(solution)/shard_map/ppermute | solution.py:32
  22.8 3.2 %copy-start = (bf16[256,384]{1,0:T(8,128)(2,1)S(1)}, bf16[256,384]{1,0:T(8,128)(2,1)}, u32[]{:S(2)}) copy-start(bf16[256,384]{1,0:T(8,128)(2,1)} %constant.16.clone.p1) | copy-start | bytes 589828
  22.8 3.2 %copy-start.1 = (bf16[128,256]{1,0:T(8,128)(2,1)S(1)}, bf16[128,256]{1,0:T(8,128)(2,1)}, u32[]{:S(2)}) copy-start(bf16[128,256]{1,0:T(8,128)(2,1)} %constant.17.clone.p2) | copy-start | bytes 196612

commit v5 on v4

--- a/solution.py
+++ b/solution.py
@@ -132,6 +132,17 @@
     for j in range(ref.shape[1]):
         for s in (0, 1):
             ref[l, j, pl.ds(s, n, stride=2), :] = part[:, 128 * j : 128 * (j + 1)]
+
+
+def slab_of(layers, at_right):
+    shape = layers[0].shape
+    lane = lax.broadcasted_iota(jnp.int32, shape, 1)
+    out = jnp.zeros(shape, jnp.float32)
+    for k, x in enumerate(layers):
+        shift = (HY * (k + 1) if at_right else HY * k) % 128
+        x = pltpu.roll(x, shift, 1) if shift else x
+        out = jnp.where((lane >= HY * k) & (lane < HY * (k + 1)), x, out)
+    return out
 
 
 def load_kernel(rs, kh, kv, owner, cell, pressure, x, panels, a_out, b_out, ints, sems):
@@ -179,6 +190,17 @@
         last(b_out)
 
 
+def own_columns_kernel(x, sub_out, strip_out):
+    count, _, cols = x.shape
+    _, _, y_even = y_sides()
+    for g in range(count // SLABS):
+        layers = range(SLABS * g, SLABS * g + SLABS)
+        to_right = slab_of([x[l, :, cols - 128 : cols] for l in layers], True)
+        to_left = slab_of([x[l, :, 0:128] for l in layers], False)
+        sub_out[g] = jnp.where(y_even, to_right, to_left)
+        strip_out[g] = jnp.where(y_even, to_left, to_right)
+
+
 def forcing_kernel(x_own, xa, xb, panels, ext, sub_out, strip_out):
     count, rows, cols = x_own.shape
     depth = count - 2
@@ -232,26 +254,50 @@
     total = parts[0:span] + parts[span : 2 * span] + parts[2 * span :]
     ext[depth - 1] = ext[depth - 1] + total
 
-    y = lax.axis_index("strip") * lax.axis_size("sub") + lax.axis_index("sub")
-    y_even = y % 2 == 0
-    lane = lax.broadcasted_iota(jnp.int32, (span, 128), 1)
-
-    def slab(g, at_right):
-        out = jnp.zeros((span, 128), jnp.float32)
-        for k in range(SLABS):
-            if at_right:
-                x = pltpu.roll(ext[SLABS * g + k, :, cols - 128 : cols], (HY + HY * k) % 128, 1)
-            else:
-                x = ext[SLABS * g + k, :, 0:128]
-                x = pltpu.roll(x, HY * k, 1) if k else x
-            out = jnp.where((lane >= HY * k) & (lane < HY * (k + 1)), x, out)
-        return out
-
-    for g in range(count // SLABS):
-        to_right = slab(g, True)
-        to_left = slab(g, False)
+    _, _, y_even = y_sides()
+    slabs = count // SLABS
+
+    def send(g, to_right, to_left):
         sub_out[g] = jnp.where(y_even, to_right, to_left)
         strip_out[g] = jnp.where(y_even, to_left, to_right)
+
+    def corners(l, first):
+        return jnp.concatenate(
+            [ext[l, 0:HX, first : first + 128], ext[l, high : high + HX, first : first + 128]], 0
+        )
+
+    for g in range(slabs):
+        layers = range(SLABS * g, SLABS * g + SLABS)
+        send(g, slab_of([corners(l, cols - 128) for l in layers], True), slab_of([corners(l, 0) for l in layers], False))
+    pad = jnp.zeros((2 * HX - rows // 2, 128), jnp.float32)
+    halves = [total[HX : HX + rows // 2], total[HX + rows // 2 : high]]
+    send(
+        slabs,
+        jnp.concatenate([slab_of([x[:, cols - 128 :] for x in halves], True), pad], 0),
+        jnp.concatenate([slab_of([x[:, :128] for x in halves], False), pad], 0),
+    )
+
+
+def rolled(x, shift):
+    return pltpu.roll(x, shift % 128, 1) if shift % 128 else x
+
+
+def base_kernel(ext, ysub, ystrip, base):
+    count, span, cols = ext.shape
+    high = span - HX
+    _, _, y_even = y_sides()
+    lane = lax.broadcasted_iota(jnp.int32, (span, 128), 1)
+    lane_own = lane[HX:high]
+    for g in range(count // SLABS):
+        from_right = jnp.where(y_even, ysub[g], ystrip[g])
+        from_left = jnp.where(y_even, ystrip[g], ysub[g])
+        for k in range(SLABS):
+            l = SLABS * g + k
+            x = jnp.where(lane >= 128 - EDGE, ext[l, :, cols - 128 : cols], 0.0)
+            x = jnp.where((lane >= 2 * HY) & (lane < 2 * HY + EDGE), rolled(ext[l, :, 0:128], 2 * HY), x)
+            base[l] = x
+            outer = jnp.where(lane_own < HY, rolled(from_right, -HY * k), rolled(from_left, HY - HY * k))
+            base[l, HX:high, :] = jnp.where(lane_own < 2 * HY, outer, x[HX:high])
 
 
 def row_inside(shape, rows, above):
@@ -349,29 +395,34 @@
 
 
 def edge_kernel(
-    ext, ysub, ystrip, c_inner, c1, c2,
+    base, ysub, ystrip, c_inner, c1, c2,
     b_out, u_out, b1_out, u1_out, c_out, a_msg, b_msg,
     w0, al0, be0, u0, u0n, r0, w1, al1, be1, u1, u1n, r1,
 ):
-    depth, span, cols = ext.shape[0] - 2, ext.shape[1], ext.shape[2]
+    count, span = base.shape[:2]
+    depth = count - 2
     rows = span - 2 * HX
-    count = depth + 2
+    high = span - HX
     even = lax.axis_index("tile") % 2 == 0
     _, _, y_even = y_sides()
-    lane = lax.broadcasted_iota(jnp.int32, (span, 128), 1)
-
-    def rolled(x, shift):
-        return pltpu.roll(x, shift % 128, 1) if shift % 128 else x
-
-    for g in range(count // SLABS):
+    slabs = count // SLABS
+    lane = lax.broadcasted_iota(jnp.int32, (2 * HX, 128), 1)
+    for g in range(slabs):
         from_right = jnp.where(y_even, ysub[g], ystrip[g])
         from_left = jnp.where(y_even, ystrip[g], ysub[g])
         for k in range(SLABS):
             l = SLABS * g + k
-            x = jnp.where(lane >= 128 - EDGE, ext[l, :, cols - 128 : cols], 0.0)
-            x = jnp.where((lane >= 2 * HY) & (lane < 2 * HY + EDGE), rolled(ext[l, :, 0:128], 2 * HY), x)
-            x = jnp.where((lane >= HY) & (lane < 2 * HY), rolled(from_left, HY - HY * k), x)
-            b_out[l] = jnp.where(lane < HY, rolled(from_right, -HY * k), x)
+            outer = jnp.where(lane < HY, rolled(from_right, -HY * k), rolled(from_left, HY - HY * k))
+            b_out[l, 0:HX, :] = jnp.where(lane[:HX] < 2 * HY, outer[:HX], base[l, 0:HX, :])
+            b_out[l, high:span, :] = jnp.where(lane[HX:] < 2 * HY, outer[HX:], base[l, high:span, :])
+    half = rows // 2
+    lane = lane[:half]
+    from_right = jnp.where(y_even, ysub[slabs, :half], ystrip[slabs, :half])
+    from_left = jnp.where(y_even, ystrip[slabs, :half], ysub[slabs, :half])
+    for k in (0, 1):
+        force = jnp.where(lane < HY, rolled(from_right, -HY * k), rolled(from_left, HY - HY * k))
+        part = pl.ds(HX + half * k, half)
+        b_out[depth - 1, part, :] = base[depth - 1, part, :] + jnp.where(lane < 2 * HY, force, 0.0)
     presmooth(
         b_out, b_out[depth], b_out[depth + 1], 1.0, edge_inside((span, 128), rows, HX, HY, EDGE),
         w0, al0, be0, u0, u0n, depth,
@@ -549,7 +600,7 @@
 VM = pl.BlockSpec(memory_space=pltpu.VMEM)
 
 
-def call(kernel, outs, scratch, *args):
+def call(kernel, outs, scratch, *args, aliases={}):
     f32 = lambda shape: jax.ShapeDtypeStruct(shape, jnp.float32)
     return pl.pallas_call(
         kernel,
@@ -557,6 +608,7 @@
         in_specs=[VM] * len(args),
         out_specs=[VM] * len(outs),
         scratch_shapes=[pltpu.VMEM(s, jnp.float32) for s in scratch],
+        input_output_aliases=aliases,
         compiler_params=pltpu.CompilerParams(vmem_limit_bytes=24 << 20),
     )(*args)
 
@@ -577,6 +629,7 @@
 
     message = (count + count // 2, 8, cols)
     f32 = lambda shape: jax.ShapeDtypeStruct(shape, jnp.float32)
+    early = (count // SLABS, rows, 128)
     x_own, panels, a, b = pl.pallas_call(
         load_kernel,
         out_shape=[f32((count, rows, cols)), f32((1, 8, 128)), f32(message), f32(message)],
@@ -596,6 +649,9 @@
     near = lax.ppermute(panels, "tile", [(i, i ^ 1) for i in range(tiles)])
     a = neighbour_swap(a, "tile", 0, "sub")
     b = neighbour_swap(b, "tile", 1, "sub")
+    sub_own, strip_own = call(own_columns_kernel, [early, early], [], x_own)
+    sub_own = neighbour_swap(sub_own, y_axes, 0, "group")
+    strip_own = neighbour_swap(strip_own, y_axes, 1, "group")
     panels = jnp.concatenate([panels, near], 0)
     step = 2
     while step < tiles:
@@ -603,7 +659,7 @@
         panels = jnp.concatenate([panels, lax.ppermute(panels, "tile", swap)], 0)
         step *= 2
 
-    slabs = (count // SLABS, span, 128)
+    slabs = (count // SLABS + 1, 2 * HX, 128)
     ext, sub, strip = call(
         forcing_kernel, [(count, span, cols), slabs, slabs], [],
         x_own, a, b, panels,
@@ -628,6 +684,7 @@
         down_scratch(cols, half),
         ext, c1_inner, c2_inner,
     )
+    (base,) = call(base_kernel, [(count, span, 128)], [], ext, sub_own, strip_own)
     message2 = (count + (count + 7) // 8, 8, half)
     edge, u_edge, b1_edge, u1_edge, c_own, a2, b2 = call(
         edge_kernel,
@@ -636,7 +693,8 @@
             (count, span2, half), message2, message2,
         ],
         down_scratch(128, 128),
-        ext, sub, strip, c_in, c1_edge, c2_edge,
+        base, sub, strip, c_in, c1_edge, c2_edge,
+        aliases={0: 0},
     )
     a2 = neighbour_swap(a2, "tile", 0, "sub")
     b2 = neighbour_swap(b2, "tile", 1, "sub")

time: 30.8 us -> 29.6 us (0.961)
  waiting for transfers between devices: 9.59 us -> 6.49 us
  starting transfers between devices: 9.25 us -> 10.9 us
    ppermute x1, waiting for transfers between devices: 3.71 us -> 1.85 us  [body(): panels = jnp.concatenate([panels, lax.ppermute(panels, 'tile', swap)], 0)]
    ppermute x6 -> x8, starting transfers between devices: 3.13 us -> 4.77 us  [neighbour_swap(): lax.ppermute(x, (spare,) + axis if leading else axis + (spare,), pairs)]
    ppermute x6 -> x8, waiting for transfers between devices: 4.37 us -> 3.13 us  [neighbour_swap(): lax.ppermute(x, (spare,) + axis if leading else axis + (spare,), pairs)]
    pallas_call x4 -> x6, Pallas kernels: 5.24 us -> 5.51 us  [call(): pl.pallas_call(kernel, out_shape=[f32(s) for s in outs], in_specs=[VM] *...]
  transfers between devices with their start and end apart: 8 -> 10, of which waited for: 4 -> 4; matrix products, arithmetic and copies ran while one was open for 0% -> 0% of each run, Pallas kernels for 9% -> 13%
where the time goes in v5:
time: 29.6 us; the launch traced here: 29.5 us
  Pallas kernels  11.3 us (38%)
  starting transfers between devices  10.9 us (37%)
  waiting for transfers between devices  6.49 us (22%)
  between operations  0.76 us (3%)
    pallas_call x6, Pallas kernels, call(): pl.pallas_call(kernel, out_shape=[f32(s) for s in outs], in_specs=[VM] *...  5.51 us
    ppermute x8, starting transfers between devices, neighbour_swap(): lax.ppermute(x, (spare,) + axis if leading else axis + (spare,), pairs)  4.77 us
    pallas_call x1, Pallas kernels, body(): pl.pallas_call(up_kernel, out_shape=[f32(own), f32(own)], in_specs=[VM] *...  4.58 us
    ppermute x8, waiting for transfers between devices, neighbour_swap(): lax.ppermute(x, (spare,) + axis if leading else axis + (spare,), pairs)  3.13 us
    ppermute x1, starting transfers between devices, body(): near = lax.ppermute(panels, 'tile', [(i, i ^ 1) for i in range(tiles)])  3.09 us
    ppermute x1, starting transfers between devices, body(): panels = jnp.concatenate([panels, lax.ppermute(panels, 'tile', swap)], 0)  3.03 us
    ppermute x1, waiting for transfers between devices, body(): panels = jnp.concatenate([panels, lax.ppermute(panels, 'tile', swap)], 0)  1.85 us
    ppermute x1, waiting for transfers between devices, body(): near = lax.ppermute(panels, 'tile', [(i, i ^ 1) for i in range(tiles)])  1.5 us
  transfers between devices with their start and end apart: 10, of which 4 were waited for; matrix products, arithmetic and copies ran while one was open for 0% of the time, Pallas kernels for 13%

profile of v5, /device:TPU:0, one launch (start us, length us, event | category | flops | bytes accessed | tf_op | source)
XLA Modules:
  0.0 29.5 jit_solution(6464361214047824819)
XLA Ops:
  0.6 1.2 %shard_map.131 = (f32[18,32,256]{2,1,0:T(8,128)S(1)}, f32[1,8,128]{2,1,0:T(8,128)S(1)}, f32[27,8,256]{2,1,0:T(8,128)S(1)}, f32[27,8,256]{2,1,0:T(8,128)S(1)}) custom-call(f32[16,32,256]{2,1,0:T(8,128)} %rs.1, f32[32,256]{1,0:T(8,128)} %kh.1, f32[32,256]{1,0:T(8,128)} %kv.1, s32[4,128]{1,0:T(4,128)} %bitcast.3, s32[4,128]{1,0:T(4,128)} %bitcast.4, ...), custom_call_target="tpu_custom_call" | custom-call | tf_op jit(solution)/shard_map/pallas_call | solution.py:633
  1.8 3.1 %collective-permute-start.2 = (f32[1,8,128]{2,1,0:T(8,128)S(1)}, f32[1,8,128]{2,1,0:T(8,128)S(1)}, u32[]{:S(2)}, u32[]{:S(2)}) collective-permute-start(f32[1,8,128]{2,1,0:T(8,128)S(1)} %get-tuple-element.34), channel_id=1, source_target_pairs={{0,4},{4,0},{8,12},{12,8},{1,5},{5,1},{9,13},{13,9},{2,6},{6,2},{1... | collective-permute-start | bytes 12296 | tf_op jit(solution)/shard_map/ppermute | solution.py:649
  4.9 0.1 collective-permute-start
  5.0 0.0 collective-permute-start.1
  5.0 1.5 %collective-permute-done.2 = f32[1,8,128]{2,1,0:T(8,128)S(1)} collective-permute-done((f32[1,8,128]{2,1,0:T(8,128)S(1)}, f32[1,8,128]{2,1,0:T(8,128)S(1)}, u32[]{:S(2)}, u32[]{:S(2)}) %collective-permute-start.2) | collective-permute-done | bytes 4128 | tf_op jit(solution)/shard_map/ppermute | solution.py:649
  6.5 3.0 %collective-permute-start.3 = (f32[2,8,128]{2,1,0:T(8,128)S(1)}, f32[2,8,128]{2,1,0:T(8,128)S(1)}, u32[]{:S(2)}, u32[]{:S(2)}) collective-permute-start(f32[2,8,128]{2,1,0:T(8,128)S(1)} %pad_maximum_fusion.1), channel_id=1, source_target_pairs={{0,8},{4,12},{8,0},{12,4},{1,9},{5,13},{9,1},{13,5},{2,10},{6,14},... | collective-permute-start | bytes 24584 | tf_op jit(solution)/shard_map/ppermute | solution.py:659
  9.5 0.2 shard_map.133
  9.7 0.1 collective-permute-start.4
  9.8 1.6 %collective-permute-start.5 = (f32[6,32,128]{2,1,0:T(8,128)S(1)}, f32[6,32,128]{2,1,0:T(8,128)S(1)}, u32[]{:S(2)}, u32[]{:S(2)}) collective-permute-start(f32[6,32,128]{2,1,0:T(8,128)S(1)} %get-tuple-element.37), channel_id=1, source_target_pairs={{0,16},{1,2},{2,1},{3,19},{16,0},{17,18},{18,17},{19,3},{4,20},{5,... | collective-permute-start | bytes 294920 | tf_op jit(solution)/shard_map/ppermute | solution.py:32
  11.4 1.9 %collective-permute-done.3 = f32[2,8,128]{2,1,0:T(8,128)S(1)} collective-permute-done((f32[2,8,128]{2,1,0:T(8,128)S(1)}, f32[2,8,128]{2,1,0:T(8,128)S(1)}, u32[]{:S(2)}, u32[]{:S(2)}) %collective-permute-start.3) | collective-permute-done | bytes 8224 | tf_op jit(solution)/shard_map/ppermute | solution.py:659
  13.3 0.0 copy-start.2
  13.3 0.0 copy-start.5
  13.3 0.0 collective-permute-done.xa
  13.3 0.0 collective-permute-done.1.xb
  13.3 0.8 %shard_map.132 = (f32[18,56,256]{2,1,0:T(8,128)S(1)}, f32[7,24,128]{2,1,0:T(8,128)S(1)}, f32[7,24,128]{2,1,0:T(8,128)S(1)}) custom-call(f32[18,32,256]{2,1,0:T(8,128)S(1)} %get-tuple-element.31.x_own.x, f32[27,8,256]{2,1,0:T(8,128)S(1)} %collective-permute-done.xa, f32[27,8,256]{2,1,0:T(8,128)S(1)} %collective-permute-done.1.xb, ...), custom_call_target="tpu_custom_call" | custom-call | tf_op jit(solution)/shard_map/pallas_call | solution.py:605
  14.0 0.1 collective-permute-start.6
  14.1 1.6 %collective-permute-start.7 = (f32[7,24,128]{2,1,0:T(8,128)S(1)}, f32[7,24,128]{2,1,0:T(8,128)S(1)}, u32[]{:S(2)}, u32[]{:S(2)}) collective-permute-start(f32[7,24,128]{2,1,0:T(8,128)S(1)} %get-tuple-element.39), channel_id=1, source_target_pairs={{0,16},{1,2},{2,1},{3,19},{16,0},{17,18},{18,17},{19,3},{4,20},{5,... | collective-permute-start | bytes 258056 | tf_op jit(solution)/shard_map/ppermute | solution.py:32
  15.7 0.0 copy-done.2
  15.7 0.0 copy-done.5
  15.7 2.1 %shard_map.135 = (f32[16,40,256]{2,1,0:T(8,128)S(1)}, f32[18,32,128]{2,1,0:T(8,128)S(1)}, f32[16,32,128]{2,1,0:T(8,128)S(1)}, f32[18,16,128]{2,1,0:T(8,128)S(1)}) custom-call(f32[18,56,256]{2,1,0:T(8,128)S(1)} %get-tuple-element.35.ext, bf16[256,128]{1,0:T(8,128)(2,1)S(1)} %copy-done.2, bf16[128,128]{1,0:T(8,128)(2,1)S(1)} %copy-done.5), custom_call_target="tpu_custom_call" | custom-call | tf_op jit(solution)/shard_map/pallas_call | solution.py:605
  17.8 0.0 copy-start.3
  17.8 0.0 copy-start.4
  17.8 0.0 collective-permute-done.4.ysub
  17.8 0.0 collective-permute-done.5.ystrip
  17.8 0.3 %shard_map.134.base = f32[18,56,128]{2,1,0:T(8,128)S(1)} custom-call(f32[18,56,256]{2,1,0:T(8,128)S(1)} %get-tuple-element.35.ext, f32[6,32,128]{2,1,0:T(8,128)S(1)} %collective-permute-done.4.ysub, f32[6,32,128]{2,1,0:T(8,128)S(1)} %collective-permute-done.5.ystrip), custom_call_target="tpu_custom_call" | custom-call | tf_op jit(solution)/shard_map/pallas_call | solution.py:605
  18.1 0.0 collective-permute-done.6.ysub
  18.1 0.5 %collective-permute-done.7.ystrip = f32[7,24,128]{2,1,0:T(8,128)S(1)} collective-permute-done((f32[7,24,128]{2,1,0:T(8,128)S(1)}, f32[7,24,128]{2,1,0:T(8,128)S(1)}, u32[]{:S(2)}, u32[]{:S(2)}) %collective-permute-start.7) | collective-permute-done | bytes 86048 | tf_op jit(solution)/shard_map/ppermute | solution.py:32
  18.7 0.0 copy-done.3
  18.7 0.0 copy-done.4
  18.7 1.6 %shard_map.136 = (f32[18,56,128]{2,1,0:T(8,128)S(1)}, f32[16,40,128]{2,1,0:T(8,128)S(1)}, f32[18,32,128]{2,1,0:T(8,128)S(1)}, f32[16,32,128]{2,1,0:T(8,128)S(1)}...) custom-call(f32[18,56,128]{2,1,0:T(8,128)S(1)} %shard_map.134.base, ...), custom_call_target="tpu_custom_call", output_to_operand_aliasing={{0}: (0, {})} | custom-call | tf_op jit(solution)/shard_map/pallas_call | solution.py:605
  20.2 1.4 %collective-permute-start.8 = (f32[21,8,128]{2,1,0:T(8,128)S(1)}, f32[21,8,128]{2,1,0:T(8,128)S(1)}, u32[]{:S(2)}, u32[]{:S(2)}) collective-permute-start(f32[21,8,128]{2,1,0:T(8,128)S(1)} %get-tuple-element.42), channel_id=1, source_target_pairs={{0,4},{4,0},{8,12},{12,8},{1,5},{5,1},{9,13},{13,9},{2,6},{6,2},{1... | collective-permute-start | bytes 258056 | tf_op jit(solution)/shard_map/ppermute | solution.py:32
  21.6 0.0 collective-permute-start.9
  21.6 0.0 copy-start
  21.6 0.0 copy-start.1
  21.6 0.6 %shard_map.137 = (f32[2,40,384]{2,1,0:T(8,128)S(1)}, f32[16,40,384]{2,1,0:T(8,128)S(1)}, f32[16,40,384]{2,1,0:T(8,128)S(1)}, f32[2,40,384]{2,1,0:T(8,128)S(1)}, ...) custom-call(f32[18,56,256]{2,1,0:T(8,128)S(1)} %get-tuple-element.35, ...), custom_call_target="tpu_custom_call" | custom-call | tf_op jit(solution)/shard_map/pallas_call | solution.py:605
  22.3 2.6 %collective-permute-done.8.xa = f32[21,8,128]{2,1,0:T(8,128)S(1)} collective-permute-done((f32[21,8,128]{2,1,0:T(8,128)S(1)}, f32[21,8,128]{2,1,0:T(8,128)S(1)}, u32[]{:S(2)}, u32[]{:S(2)}) %collective-permute-start.8) | collective-permute-done | bytes 86048 | tf_op jit(solution)/shard_map/ppermute | solution.py:32
  24.9 0.0 collective-permute-done.9.xb
  24.9 0.0 copy-done
  24.9 0.0 copy-done.1
  24.9 4.6 %shard_map.138 = (f32[16,32,256]{2,1,0:T(8,128)}, f32[16,32,256]{2,1,0:T(8,128)}) custom-call(f32[18,16,128]{2,1,0:T(8,128)S(1)} %get-tuple-element.41.c_in, f32[21,8,128]{2,1,0:T(8,128)S(1)} %collective-permute-done.8.xa, f32[21,8,128]{2,1,0:T(8,128)S(1)} %collective-permute-done.9.xb, f32[18,56,256]{2,1,0:T(8,128)S(1)} %get-tuple-element.35.ext, ...), custom_call_target="tpu_custom_call" | custom-call | tf_op jit(solution)/shard_map/pallas_call | solution.py:714
  (2 shorter events, 0.0 us)
Async XLA Ops:
  1.8 4.7 %collective-permute-start.2 = (f32[1,8,128]{2,1,0:T(8,128)S(1)}, f32[1,8,128]{2,1,0:T(8,128)S(1)}, u32[]{:S(2)}, u32[]{:S(2)}) collective-permute-start(f32[1,8,128]{2,1,0:T(8,128)S(1)} %get-tuple-element.34), channel_id=1, source_target_pairs={{0,4},{4,0},{8,12},{12,8},{1,5},{5,1},{9,13},{13,9},{2,6},{6,2},{1... | collective-permute-start | bytes 12296 | tf_op jit(solution)/shard_map/ppermute | solution.py:649
  4.9 8.3 %collective-permute-start = (f32[27,8,256]{2,1,0:T(8,128)S(1)}, f32[27,8,256]{2,1,0:T(8,128)S(1)}, u32[]{:S(2)}, u32[]{:S(2)}) collective-permute-start(f32[27,8,256]{2,1,0:T(8,128)S(1)} %get-tuple-element.32), channel_id=1, source_target_pairs={{0,4},{4,0},{8,12},{12,8},{1,5},{5,1},{9,13},{13,9},{2,6},{6,2},{1... | collective-permute-start | bytes 663560 | tf_op jit(solution)/shard_map/ppermute | solution.py:32
  5.0 8.3 %collective-permute-start.1 = (f32[27,8,256]{2,1,0:T(8,128)S(1)}, f32[27,8,256]{2,1,0:T(8,128)S(1)}, u32[]{:S(2)}, u32[]{:S(2)}) collective-permute-start(f32[27,8,256]{2,1,0:T(8,128)S(1)} %get-tuple-element.33), channel_id=1, source_target_pairs={{0,1},{4,8},{8,4},{12,13},{1,0},{5,9},{9,5},{13,12},{2,3},{6,10},{... | collective-permute-start | bytes 663560 | tf_op jit(solution)/shard_map/ppermute | solution.py:32
  6.5 6.7 %collective-permute-start.3 = (f32[2,8,128]{2,1,0:T(8,128)S(1)}, f32[2,8,128]{2,1,0:T(8,128)S(1)}, u32[]{:S(2)}, u32[]{:S(2)}) collective-permute-start(f32[2,8,128]{2,1,0:T(8,128)S(1)} %pad_maximum_fusion.1), channel_id=1, source_target_pairs={{0,8},{4,12},{8,0},{12,4},{1,9},{5,13},{9,1},{13,5},{2,10},{6,14},... | collective-permute-start | bytes 24584 | tf_op jit(solution)/shard_map/ppermute | solution.py:659
  9.7 8.1 %collective-permute-start.4 = (f32[6,32,128]{2,1,0:T(8,128)S(1)}, f32[6,32,128]{2,1,0:T(8,128)S(1)}, u32[]{:S(2)}, u32[]{:S(2)}) collective-permute-start(f32[6,32,128]{2,1,0:T(8,128)S(1)} %get-tuple-element.36), channel_id=1, source_target_pairs={{0,1},{1,0},{2,3},{3,2},{16,17},{17,16},{18,19},{19,18},{4,5},{5,4... | collective-permute-start | bytes 294920 | tf_op jit(solution)/shard_map/ppermute | solution.py:32
  9.8 8.0 %collective-permute-start.5 = (f32[6,32,128]{2,1,0:T(8,128)S(1)}, f32[6,32,128]{2,1,0:T(8,128)S(1)}, u32[]{:S(2)}, u32[]{:S(2)}) collective-permute-start(f32[6,32,128]{2,1,0:T(8,128)S(1)} %get-tuple-element.37), channel_id=1, source_target_pairs={{0,16},{1,2},{2,1},{3,19},{16,0},{17,18},{18,17},{19,3},{4,20},{5,... | collective-permute-start | bytes 294920 | tf_op jit(solution)/shard_map/ppermute | solution.py:32
  13.3 2.5 %copy-start.2 = (bf16[256,128]{1,0:T(8,128)(2,1)S(1)}, bf16[256,128]{1,0:T(8,128)(2,1)}, u32[]{:S(2)}) copy-start(bf16[256,128]{1,0:T(8,128)(2,1)} %constant.12.clone.c1) | copy-start | bytes 196612
  13.3 2.5 %copy-start.5 = (bf16[128,128]{1,0:T(8,128)(2,1)S(1)}, bf16[128,128]{1,0:T(8,128)(2,1)}, u32[]{:S(2)}) copy-start(bf16[128,128]{1,0:T(8,128)(2,1)} %constant.13.clone.c2) | copy-start | bytes 98308
  14.0 4.1 %collective-permute-start.6 = (f32[7,24,128]{2,1,0:T(8,128)S(1)}, f32[7,24,128]{2,1,0:T(8,128)S(1)}, u32[]{:S(2)}, u32[]{:S(2)}) collective-permute-start(f32[7,24,128]{2,1,0:T(8,128)S(1)} %get-tuple-element.38), channel_id=1, source_target_pairs={{0,1},{1,0},{2,3},{3,2},{16,17},{17,16},{18,19},{19,18},{4,5},{5,4... | collective-permute-start | bytes 258056 | tf_op jit(solution)/shard_map/ppermute | solution.py:32
  14.1 4.6 %collective-permute-start.7 = (f32[7,24,128]{2,1,0:T(8,128)S(1)}, f32[7,24,128]{2,1,0:T(8,128)S(1)}, u32[]{:S(2)}, u32[]{:S(2)}) collective-permute-start(f32[7,24,128]{2,1,0:T(8,128)S(1)} %get-tuple-element.39), channel_id=1, source_target_pairs={{0,16},{1,2},{2,1},{3,19},{16,0},{17,18},{18,17},{19,3},{4,20},{5,... | collective-permute-start | bytes 258056 | tf_op jit(solution)/shard_map/ppermute | solution.py:32
  17.8 0.9 %copy-start.3 = (bf16[128,128]{1,0:T(8,128)(2,1)S(1)}, bf16[128,128]{1,0:T(8,128)(2,1)}, u32[]{:S(2)}) copy-start(bf16[128,128]{1,0:T(8,128)(2,1)} %constant.15.clone.c2) | copy-start | bytes 98308
  17.8 0.9 %copy-start.4 = (bf16[128,128]{1,0:T(8,128)(2,1)S(1)}, bf16[128,128]{1,0:T(8,128)(2,1)}, u32[]{:S(2)}) copy-start(bf16[128,128]{1,0:T(8,128)(2,1)} %constant.14.clone.c1) | copy-start | bytes 98308
  20.2 4.6 %collective-permute-start.8 = (f32[21,8,128]{2,1,0:T(8,128)S(1)}, f32[21,8,128]{2,1,0:T(8,128)S(1)}, u32[]{:S(2)}, u32[]{:S(2)}) collective-permute-start(f32[21,8,128]{2,1,0:T(8,128)S(1)} %get-tuple-element.42), channel_id=1, source_target_pairs={{0,4},{4,0},{8,12},{12,8},{1,5},{5,1},{9,13},{13,9},{2,6},{6,2},{1... | collective-permute-start | bytes 258056 | tf_op jit(solution)/shard_map/ppermute | solution.py:32
  21.6 3.2 %collective-permute-start.9 = (f32[21,8,128]{2,1,0:T(8,128)S(1)}, f32[21,8,128]{2,1,0:T(8,128)S(1)}, u32[]{:S(2)}, u32[]{:S(2)}) collective-permute-start(f32[21,8,128]{2,1,0:T(8,128)S(1)} %get-tuple-element.43), channel_id=1, source_target_pairs={{0,1},{4,8},{8,4},{12,13},{1,0},{5,9},{9,5},{13,12},{2,3},{6,10},{... | collective-permute-start | bytes 258056 | tf_op jit(solution)/shard_map/ppermute | solution.py:32
  21.6 3.2 %copy-start = (bf16[256,384]{1,0:T(8,128)(2,1)S(1)}, bf16[256,384]{1,0:T(8,128)(2,1)}, u32[]{:S(2)}) copy-start(bf16[256,384]{1,0:T(8,128)(2,1)} %constant.16.clone.p1) | copy-start | bytes 589828
  21.6 3.2 %copy-start.1 = (bf16[128,256]{1,0:T(8,128)(2,1)S(1)}, bf16[128,256]{1,0:T(8,128)(2,1)}, u32[]{:S(2)}) copy-start(bf16[128,256]{1,0:T(8,128)(2,1)} %constant.17.clone.p2) | copy-start | bytes 196612

commit v6 on v5

--- a/solution.py
+++ b/solution.py
@@ -68,7 +68,7 @@
 
 
 def exact_dot(left, right):
-    return sum(jnp.dot(part, right, preferred_element_type=jnp.float32) for part in split(left, 2))
+    return jnp.dot(jnp.concatenate(split(left, 2), 1), jnp.concatenate([right, right], 0), preferred_element_type=jnp.float32)
 
 
 def neighbours(u):

time: 29.6 us -> 29.5 us (level)
  no operation moved by 1% of the time
where the time goes in v6:
time: 29.5 us; the launch traced here: 29.3 us
  Pallas kernels  11.1 us (38%)
  starting transfers between devices  10.9 us (37%)
  waiting for transfers between devices  6.53 us (22%)
  between operations  0.76 us (3%)
    pallas_call x6, Pallas kernels, call(): pl.pallas_call(kernel, out_shape=[f32(s) for s in outs], in_specs=[VM] *...  5.28 us
    ppermute x8, starting transfers between devices, neighbour_swap(): lax.ppermute(x, (spare,) + axis if leading else axis + (spare,), pairs)  4.78 us
    pallas_call x1, Pallas kernels, body(): pl.pallas_call(up_kernel, out_shape=[f32(own), f32(own)], in_specs=[VM] *...  4.61 us
    ppermute x8, waiting for transfers between devices, neighbour_swap(): lax.ppermute(x, (spare,) + axis if leading else axis + (spare,), pairs)  3.17 us
    ppermute x1, starting transfers between devices, body(): near = lax.ppermute(panels, 'tile', [(i, i ^ 1) for i in range(tiles)])  3.09 us
    ppermute x1, starting transfers between devices, body(): panels = jnp.concatenate([panels, lax.ppermute(panels, 'tile', swap)], 0)  3.03 us
    ppermute x1, waiting for transfers between devices, body(): panels = jnp.concatenate([panels, lax.ppermute(panels, 'tile', swap)], 0)  1.85 us
    ppermute x1, waiting for transfers between devices, body(): near = lax.ppermute(panels, 'tile', [(i, i ^ 1) for i in range(tiles)])  1.5 us
  transfers between devices with their start and end apart: 10, of which 4 were waited for; matrix products, arithmetic and copies ran while one was open for 0% of the time, Pallas kernels for 13%

profile of v6, /device:TPU:0, one launch (start us, length us, event | category | flops | bytes accessed | tf_op | source)
XLA Modules:
  0.0 29.3 jit_solution(16948857907897879671)
XLA Ops:
  0.6 1.2 %shard_map.131 = (f32[18,32,256]{2,1,0:T(8,128)S(1)}, f32[1,8,128]{2,1,0:T(8,128)S(1)}, f32[27,8,256]{2,1,0:T(8,128)S(1)}, f32[27,8,256]{2,1,0:T(8,128)S(1)}) custom-call(f32[16,32,256]{2,1,0:T(8,128)} %rs.1, f32[32,256]{1,0:T(8,128)} %kh.1, f32[32,256]{1,0:T(8,128)} %kv.1, s32[4,128]{1,0:T(4,128)} %bitcast.3, s32[4,128]{1,0:T(4,128)} %bitcast.4, ...), custom_call_target="tpu_custom_call" | custom-call | tf_op jit(solution)/shard_map/pallas_call | solution.py:633
  1.8 3.1 %collective-permute-start.2 = (f32[1,8,128]{2,1,0:T(8,128)S(1)}, f32[1,8,128]{2,1,0:T(8,128)S(1)}, u32[]{:S(2)}, u32[]{:S(2)}) collective-permute-start(f32[1,8,128]{2,1,0:T(8,128)S(1)} %get-tuple-element.34), channel_id=1, source_target_pairs={{0,4},{4,0},{8,12},{12,8},{1,5},{5,1},{9,13},{13,9},{2,6},{6,2},{1... | collective-permute-start | bytes 12296 | tf_op jit(solution)/shard_map/ppermute | solution.py:649
  4.9 0.1 collective-permute-start
  5.0 0.0 collective-permute-start.1
  5.0 1.5 %collective-permute-done.2 = f32[1,8,128]{2,1,0:T(8,128)S(1)} collective-permute-done((f32[1,8,128]{2,1,0:T(8,128)S(1)}, f32[1,8,128]{2,1,0:T(8,128)S(1)}, u32[]{:S(2)}, u32[]{:S(2)}) %collective-permute-start.2) | collective-permute-done | bytes 4128 | tf_op jit(solution)/shard_map/ppermute | solution.py:649
  6.5 3.0 %collective-permute-start.3 = (f32[2,8,128]{2,1,0:T(8,128)S(1)}, f32[2,8,128]{2,1,0:T(8,128)S(1)}, u32[]{:S(2)}, u32[]{:S(2)}) collective-permute-start(f32[2,8,128]{2,1,0:T(8,128)S(1)} %pad_maximum_fusion.1), channel_id=1, source_target_pairs={{0,8},{4,12},{8,0},{12,4},{1,9},{5,13},{9,1},{13,5},{2,10},{6,14},... | collective-permute-start | bytes 24584 | tf_op jit(solution)/shard_map/ppermute | solution.py:659
  9.5 0.2 shard_map.133
  9.7 0.1 collective-permute-start.4
  9.8 1.6 %collective-permute-start.5 = (f32[6,32,128]{2,1,0:T(8,128)S(1)}, f32[6,32,128]{2,1,0:T(8,128)S(1)}, u32[]{:S(2)}, u32[]{:S(2)}) collective-permute-start(f32[6,32,128]{2,1,0:T(8,128)S(1)} %get-tuple-element.37), channel_id=1, source_target_pairs={{0,16},{1,2},{2,1},{3,19},{16,0},{17,18},{18,17},{19,3},{4,20},{5,... | collective-permute-start | bytes 294920 | tf_op jit(solution)/shard_map/ppermute | solution.py:32
  11.4 1.9 %collective-permute-done.3 = f32[2,8,128]{2,1,0:T(8,128)S(1)} collective-permute-done((f32[2,8,128]{2,1,0:T(8,128)S(1)}, f32[2,8,128]{2,1,0:T(8,128)S(1)}, u32[]{:S(2)}, u32[]{:S(2)}) %collective-permute-start.3) | collective-permute-done | bytes 8224 | tf_op jit(solution)/shard_map/ppermute | solution.py:659
  13.3 0.0 copy-start.2
  13.3 0.0 copy-start.5
  13.3 0.0 collective-permute-done.xa
  13.3 0.0 collective-permute-done.1.xb
  13.3 0.8 %shard_map.132 = (f32[18,56,256]{2,1,0:T(8,128)S(1)}, f32[7,24,128]{2,1,0:T(8,128)S(1)}, f32[7,24,128]{2,1,0:T(8,128)S(1)}) custom-call(f32[18,32,256]{2,1,0:T(8,128)S(1)} %get-tuple-element.31.x_own.x, f32[27,8,256]{2,1,0:T(8,128)S(1)} %collective-permute-done.xa, f32[27,8,256]{2,1,0:T(8,128)S(1)} %collective-permute-done.1.xb, ...), custom_call_target="tpu_custom_call" | custom-call | tf_op jit(solution)/shard_map/pallas_call | solution.py:605
  14.0 0.1 collective-permute-start.6
  14.1 1.6 %collective-permute-start.7 = (f32[7,24,128]{2,1,0:T(8,128)S(1)}, f32[7,24,128]{2,1,0:T(8,128)S(1)}, u32[]{:S(2)}, u32[]{:S(2)}) collective-permute-start(f32[7,24,128]{2,1,0:T(8,128)S(1)} %get-tuple-element.39), channel_id=1, source_target_pairs={{0,16},{1,2},{2,1},{3,19},{16,0},{17,18},{18,17},{19,3},{4,20},{5,... | collective-permute-start | bytes 258056 | tf_op jit(solution)/shard_map/ppermute | solution.py:32
  15.7 0.0 copy-done.2
  15.7 0.0 copy-done.5
  15.7 2.0 %shard_map.135 = (f32[16,40,256]{2,1,0:T(8,128)S(1)}, f32[18,32,128]{2,1,0:T(8,128)S(1)}, f32[16,32,128]{2,1,0:T(8,128)S(1)}, f32[18,16,128]{2,1,0:T(8,128)S(1)}) custom-call(f32[18,56,256]{2,1,0:T(8,128)S(1)} %get-tuple-element.35.ext, bf16[256,128]{1,0:T(8,128)(2,1)S(1)} %copy-done.2, bf16[128,128]{1,0:T(8,128)(2,1)S(1)} %copy-done.5), custom_call_target="tpu_custom_call" | custom-call | tf_op jit(solution)/shard_map/pallas_call | solution.py:605
  17.7 0.0 copy-start.3
  17.7 0.0 copy-start.4
  17.8 0.0 collective-permute-done.4.ysub
  17.8 0.0 collective-permute-done.5.ystrip
  17.8 0.3 %shard_map.134.base = f32[18,56,128]{2,1,0:T(8,128)S(1)} custom-call(f32[18,56,256]{2,1,0:T(8,128)S(1)} %get-tuple-element.35.ext, f32[6,32,128]{2,1,0:T(8,128)S(1)} %collective-permute-done.4.ysub, f32[6,32,128]{2,1,0:T(8,128)S(1)} %collective-permute-done.5.ystrip), custom_call_target="tpu_custom_call" | custom-call | tf_op jit(solution)/shard_map/pallas_call | solution.py:605
  18.1 0.0 collective-permute-done.6.ysub
  18.1 0.6 %collective-permute-done.7.ystrip = f32[7,24,128]{2,1,0:T(8,128)S(1)} collective-permute-done((f32[7,24,128]{2,1,0:T(8,128)S(1)}, f32[7,24,128]{2,1,0:T(8,128)S(1)}, u32[]{:S(2)}, u32[]{:S(2)}) %collective-permute-start.7) | collective-permute-done | bytes 86048 | tf_op jit(solution)/shard_map/ppermute | solution.py:32
  18.7 0.0 copy-done.3
  18.7 0.0 copy-done.4
  18.7 1.4 %shard_map.136 = (f32[18,56,128]{2,1,0:T(8,128)S(1)}, f32[16,40,128]{2,1,0:T(8,128)S(1)}, f32[18,32,128]{2,1,0:T(8,128)S(1)}, f32[16,32,128]{2,1,0:T(8,128)S(1)}...) custom-call(f32[18,56,128]{2,1,0:T(8,128)S(1)} %shard_map.134.base, ...), custom_call_target="tpu_custom_call", output_to_operand_aliasing={{0}: (0, {})} | custom-call | tf_op jit(solution)/shard_map/pallas_call | solution.py:605
  20.1 1.4 %collective-permute-start.8 = (f32[21,8,128]{2,1,0:T(8,128)S(1)}, f32[21,8,128]{2,1,0:T(8,128)S(1)}, u32[]{:S(2)}, u32[]{:S(2)}) collective-permute-start(f32[21,8,128]{2,1,0:T(8,128)S(1)} %get-tuple-element.42), channel_id=1, source_target_pairs={{0,4},{4,0},{8,12},{12,8},{1,5},{5,1},{9,13},{13,9},{2,6},{6,2},{1... | collective-permute-start | bytes 258056 | tf_op jit(solution)/shard_map/ppermute | solution.py:32
  21.5 0.0 collective-permute-start.9
  21.5 0.0 copy-start
  21.5 0.0 copy-start.1
  21.5 0.6 %shard_map.137 = (f32[2,40,384]{2,1,0:T(8,128)S(1)}, f32[16,40,384]{2,1,0:T(8,128)S(1)}, f32[16,40,384]{2,1,0:T(8,128)S(1)}, f32[2,40,384]{2,1,0:T(8,128)S(1)}, ...) custom-call(f32[18,56,256]{2,1,0:T(8,128)S(1)} %get-tuple-element.35, ...), custom_call_target="tpu_custom_call" | custom-call | tf_op jit(solution)/shard_map/pallas_call | solution.py:605
  22.1 2.6 %collective-permute-done.8.xa = f32[21,8,128]{2,1,0:T(8,128)S(1)} collective-permute-done((f32[21,8,128]{2,1,0:T(8,128)S(1)}, f32[21,8,128]{2,1,0:T(8,128)S(1)}, u32[]{:S(2)}, u32[]{:S(2)}) %collective-permute-start.8) | collective-permute-done | bytes 86048 | tf_op jit(solution)/shard_map/ppermute | solution.py:32
  24.7 0.0 collective-permute-done.9.xb
  24.7 0.0 copy-done
  24.7 0.0 copy-done.1
  24.7 4.6 %shard_map.138 = (f32[16,32,256]{2,1,0:T(8,128)}, f32[16,32,256]{2,1,0:T(8,128)}) custom-call(f32[18,16,128]{2,1,0:T(8,128)S(1)} %get-tuple-element.41.c_in, f32[21,8,128]{2,1,0:T(8,128)S(1)} %collective-permute-done.8.xa, f32[21,8,128]{2,1,0:T(8,128)S(1)} %collective-permute-done.9.xb, f32[18,56,256]{2,1,0:T(8,128)S(1)} %get-tuple-element.35.ext, ...), custom_call_target="tpu_custom_call" | custom-call | tf_op jit(solution)/shard_map/pallas_call | solution.py:714
  (2 shorter events, 0.0 us)
Async XLA Ops:
  1.8 4.7 %collective-permute-start.2 = (f32[1,8,128]{2,1,0:T(8,128)S(1)}, f32[1,8,128]{2,1,0:T(8,128)S(1)}, u32[]{:S(2)}, u32[]{:S(2)}) collective-permute-start(f32[1,8,128]{2,1,0:T(8,128)S(1)} %get-tuple-element.34), channel_id=1, source_target_pairs={{0,4},{4,0},{8,12},{12,8},{1,5},{5,1},{9,13},{13,9},{2,6},{6,2},{1... | collective-permute-start | bytes 12296 | tf_op jit(solution)/shard_map/ppermute | solution.py:649
  4.9 8.3 %collective-permute-start = (f32[27,8,256]{2,1,0:T(8,128)S(1)}, f32[27,8,256]{2,1,0:T(8,128)S(1)}, u32[]{:S(2)}, u32[]{:S(2)}) collective-permute-start(f32[27,8,256]{2,1,0:T(8,128)S(1)} %get-tuple-element.32), channel_id=1, source_target_pairs={{0,4},{4,0},{8,12},{12,8},{1,5},{5,1},{9,13},{13,9},{2,6},{6,2},{1... | collective-permute-start | bytes 663560 | tf_op jit(solution)/shard_map/ppermute | solution.py:32
  5.0 8.3 %collective-permute-start.1 = (f32[27,8,256]{2,1,0:T(8,128)S(1)}, f32[27,8,256]{2,1,0:T(8,128)S(1)}, u32[]{:S(2)}, u32[]{:S(2)}) collective-permute-start(f32[27,8,256]{2,1,0:T(8,128)S(1)} %get-tuple-element.33), channel_id=1, source_target_pairs={{0,1},{4,8},{8,4},{12,13},{1,0},{5,9},{9,5},{13,12},{2,3},{6,10},{... | collective-permute-start | bytes 663560 | tf_op jit(solution)/shard_map/ppermute | solution.py:32
  6.5 6.7 %collective-permute-start.3 = (f32[2,8,128]{2,1,0:T(8,128)S(1)}, f32[2,8,128]{2,1,0:T(8,128)S(1)}, u32[]{:S(2)}, u32[]{:S(2)}) collective-permute-start(f32[2,8,128]{2,1,0:T(8,128)S(1)} %pad_maximum_fusion.1), channel_id=1, source_target_pairs={{0,8},{4,12},{8,0},{12,4},{1,9},{5,13},{9,1},{13,5},{2,10},{6,14},... | collective-permute-start | bytes 24584 | tf_op jit(solution)/shard_map/ppermute | solution.py:659
  9.7 8.0 %collective-permute-start.4 = (f32[6,32,128]{2,1,0:T(8,128)S(1)}, f32[6,32,128]{2,1,0:T(8,128)S(1)}, u32[]{:S(2)}, u32[]{:S(2)}) collective-permute-start(f32[6,32,128]{2,1,0:T(8,128)S(1)} %get-tuple-element.36), channel_id=1, source_target_pairs={{0,1},{1,0},{2,3},{3,2},{16,17},{17,16},{18,19},{19,18},{4,5},{5,4... | collective-permute-start | bytes 294920 | tf_op jit(solution)/shard_map/ppermute | solution.py:32
  9.8 8.0 %collective-permute-start.5 = (f32[6,32,128]{2,1,0:T(8,128)S(1)}, f32[6,32,128]{2,1,0:T(8,128)S(1)}, u32[]{:S(2)}, u32[]{:S(2)}) collective-permute-start(f32[6,32,128]{2,1,0:T(8,128)S(1)} %get-tuple-element.37), channel_id=1, source_target_pairs={{0,16},{1,2},{2,1},{3,19},{16,0},{17,18},{18,17},{19,3},{4,20},{5,... | collective-permute-start | bytes 294920 | tf_op jit(solution)/shard_map/ppermute | solution.py:32
  13.3 2.5 %copy-start.2 = (bf16[256,128]{1,0:T(8,128)(2,1)S(1)}, bf16[256,128]{1,0:T(8,128)(2,1)}, u32[]{:S(2)}) copy-start(bf16[256,128]{1,0:T(8,128)(2,1)} %constant.12.clone.c1) | copy-start | bytes 196612
  13.3 2.5 %copy-start.5 = (bf16[128,128]{1,0:T(8,128)(2,1)S(1)}, bf16[128,128]{1,0:T(8,128)(2,1)}, u32[]{:S(2)}) copy-start(bf16[128,128]{1,0:T(8,128)(2,1)} %constant.13.clone.c2) | copy-start | bytes 98308
  14.0 4.0 %collective-permute-start.6 = (f32[7,24,128]{2,1,0:T(8,128)S(1)}, f32[7,24,128]{2,1,0:T(8,128)S(1)}, u32[]{:S(2)}, u32[]{:S(2)}) collective-permute-start(f32[7,24,128]{2,1,0:T(8,128)S(1)} %get-tuple-element.38), channel_id=1, source_target_pairs={{0,1},{1,0},{2,3},{3,2},{16,17},{17,16},{18,19},{19,18},{4,5},{5,4... | collective-permute-start | bytes 258056 | tf_op jit(solution)/shard_map/ppermute | solution.py:32
  14.1 4.6 %collective-permute-start.7 = (f32[7,24,128]{2,1,0:T(8,128)S(1)}, f32[7,24,128]{2,1,0:T(8,128)S(1)}, u32[]{:S(2)}, u32[]{:S(2)}) collective-permute-start(f32[7,24,128]{2,1,0:T(8,128)S(1)} %get-tuple-element.39), channel_id=1, source_target_pairs={{0,16},{1,2},{2,1},{3,19},{16,0},{17,18},{18,17},{19,3},{4,20},{5,... | collective-permute-start | bytes 258056 | tf_op jit(solution)/shard_map/ppermute | solution.py:32
  17.7 0.9 %copy-start.3 = (bf16[128,128]{1,0:T(8,128)(2,1)S(1)}, bf16[128,128]{1,0:T(8,128)(2,1)}, u32[]{:S(2)}) copy-start(bf16[128,128]{1,0:T(8,128)(2,1)} %constant.15.clone.c2) | copy-start | bytes 98308
  17.7 0.9 %copy-start.4 = (bf16[128,128]{1,0:T(8,128)(2,1)S(1)}, bf16[128,128]{1,0:T(8,128)(2,1)}, u32[]{:S(2)}) copy-start(bf16[128,128]{1,0:T(8,128)(2,1)} %constant.14.clone.c1) | copy-start | bytes 98308
  20.1 4.6 %collective-permute-start.8 = (f32[21,8,128]{2,1,0:T(8,128)S(1)}, f32[21,8,128]{2,1,0:T(8,128)S(1)}, u32[]{:S(2)}, u32[]{:S(2)}) collective-permute-start(f32[21,8,128]{2,1,0:T(8,128)S(1)} %get-tuple-element.42), channel_id=1, source_target_pairs={{0,4},{4,0},{8,12},{12,8},{1,5},{5,1},{9,13},{13,9},{2,6},{6,2},{1... | collective-permute-start | bytes 258056 | tf_op jit(solution)/shard_map/ppermute | solution.py:32
  21.5 3.2 %collective-permute-start.9 = (f32[21,8,128]{2,1,0:T(8,128)S(1)}, f32[21,8,128]{2,1,0:T(8,128)S(1)}, u32[]{:S(2)}, u32[]{:S(2)}) collective-permute-start(f32[21,8,128]{2,1,0:T(8,128)S(1)} %get-tuple-element.43), channel_id=1, source_target_pairs={{0,1},{4,8},{8,4},{12,13},{1,0},{5,9},{9,5},{13,12},{2,3},{6,10},{... | collective-permute-start | bytes 258056 | tf_op jit(solution)/shard_map/ppermute | solution.py:32
  21.5 3.2 %copy-start = (bf16[256,384]{1,0:T(8,128)(2,1)S(1)}, bf16[256,384]{1,0:T(8,128)(2,1)}, u32[]{:S(2)}) copy-start(bf16[256,384]{1,0:T(8,128)(2,1)} %constant.16.clone.p1) | copy-start | bytes 589828
  21.5 3.2 %copy-start.1 = (bf16[128,256]{1,0:T(8,128)(2,1)S(1)}, bf16[128,256]{1,0:T(8,128)(2,1)}, u32[]{:S(2)}) copy-start(bf16[128,256]{1,0:T(8,128)(2,1)} %constant.17.clone.p2) | copy-start | bytes 196612

commit v7 on v6

--- a/solution.py
+++ b/solution.py
@@ -564,12 +564,13 @@
     span0, lanes0 = u0.shape[1], u0.shape[2]
     above = (span0 - rows) // 2
     off1 = (HX - above) // 2
-    fine = exact_dot(f1[pl.ds(1, depth)].reshape(depth * span1, lanes1), p1[...])
+    end1 = off1 + span0 // 2
+    fine = exact_dot(jnp.concatenate([f1[z + 1, 0:end1, :] for z in range(depth)], 0), p1[...])
     for z in range(depth):
-        rows_doubled(e0, z, fine[z * span1 + off1 : z * span1 + off1 + span0 // 2])
+        rows_doubled(e0, z, fine[z * end1 + off1 : (z + 1) * end1])
 
     def first0(z, c):
-        f0[z + 1] = u0[z] + blocks_in(e0, z)
+        f0[z + 1] = u0[z] + blocks_in(e0, z)[:span0]
         return c
 
     loop(depth, first0, 15)
@@ -722,7 +723,7 @@
                 (count, wide2, half), (2, wide2, half), (2, wide2, half), (2, wide2, half), (depth, wide2, half),
                 field2, field2, (depth + 2, span1, cols), (depth + 2, span1, cols),
                 (depth + 2, small, lanes), (depth + 2, small, lanes),
-                (depth, cols // 128, span1, 128), (depth, lanes // 128, small, 128), own, own,
+                (depth, cols // 128, span1, 128), (depth, lanes // 128, small + 8, 128), own, own,
             )
         ]
         + [pltpu.SemaphoreType.DMA((5,))],

time: 29.5 us -> 29.4 us (level)
  no operation moved by 1% of the time
where the time goes in v7:
time: 29.4 us; the launch traced here: 29.2 us
  Pallas kernels  11 us (37%)
  starting transfers between devices  10.9 us (37%)
  waiting for transfers between devices  6.53 us (22%)
  between operations  0.76 us (3%)
    pallas_call x6, Pallas kernels, call(): pl.pallas_call(kernel, out_shape=[f32(s) for s in outs], in_specs=[VM] *...  5.28 us
    ppermute x8, starting transfers between devices, neighbour_swap(): lax.ppermute(x, (spare,) + axis if leading else axis + (spare,), pairs)  4.78 us
    pallas_call x1, Pallas kernels, body(): pl.pallas_call(up_kernel, out_shape=[f32(own), f32(own)], in_specs=[VM] *...  4.53 us
    ppermute x8, waiting for transfers between devices, neighbour_swap(): lax.ppermute(x, (spare,) + axis if leading else axis + (spare,), pairs)  3.17 us
    ppermute x1, starting transfers between devices, body(): near = lax.ppermute(panels, 'tile', [(i, i ^ 1) for i in range(tiles)])  3.09 us
    ppermute x1, starting transfers between devices, body(): panels = jnp.concatenate([panels, lax.ppermute(panels, 'tile', swap)], 0)  3.03 us
    ppermute x1, waiting for transfers between devices, body(): panels = jnp.concatenate([panels, lax.ppermute(panels, 'tile', swap)], 0)  1.85 us
    ppermute x1, waiting for transfers between devices, body(): near = lax.ppermute(panels, 'tile', [(i, i ^ 1) for i in range(tiles)])  1.5 us
  transfers between devices with their start and end apart: 10, of which 4 were waited for; matrix products, arithmetic and copies ran while one was open for 0% of the time, Pallas kernels for 13%

profile of v7, /device:TPU:0, one launch (start us, length us, event | category | flops | bytes accessed | tf_op | source)
XLA Modules:
  0.0 29.2 jit_solution(17091262684990842192)
XLA Ops:
  0.6 1.2 %shard_map.131 = (f32[18,32,256]{2,1,0:T(8,128)S(1)}, f32[1,8,128]{2,1,0:T(8,128)S(1)}, f32[27,8,256]{2,1,0:T(8,128)S(1)}, f32[27,8,256]{2,1,0:T(8,128)S(1)}) custom-call(f32[16,32,256]{2,1,0:T(8,128)} %rs.1, f32[32,256]{1,0:T(8,128)} %kh.1, f32[32,256]{1,0:T(8,128)} %kv.1, s32[4,128]{1,0:T(4,128)} %bitcast.3, s32[4,128]{1,0:T(4,128)} %bitcast.4, ...), custom_call_target="tpu_custom_call" | custom-call | tf_op jit(solution)/shard_map/pallas_call | solution.py:634
  1.8 3.1 %collective-permute-start.2 = (f32[1,8,128]{2,1,0:T(8,128)S(1)}, f32[1,8,128]{2,1,0:T(8,128)S(1)}, u32[]{:S(2)}, u32[]{:S(2)}) collective-permute-start(f32[1,8,128]{2,1,0:T(8,128)S(1)} %get-tuple-element.34), channel_id=1, source_target_pairs={{0,4},{4,0},{8,12},{12,8},{1,5},{5,1},{9,13},{13,9},{2,6},{6,2},{1... | collective-permute-start | bytes 12296 | tf_op jit(solution)/shard_map/ppermute | solution.py:650
  4.9 0.1 collective-permute-start
  5.0 0.0 collective-permute-start.1
  5.0 1.5 %collective-permute-done.2 = f32[1,8,128]{2,1,0:T(8,128)S(1)} collective-permute-done((f32[1,8,128]{2,1,0:T(8,128)S(1)}, f32[1,8,128]{2,1,0:T(8,128)S(1)}, u32[]{:S(2)}, u32[]{:S(2)}) %collective-permute-start.2) | collective-permute-done | bytes 4128 | tf_op jit(solution)/shard_map/ppermute | solution.py:650
  6.5 3.0 %collective-permute-start.3 = (f32[2,8,128]{2,1,0:T(8,128)S(1)}, f32[2,8,128]{2,1,0:T(8,128)S(1)}, u32[]{:S(2)}, u32[]{:S(2)}) collective-permute-start(f32[2,8,128]{2,1,0:T(8,128)S(1)} %pad_maximum_fusion.1), channel_id=1, source_target_pairs={{0,8},{4,12},{8,0},{12,4},{1,9},{5,13},{9,1},{13,5},{2,10},{6,14},... | collective-permute-start | bytes 24584 | tf_op jit(solution)/shard_map/ppermute | solution.py:660
  9.5 0.2 shard_map.133
  9.7 0.1 collective-permute-start.4
  9.8 1.6 %collective-permute-start.5 = (f32[6,32,128]{2,1,0:T(8,128)S(1)}, f32[6,32,128]{2,1,0:T(8,128)S(1)}, u32[]{:S(2)}, u32[]{:S(2)}) collective-permute-start(f32[6,32,128]{2,1,0:T(8,128)S(1)} %get-tuple-element.37), channel_id=1, source_target_pairs={{0,16},{1,2},{2,1},{3,19},{16,0},{17,18},{18,17},{19,3},{4,20},{5,... | collective-permute-start | bytes 294920 | tf_op jit(solution)/shard_map/ppermute | solution.py:32
  11.4 1.9 %collective-permute-done.3 = f32[2,8,128]{2,1,0:T(8,128)S(1)} collective-permute-done((f32[2,8,128]{2,1,0:T(8,128)S(1)}, f32[2,8,128]{2,1,0:T(8,128)S(1)}, u32[]{:S(2)}, u32[]{:S(2)}) %collective-permute-start.3) | collective-permute-done | bytes 8224 | tf_op jit(solution)/shard_map/ppermute | solution.py:660
  13.3 0.0 copy-start.2
  13.3 0.0 copy-start.5
  13.3 0.0 collective-permute-done.xa
  13.3 0.0 collective-permute-done.1.xb
  13.3 0.8 %shard_map.132 = (f32[18,56,256]{2,1,0:T(8,128)S(1)}, f32[7,24,128]{2,1,0:T(8,128)S(1)}, f32[7,24,128]{2,1,0:T(8,128)S(1)}) custom-call(f32[18,32,256]{2,1,0:T(8,128)S(1)} %get-tuple-element.31.x_own.x, f32[27,8,256]{2,1,0:T(8,128)S(1)} %collective-permute-done.xa, f32[27,8,256]{2,1,0:T(8,128)S(1)} %collective-permute-done.1.xb, ...), custom_call_target="tpu_custom_call" | custom-call | tf_op jit(solution)/shard_map/pallas_call | solution.py:606
  14.0 0.1 collective-permute-start.6
  14.1 1.6 %collective-permute-start.7 = (f32[7,24,128]{2,1,0:T(8,128)S(1)}, f32[7,24,128]{2,1,0:T(8,128)S(1)}, u32[]{:S(2)}, u32[]{:S(2)}) collective-permute-start(f32[7,24,128]{2,1,0:T(8,128)S(1)} %get-tuple-element.39), channel_id=1, source_target_pairs={{0,16},{1,2},{2,1},{3,19},{16,0},{17,18},{18,17},{19,3},{4,20},{5,... | collective-permute-start | bytes 258056 | tf_op jit(solution)/shard_map/ppermute | solution.py:32
  15.7 0.0 copy-done.2
  15.7 0.0 copy-done.5
  15.7 2.0 %shard_map.135 = (f32[16,40,256]{2,1,0:T(8,128)S(1)}, f32[18,32,128]{2,1,0:T(8,128)S(1)}, f32[16,32,128]{2,1,0:T(8,128)S(1)}, f32[18,16,128]{2,1,0:T(8,128)S(1)}) custom-call(f32[18,56,256]{2,1,0:T(8,128)S(1)} %get-tuple-element.35.ext, bf16[256,128]{1,0:T(8,128)(2,1)S(1)} %copy-done.2, bf16[128,128]{1,0:T(8,128)(2,1)S(1)} %copy-done.5), custom_call_target="tpu_custom_call" | custom-call | tf_op jit(solution)/shard_map/pallas_call | solution.py:606
  17.7 0.0 copy-start.3
  17.7 0.0 copy-start.4
  17.8 0.0 collective-permute-done.4.ysub
  17.8 0.0 collective-permute-done.5.ystrip
  17.8 0.3 %shard_map.134.base = f32[18,56,128]{2,1,0:T(8,128)S(1)} custom-call(f32[18,56,256]{2,1,0:T(8,128)S(1)} %get-tuple-element.35.ext, f32[6,32,128]{2,1,0:T(8,128)S(1)} %collective-permute-done.4.ysub, f32[6,32,128]{2,1,0:T(8,128)S(1)} %collective-permute-done.5.ystrip), custom_call_target="tpu_custom_call" | custom-call | tf_op jit(solution)/shard_map/pallas_call | solution.py:606
  18.1 0.0 collective-permute-done.6.ysub
  18.1 0.6 %collective-permute-done.7.ystrip = f32[7,24,128]{2,1,0:T(8,128)S(1)} collective-permute-done((f32[7,24,128]{2,1,0:T(8,128)S(1)}, f32[7,24,128]{2,1,0:T(8,128)S(1)}, u32[]{:S(2)}, u32[]{:S(2)}) %collective-permute-start.7) | collective-permute-done | bytes 86048 | tf_op jit(solution)/shard_map/ppermute | solution.py:32
  18.7 0.0 copy-done.3
  18.7 0.0 copy-done.4
  18.7 1.4 %shard_map.136 = (f32[18,56,128]{2,1,0:T(8,128)S(1)}, f32[16,40,128]{2,1,0:T(8,128)S(1)}, f32[18,32,128]{2,1,0:T(8,128)S(1)}, f32[16,32,128]{2,1,0:T(8,128)S(1)}...) custom-call(f32[18,56,128]{2,1,0:T(8,128)S(1)} %shard_map.134.base, ...), custom_call_target="tpu_custom_call", output_to_operand_aliasing={{0}: (0, {})} | custom-call | tf_op jit(solution)/shard_map/pallas_call | solution.py:606
  20.1 1.4 %collective-permute-start.8 = (f32[21,8,128]{2,1,0:T(8,128)S(1)}, f32[21,8,128]{2,1,0:T(8,128)S(1)}, u32[]{:S(2)}, u32[]{:S(2)}) collective-permute-start(f32[21,8,128]{2,1,0:T(8,128)S(1)} %get-tuple-element.42), channel_id=1, source_target_pairs={{0,4},{4,0},{8,12},{12,8},{1,5},{5,1},{9,13},{13,9},{2,6},{6,2},{1... | collective-permute-start | bytes 258056 | tf_op jit(solution)/shard_map/ppermute | solution.py:32
  21.5 0.0 collective-permute-start.9
  21.5 0.0 copy-start
  21.5 0.0 copy-start.1
  21.5 0.6 %shard_map.137 = (f32[2,40,384]{2,1,0:T(8,128)S(1)}, f32[16,40,384]{2,1,0:T(8,128)S(1)}, f32[16,40,384]{2,1,0:T(8,128)S(1)}, f32[2,40,384]{2,1,0:T(8,128)S(1)}, ...) custom-call(f32[18,56,256]{2,1,0:T(8,128)S(1)} %get-tuple-element.35, ...), custom_call_target="tpu_custom_call" | custom-call | tf_op jit(solution)/shard_map/pallas_call | solution.py:606
  22.1 2.6 %collective-permute-done.8.xa = f32[21,8,128]{2,1,0:T(8,128)S(1)} collective-permute-done((f32[21,8,128]{2,1,0:T(8,128)S(1)}, f32[21,8,128]{2,1,0:T(8,128)S(1)}, u32[]{:S(2)}, u32[]{:S(2)}) %collective-permute-start.8) | collective-permute-done | bytes 86048 | tf_op jit(solution)/shard_map/ppermute | solution.py:32
  24.7 0.0 collective-permute-done.9.xb
  24.7 0.0 copy-done
  24.7 0.0 copy-done.1
  24.7 4.5 %shard_map.138 = (f32[16,32,256]{2,1,0:T(8,128)}, f32[16,32,256]{2,1,0:T(8,128)}) custom-call(f32[18,16,128]{2,1,0:T(8,128)S(1)} %get-tuple-element.41.c_in, f32[21,8,128]{2,1,0:T(8,128)S(1)} %collective-permute-done.8.xa, f32[21,8,128]{2,1,0:T(8,128)S(1)} %collective-permute-done.9.xb, f32[18,56,256]{2,1,0:T(8,128)S(1)} %get-tuple-element.35.ext, ...), custom_call_target="tpu_custom_call" | custom-call | tf_op jit(solution)/shard_map/pallas_call | solution.py:715
  (2 shorter events, 0.0 us)
Async XLA Ops:
  1.8 4.7 %collective-permute-start.2 = (f32[1,8,128]{2,1,0:T(8,128)S(1)}, f32[1,8,128]{2,1,0:T(8,128)S(1)}, u32[]{:S(2)}, u32[]{:S(2)}) collective-permute-start(f32[1,8,128]{2,1,0:T(8,128)S(1)} %get-tuple-element.34), channel_id=1, source_target_pairs={{0,4},{4,0},{8,12},{12,8},{1,5},{5,1},{9,13},{13,9},{2,6},{6,2},{1... | collective-permute-start | bytes 12296 | tf_op jit(solution)/shard_map/ppermute | solution.py:650
  4.9 8.3 %collective-permute-start = (f32[27,8,256]{2,1,0:T(8,128)S(1)}, f32[27,8,256]{2,1,0:T(8,128)S(1)}, u32[]{:S(2)}, u32[]{:S(2)}) collective-permute-start(f32[27,8,256]{2,1,0:T(8,128)S(1)} %get-tuple-element.32), channel_id=1, source_target_pairs={{0,4},{4,0},{8,12},{12,8},{1,5},{5,1},{9,13},{13,9},{2,6},{6,2},{1... | collective-permute-start | bytes 663560 | tf_op jit(solution)/shard_map/ppermute | solution.py:32
  5.0 8.3 %collective-permute-start.1 = (f32[27,8,256]{2,1,0:T(8,128)S(1)}, f32[27,8,256]{2,1,0:T(8,128)S(1)}, u32[]{:S(2)}, u32[]{:S(2)}) collective-permute-start(f32[27,8,256]{2,1,0:T(8,128)S(1)} %get-tuple-element.33), channel_id=1, source_target_pairs={{0,1},{4,8},{8,4},{12,13},{1,0},{5,9},{9,5},{13,12},{2,3},{6,10},{... | collective-permute-start | bytes 663560 | tf_op jit(solution)/shard_map/ppermute | solution.py:32
  6.5 6.7 %collective-permute-start.3 = (f32[2,8,128]{2,1,0:T(8,128)S(1)}, f32[2,8,128]{2,1,0:T(8,128)S(1)}, u32[]{:S(2)}, u32[]{:S(2)}) collective-permute-start(f32[2,8,128]{2,1,0:T(8,128)S(1)} %pad_maximum_fusion.1), channel_id=1, source_target_pairs={{0,8},{4,12},{8,0},{12,4},{1,9},{5,13},{9,1},{13,5},{2,10},{6,14},... | collective-permute-start | bytes 24584 | tf_op jit(solution)/shard_map/ppermute | solution.py:660
  9.7 8.0 %collective-permute-start.4 = (f32[6,32,128]{2,1,0:T(8,128)S(1)}, f32[6,32,128]{2,1,0:T(8,128)S(1)}, u32[]{:S(2)}, u32[]{:S(2)}) collective-permute-start(f32[6,32,128]{2,1,0:T(8,128)S(1)} %get-tuple-element.36), channel_id=1, source_target_pairs={{0,1},{1,0},{2,3},{3,2},{16,17},{17,16},{18,19},{19,18},{4,5},{5,4... | collective-permute-start | bytes 294920 | tf_op jit(solution)/shard_map/ppermute | solution.py:32
  9.8 8.0 %collective-permute-start.5 = (f32[6,32,128]{2,1,0:T(8,128)S(1)}, f32[6,32,128]{2,1,0:T(8,128)S(1)}, u32[]{:S(2)}, u32[]{:S(2)}) collective-permute-start(f32[6,32,128]{2,1,0:T(8,128)S(1)} %get-tuple-element.37), channel_id=1, source_target_pairs={{0,16},{1,2},{2,1},{3,19},{16,0},{17,18},{18,17},{19,3},{4,20},{5,... | collective-permute-start | bytes 294920 | tf_op jit(solution)/shard_map/ppermute | solution.py:32
  13.3 2.5 %copy-start.2 = (bf16[256,128]{1,0:T(8,128)(2,1)S(1)}, bf16[256,128]{1,0:T(8,128)(2,1)}, u32[]{:S(2)}) copy-start(bf16[256,128]{1,0:T(8,128)(2,1)} %constant.12.clone.c1) | copy-start | bytes 196612
  13.3 2.5 %copy-start.5 = (bf16[128,128]{1,0:T(8,128)(2,1)S(1)}, bf16[128,128]{1,0:T(8,128)(2,1)}, u32[]{:S(2)}) copy-start(bf16[128,128]{1,0:T(8,128)(2,1)} %constant.13.clone.c2) | copy-start | bytes 98308
  14.0 4.0 %collective-permute-start.6 = (f32[7,24,128]{2,1,0:T(8,128)S(1)}, f32[7,24,128]{2,1,0:T(8,128)S(1)}, u32[]{:S(2)}, u32[]{:S(2)}) collective-permute-start(f32[7,24,128]{2,1,0:T(8,128)S(1)} %get-tuple-element.38), channel_id=1, source_target_pairs={{0,1},{1,0},{2,3},{3,2},{16,17},{17,16},{18,19},{19,18},{4,5},{5,4... | collective-permute-start | bytes 258056 | tf_op jit(solution)/shard_map/ppermute | solution.py:32
  14.1 4.6 %collective-permute-start.7 = (f32[7,24,128]{2,1,0:T(8,128)S(1)}, f32[7,24,128]{2,1,0:T(8,128)S(1)}, u32[]{:S(2)}, u32[]{:S(2)}) collective-permute-start(f32[7,24,128]{2,1,0:T(8,128)S(1)} %get-tuple-element.39), channel_id=1, source_target_pairs={{0,16},{1,2},{2,1},{3,19},{16,0},{17,18},{18,17},{19,3},{4,20},{5,... | collective-permute-start | bytes 258056 | tf_op jit(solution)/shard_map/ppermute | solution.py:32
  17.7 0.9 %copy-start.3 = (bf16[128,128]{1,0:T(8,128)(2,1)S(1)}, bf16[128,128]{1,0:T(8,128)(2,1)}, u32[]{:S(2)}) copy-start(bf16[128,128]{1,0:T(8,128)(2,1)} %constant.15.clone.c2) | copy-start | bytes 98308
  17.7 0.9 %copy-start.4 = (bf16[128,128]{1,0:T(8,128)(2,1)S(1)}, bf16[128,128]{1,0:T(8,128)(2,1)}, u32[]{:S(2)}) copy-start(bf16[128,128]{1,0:T(8,128)(2,1)} %constant.14.clone.c1) | copy-start | bytes 98308
  20.1 4.6 %collective-permute-start.8 = (f32[21,8,128]{2,1,0:T(8,128)S(1)}, f32[21,8,128]{2,1,0:T(8,128)S(1)}, u32[]{:S(2)}, u32[]{:S(2)}) collective-permute-start(f32[21,8,128]{2,1,0:T(8,128)S(1)} %get-tuple-element.42), channel_id=1, source_target_pairs={{0,4},{4,0},{8,12},{12,8},{1,5},{5,1},{9,13},{13,9},{2,6},{6,2},{1... | collective-permute-start | bytes 258056 | tf_op jit(solution)/shard_map/ppermute | solution.py:32
  21.5 3.2 %collective-permute-start.9 = (f32[21,8,128]{2,1,0:T(8,128)S(1)}, f32[21,8,128]{2,1,0:T(8,128)S(1)}, u32[]{:S(2)}, u32[]{:S(2)}) collective-permute-start(f32[21,8,128]{2,1,0:T(8,128)S(1)} %get-tuple-element.43), channel_id=1, source_target_pairs={{0,1},{4,8},{8,4},{12,13},{1,0},{5,9},{9,5},{13,12},{2,3},{6,10},{... | collective-permute-start | bytes 258056 | tf_op jit(solution)/shard_map/ppermute | solution.py:32
  21.5 3.2 %copy-start = (bf16[256,384]{1,0:T(8,128)(2,1)S(1)}, bf16[256,384]{1,0:T(8,128)(2,1)}, u32[]{:S(2)}) copy-start(bf16[256,384]{1,0:T(8,128)(2,1)} %constant.16.clone.p1) | copy-start | bytes 589828
  21.5 3.2 %copy-start.1 = (bf16[128,256]{1,0:T(8,128)(2,1)S(1)}, bf16[128,256]{1,0:T(8,128)(2,1)}, u32[]{:S(2)}) copy-start(bf16[128,256]{1,0:T(8,128)(2,1)} %constant.17.clone.p2) | copy-start | bytes 196612

commit v8 on v7

--- a/solution.py
+++ b/solution.py
@@ -190,8 +190,10 @@
         last(b_out)
 
 
-def own_columns_kernel(x, sub_out, strip_out):
-    count, _, cols = x.shape
+def own_columns_kernel(x, ext, sub_out, strip_out):
+    count, rows, cols = x.shape
+    for l in range(count):
+        ext[l, HX : HX + rows, :] = x[l]
     _, _, y_even = y_sides()
     for g in range(count // SLABS):
         layers = range(SLABS * g, SLABS * g + SLABS)
@@ -201,8 +203,9 @@
         strip_out[g] = jnp.where(y_even, to_left, to_right)
 
 
-def forcing_kernel(x_own, xa, xb, panels, ext, sub_out, strip_out):
-    count, rows, cols = x_own.shape
+def forcing_kernel(ext_in, xa, xb, panels, ext, sub_out, strip_out):
+    count, span, cols = ext.shape
+    rows = span - 2 * HX
     depth = count - 2
     half = count // 2
     tile = lax.axis_index("tile")
@@ -229,8 +232,6 @@
         upper(xa)
         lower(xb)
 
-    for l in range(count):
-        ext[l, HX:high, :] = x_own[l]
 
     span = rows + 2 * HX
     left, right = [], []
@@ -650,7 +651,7 @@
     near = lax.ppermute(panels, "tile", [(i, i ^ 1) for i in range(tiles)])
     a = neighbour_swap(a, "tile", 0, "sub")
     b = neighbour_swap(b, "tile", 1, "sub")
-    sub_own, strip_own = call(own_columns_kernel, [early, early], [], x_own)
+    ext, sub_own, strip_own = call(own_columns_kernel, [(count, span, cols), early, early], [], x_own)
     sub_own = neighbour_swap(sub_own, y_axes, 0, "group")
     strip_own = neighbour_swap(strip_own, y_axes, 1, "group")
     panels = jnp.concatenate([panels, near], 0)
@@ -663,7 +664,8 @@
     slabs = (count // SLABS + 1, 2 * HX, 128)
     ext, sub, strip = call(
         forcing_kernel, [(count, span, cols), slabs, slabs], [],
-        x_own, a, b, panels,
+        ext, a, b, panels,
+        aliases={0: 0},
     )
     sub = neighbour_swap(sub, y_axes, 0, "group")
     strip = neighbour_swap(strip, y_axes, 1, "group")

time: 29.4 us -> 29.3 us (level)
  no operation moved by 1% of the time
where the time goes in v8:
time: 29.3 us; the launch traced here: 29.2 us
  Pallas kernels  10.9 us (37%)
  starting transfers between devices  10.9 us (37%)
  waiting for transfers between devices  6.53 us (22%)
  between operations  0.77 us (3%)
    pallas_call x6, Pallas kernels, call(): pl.pallas_call(kernel, out_shape=[f32(s) for s in outs], in_specs=[VM] *...  5.19 us
    ppermute x8, starting transfers between devices, neighbour_swap(): lax.ppermute(x, (spare,) + axis if leading else axis + (spare,), pairs)  4.79 us
    pallas_call x1, Pallas kernels, body(): pl.pallas_call(up_kernel, out_shape=[f32(own), f32(own)], in_specs=[VM] *...  4.53 us
    ppermute x8, waiting for transfers between devices, neighbour_swap(): lax.ppermute(x, (spare,) + axis if leading else axis + (spare,), pairs)  3.18 us
    ppermute x1, starting transfers between devices, body(): near = lax.ppermute(panels, 'tile', [(i, i ^ 1) for i in range(tiles)])  3.09 us
    ppermute x1, starting transfers between devices, body(): panels = jnp.concatenate([panels, lax.ppermute(panels, 'tile', swap)], 0)  3.03 us
    ppermute x1, waiting for transfers between devices, body(): panels = jnp.concatenate([panels, lax.ppermute(panels, 'tile', swap)], 0)  1.85 us
    ppermute x1, waiting for transfers between devices, body(): near = lax.ppermute(panels, 'tile', [(i, i ^ 1) for i in range(tiles)])  1.5 us
  transfers between devices with their start and end apart: 10, of which 4 were waited for; matrix products, arithmetic and copies ran while one was open for 0% of the time, Pallas kernels for 13%

profile of v8, /device:TPU:0, one launch (start us, length us, event | category | flops | bytes accessed | tf_op | source)
XLA Modules:
  0.0 29.2 jit_solution(8870623282640620459)
XLA Ops:
  0.6 1.2 %shard_map.131 = (f32[18,32,256]{2,1,0:T(8,128)S(1)}, f32[1,8,128]{2,1,0:T(8,128)S(1)}, f32[27,8,256]{2,1,0:T(8,128)S(1)}, f32[27,8,256]{2,1,0:T(8,128)S(1)}) custom-call(f32[16,32,256]{2,1,0:T(8,128)} %rs.1, f32[32,256]{1,0:T(8,128)} %kh.1, f32[32,256]{1,0:T(8,128)} %kv.1, s32[4,128]{1,0:T(4,128)} %bitcast.3, s32[4,128]{1,0:T(4,128)} %bitcast.4, ...), custom_call_target="tpu_custom_call" | custom-call | tf_op jit(solution)/shard_map/pallas_call | solution.py:635
  1.8 3.1 %collective-permute-start.2 = (f32[1,8,128]{2,1,0:T(8,128)S(1)}, f32[1,8,128]{2,1,0:T(8,128)S(1)}, u32[]{:S(2)}, u32[]{:S(2)}) collective-permute-start(f32[1,8,128]{2,1,0:T(8,128)S(1)} %get-tuple-element.36), channel_id=1, source_target_pairs={{0,4},{4,0},{8,12},{12,8},{1,5},{5,1},{9,13},{13,9},{2,6},{6,2},{1... | collective-permute-start | bytes 12296 | tf_op jit(solution)/shard_map/ppermute | solution.py:651
  4.9 0.1 collective-permute-start
  5.0 0.0 collective-permute-start.1
  5.0 1.5 %collective-permute-done.2 = f32[1,8,128]{2,1,0:T(8,128)S(1)} collective-permute-done((f32[1,8,128]{2,1,0:T(8,128)S(1)}, f32[1,8,128]{2,1,0:T(8,128)S(1)}, u32[]{:S(2)}, u32[]{:S(2)}) %collective-permute-start.2) | collective-permute-done | bytes 4128 | tf_op jit(solution)/shard_map/ppermute | solution.py:651
  6.5 3.0 %collective-permute-start.3 = (f32[2,8,128]{2,1,0:T(8,128)S(1)}, f32[2,8,128]{2,1,0:T(8,128)S(1)}, u32[]{:S(2)}, u32[]{:S(2)}) collective-permute-start(f32[2,8,128]{2,1,0:T(8,128)S(1)} %pad_maximum_fusion.1), channel_id=1, source_target_pairs={{0,8},{4,12},{8,0},{12,4},{1,9},{5,13},{9,1},{13,5},{2,10},{6,14},... | collective-permute-start | bytes 24584 | tf_op jit(solution)/shard_map/ppermute | solution.py:661
  9.5 0.2 shard_map.132
  9.7 0.1 collective-permute-start.4
  9.8 1.6 %collective-permute-start.5 = (f32[6,32,128]{2,1,0:T(8,128)S(1)}, f32[6,32,128]{2,1,0:T(8,128)S(1)}, u32[]{:S(2)}, u32[]{:S(2)}) collective-permute-start(f32[6,32,128]{2,1,0:T(8,128)S(1)} %get-tuple-element.39), channel_id=1, source_target_pairs={{0,16},{1,2},{2,1},{3,19},{16,0},{17,18},{18,17},{19,3},{4,20},{5,... | collective-permute-start | bytes 294920 | tf_op jit(solution)/shard_map/ppermute | solution.py:32
  11.4 1.8 %collective-permute-done.3 = f32[2,8,128]{2,1,0:T(8,128)S(1)} collective-permute-done((f32[2,8,128]{2,1,0:T(8,128)S(1)}, f32[2,8,128]{2,1,0:T(8,128)S(1)}, u32[]{:S(2)}, u32[]{:S(2)}) %collective-permute-start.3) | collective-permute-done | bytes 8224 | tf_op jit(solution)/shard_map/ppermute | solution.py:661
  13.3 0.0 collective-permute-done.xa
  13.3 0.0 collective-permute-done.1.xb
  13.3 0.0 copy-start.2
  13.3 0.0 copy-start.5
  13.3 0.7 %shard_map.133 = (f32[18,56,256]{2,1,0:T(8,128)S(1)}, f32[7,24,128]{2,1,0:T(8,128)S(1)}, f32[7,24,128]{2,1,0:T(8,128)S(1)}) custom-call(f32[18,56,256]{2,1,0:T(8,128)S(1)} %get-tuple-element.33.ext_in, f32[27,8,256]{2,1,0:T(8,128)S(1)} %collective-permute-done.xa, f32[27,8,256]{2,1,0:T(8,128)S(1)} %collective-permute-done.1.xb, ...), custom_call_target="tpu_custom_call", output_to_operand_aliasing={{0}: (0, {})} | custom-call | tf_op jit(solution)/shard_map/pallas_call | solution.py:607
  14.0 0.1 collective-permute-start.6
  14.1 1.6 %collective-permute-start.7 = (f32[7,24,128]{2,1,0:T(8,128)S(1)}, f32[7,24,128]{2,1,0:T(8,128)S(1)}, u32[]{:S(2)}, u32[]{:S(2)}) collective-permute-start(f32[7,24,128]{2,1,0:T(8,128)S(1)} %get-tuple-element.41), channel_id=1, source_target_pairs={{0,16},{1,2},{2,1},{3,19},{16,0},{17,18},{18,17},{19,3},{4,20},{5,... | collective-permute-start | bytes 258056 | tf_op jit(solution)/shard_map/ppermute | solution.py:32
  15.6 0.0 copy-done.2
  15.6 0.0 copy-done.5
  15.6 2.0 %shard_map.135 = (f32[16,40,256]{2,1,0:T(8,128)S(1)}, f32[18,32,128]{2,1,0:T(8,128)S(1)}, f32[16,32,128]{2,1,0:T(8,128)S(1)}, f32[18,16,128]{2,1,0:T(8,128)S(1)}) custom-call(f32[18,56,256]{2,1,0:T(8,128)S(1)} %get-tuple-element.37.ext, bf16[256,128]{1,0:T(8,128)(2,1)S(1)} %copy-done.2, bf16[128,128]{1,0:T(8,128)(2,1)S(1)} %copy-done.5), custom_call_target="tpu_custom_call" | custom-call | tf_op jit(solution)/shard_map/pallas_call | solution.py:607
  17.7 0.0 copy-start.3
  17.7 0.0 copy-start.4
  17.7 0.0 collective-permute-done.4.ysub
  17.7 0.0 collective-permute-done.5.ystrip
  17.7 0.3 %shard_map.134.base = f32[18,56,128]{2,1,0:T(8,128)S(1)} custom-call(f32[18,56,256]{2,1,0:T(8,128)S(1)} %get-tuple-element.37.ext, f32[6,32,128]{2,1,0:T(8,128)S(1)} %collective-permute-done.4.ysub, f32[6,32,128]{2,1,0:T(8,128)S(1)} %collective-permute-done.5.ystrip), custom_call_target="tpu_custom_call" | custom-call | tf_op jit(solution)/shard_map/pallas_call | solution.py:607
  18.0 0.0 collective-permute-done.6.ysub
  18.0 0.6 %collective-permute-done.7.ystrip = f32[7,24,128]{2,1,0:T(8,128)S(1)} collective-permute-done((f32[7,24,128]{2,1,0:T(8,128)S(1)}, f32[7,24,128]{2,1,0:T(8,128)S(1)}, u32[]{:S(2)}, u32[]{:S(2)}) %collective-permute-start.7) | collective-permute-done | bytes 86048 | tf_op jit(solution)/shard_map/ppermute | solution.py:32
  18.6 0.0 copy-done.3
  18.6 0.0 copy-done.4
  18.6 1.4 %shard_map.136 = (f32[18,56,128]{2,1,0:T(8,128)S(1)}, f32[16,40,128]{2,1,0:T(8,128)S(1)}, f32[18,32,128]{2,1,0:T(8,128)S(1)}, f32[16,32,128]{2,1,0:T(8,128)S(1)}...) custom-call(f32[18,56,128]{2,1,0:T(8,128)S(1)} %shard_map.134.base, ...), custom_call_target="tpu_custom_call", output_to_operand_aliasing={{0}: (0, {})} | custom-call | tf_op jit(solution)/shard_map/pallas_call | solution.py:607
  20.0 1.4 %collective-permute-start.8 = (f32[21,8,128]{2,1,0:T(8,128)S(1)}, f32[21,8,128]{2,1,0:T(8,128)S(1)}, u32[]{:S(2)}, u32[]{:S(2)}) collective-permute-start(f32[21,8,128]{2,1,0:T(8,128)S(1)} %get-tuple-element.44), channel_id=1, source_target_pairs={{0,4},{4,0},{8,12},{12,8},{1,5},{5,1},{9,13},{13,9},{2,6},{6,2},{1... | collective-permute-start | bytes 258056 | tf_op jit(solution)/shard_map/ppermute | solution.py:32
  21.4 0.0 collective-permute-start.9
  21.4 0.0 copy-start
  21.4 0.0 copy-start.1
  21.4 0.6 %shard_map.137 = (f32[2,40,384]{2,1,0:T(8,128)S(1)}, f32[16,40,384]{2,1,0:T(8,128)S(1)}, f32[16,40,384]{2,1,0:T(8,128)S(1)}, f32[2,40,384]{2,1,0:T(8,128)S(1)}, ...) custom-call(f32[18,56,256]{2,1,0:T(8,128)S(1)} %get-tuple-element.37, ...), custom_call_target="tpu_custom_call" | custom-call | tf_op jit(solution)/shard_map/pallas_call | solution.py:607
  22.0 2.6 %collective-permute-done.8.xa = f32[21,8,128]{2,1,0:T(8,128)S(1)} collective-permute-done((f32[21,8,128]{2,1,0:T(8,128)S(1)}, f32[21,8,128]{2,1,0:T(8,128)S(1)}, u32[]{:S(2)}, u32[]{:S(2)}) %collective-permute-start.8) | collective-permute-done | bytes 86048 | tf_op jit(solution)/shard_map/ppermute | solution.py:32
  24.6 0.0 collective-permute-done.9.xb
  24.6 0.0 copy-done
  24.6 0.0 copy-done.1
  24.6 4.5 %shard_map.138 = (f32[16,32,256]{2,1,0:T(8,128)}, f32[16,32,256]{2,1,0:T(8,128)}) custom-call(f32[18,16,128]{2,1,0:T(8,128)S(1)} %get-tuple-element.43.c_in, f32[21,8,128]{2,1,0:T(8,128)S(1)} %collective-permute-done.8.xa, f32[21,8,128]{2,1,0:T(8,128)S(1)} %collective-permute-done.9.xb, f32[18,56,256]{2,1,0:T(8,128)S(1)} %get-tuple-element.37.ext, ...), custom_call_target="tpu_custom_call" | custom-call | tf_op jit(solution)/shard_map/pallas_call | solution.py:717
  (2 shorter events, 0.0 us)
Async XLA Ops:
  1.8 4.7 %collective-permute-start.2 = (f32[1,8,128]{2,1,0:T(8,128)S(1)}, f32[1,8,128]{2,1,0:T(8,128)S(1)}, u32[]{:S(2)}, u32[]{:S(2)}) collective-permute-start(f32[1,8,128]{2,1,0:T(8,128)S(1)} %get-tuple-element.36), channel_id=1, source_target_pairs={{0,4},{4,0},{8,12},{12,8},{1,5},{5,1},{9,13},{13,9},{2,6},{6,2},{1... | collective-permute-start | bytes 12296 | tf_op jit(solution)/shard_map/ppermute | solution.py:651
  4.9 8.3 %collective-permute-start = (f32[27,8,256]{2,1,0:T(8,128)S(1)}, f32[27,8,256]{2,1,0:T(8,128)S(1)}, u32[]{:S(2)}, u32[]{:S(2)}) collective-permute-start(f32[27,8,256]{2,1,0:T(8,128)S(1)} %get-tuple-element.34), channel_id=1, source_target_pairs={{0,4},{4,0},{8,12},{12,8},{1,5},{5,1},{9,13},{13,9},{2,6},{6,2},{1... | collective-permute-start | bytes 663560 | tf_op jit(solution)/shard_map/ppermute | solution.py:32
  5.0 8.3 %collective-permute-start.1 = (f32[27,8,256]{2,1,0:T(8,128)S(1)}, f32[27,8,256]{2,1,0:T(8,128)S(1)}, u32[]{:S(2)}, u32[]{:S(2)}) collective-permute-start(f32[27,8,256]{2,1,0:T(8,128)S(1)} %get-tuple-element.35), channel_id=1, source_target_pairs={{0,1},{4,8},{8,4},{12,13},{1,0},{5,9},{9,5},{13,12},{2,3},{6,10},{... | collective-permute-start | bytes 663560 | tf_op jit(solution)/shard_map/ppermute | solution.py:32
  6.5 6.7 %collective-permute-start.3 = (f32[2,8,128]{2,1,0:T(8,128)S(1)}, f32[2,8,128]{2,1,0:T(8,128)S(1)}, u32[]{:S(2)}, u32[]{:S(2)}) collective-permute-start(f32[2,8,128]{2,1,0:T(8,128)S(1)} %pad_maximum_fusion.1), channel_id=1, source_target_pairs={{0,8},{4,12},{8,0},{12,4},{1,9},{5,13},{9,1},{13,5},{2,10},{6,14},... | collective-permute-start | bytes 24584 | tf_op jit(solution)/shard_map/ppermute | solution.py:661
  9.7 7.9 %collective-permute-start.4 = (f32[6,32,128]{2,1,0:T(8,128)S(1)}, f32[6,32,128]{2,1,0:T(8,128)S(1)}, u32[]{:S(2)}, u32[]{:S(2)}) collective-permute-start(f32[6,32,128]{2,1,0:T(8,128)S(1)} %get-tuple-element.38), channel_id=1, source_target_pairs={{0,1},{1,0},{2,3},{3,2},{16,17},{17,16},{18,19},{19,18},{4,5},{5,4... | collective-permute-start | bytes 294920 | tf_op jit(solution)/shard_map/ppermute | solution.py:32
  9.8 7.9 %collective-permute-start.5 = (f32[6,32,128]{2,1,0:T(8,128)S(1)}, f32[6,32,128]{2,1,0:T(8,128)S(1)}, u32[]{:S(2)}, u32[]{:S(2)}) collective-permute-start(f32[6,32,128]{2,1,0:T(8,128)S(1)} %get-tuple-element.39), channel_id=1, source_target_pairs={{0,16},{1,2},{2,1},{3,19},{16,0},{17,18},{18,17},{19,3},{4,20},{5,... | collective-permute-start | bytes 294920 | tf_op jit(solution)/shard_map/ppermute | solution.py:32
  13.3 2.4 %copy-start.2 = (bf16[256,128]{1,0:T(8,128)(2,1)S(1)}, bf16[256,128]{1,0:T(8,128)(2,1)}, u32[]{:S(2)}) copy-start(bf16[256,128]{1,0:T(8,128)(2,1)} %constant.12.clone.c1) | copy-start | bytes 196612
  13.3 2.4 %copy-start.5 = (bf16[128,128]{1,0:T(8,128)(2,1)S(1)}, bf16[128,128]{1,0:T(8,128)(2,1)}, u32[]{:S(2)}) copy-start(bf16[128,128]{1,0:T(8,128)(2,1)} %constant.13.clone.c2) | copy-start | bytes 98308
  14.0 4.0 %collective-permute-start.6 = (f32[7,24,128]{2,1,0:T(8,128)S(1)}, f32[7,24,128]{2,1,0:T(8,128)S(1)}, u32[]{:S(2)}, u32[]{:S(2)}) collective-permute-start(f32[7,24,128]{2,1,0:T(8,128)S(1)} %get-tuple-element.40), channel_id=1, source_target_pairs={{0,1},{1,0},{2,3},{3,2},{16,17},{17,16},{18,19},{19,18},{4,5},{5,4... | collective-permute-start | bytes 258056 | tf_op jit(solution)/shard_map/ppermute | solution.py:32
  14.1 4.6 %collective-permute-start.7 = (f32[7,24,128]{2,1,0:T(8,128)S(1)}, f32[7,24,128]{2,1,0:T(8,128)S(1)}, u32[]{:S(2)}, u32[]{:S(2)}) collective-permute-start(f32[7,24,128]{2,1,0:T(8,128)S(1)} %get-tuple-element.41), channel_id=1, source_target_pairs={{0,16},{1,2},{2,1},{3,19},{16,0},{17,18},{18,17},{19,3},{4,20},{5,... | collective-permute-start | bytes 258056 | tf_op jit(solution)/shard_map/ppermute | solution.py:32
  17.7 1.0 %copy-start.3 = (bf16[128,128]{1,0:T(8,128)(2,1)S(1)}, bf16[128,128]{1,0:T(8,128)(2,1)}, u32[]{:S(2)}) copy-start(bf16[128,128]{1,0:T(8,128)(2,1)} %constant.15.clone.c2) | copy-start | bytes 98308
  17.7 0.9 %copy-start.4 = (bf16[128,128]{1,0:T(8,128)(2,1)S(1)}, bf16[128,128]{1,0:T(8,128)(2,1)}, u32[]{:S(2)}) copy-start(bf16[128,128]{1,0:T(8,128)(2,1)} %constant.14.clone.c1) | copy-start | bytes 98308
  20.0 4.6 %collective-permute-start.8 = (f32[21,8,128]{2,1,0:T(8,128)S(1)}, f32[21,8,128]{2,1,0:T(8,128)S(1)}, u32[]{:S(2)}, u32[]{:S(2)}) collective-permute-start(f32[21,8,128]{2,1,0:T(8,128)S(1)} %get-tuple-element.44), channel_id=1, source_target_pairs={{0,4},{4,0},{8,12},{12,8},{1,5},{5,1},{9,13},{13,9},{2,6},{6,2},{1... | collective-permute-start | bytes 258056 | tf_op jit(solution)/shard_map/ppermute | solution.py:32
  21.4 3.2 %collective-permute-start.9 = (f32[21,8,128]{2,1,0:T(8,128)S(1)}, f32[21,8,128]{2,1,0:T(8,128)S(1)}, u32[]{:S(2)}, u32[]{:S(2)}) collective-permute-start(f32[21,8,128]{2,1,0:T(8,128)S(1)} %get-tuple-element.45), channel_id=1, source_target_pairs={{0,1},{4,8},{8,4},{12,13},{1,0},{5,9},{9,5},{13,12},{2,3},{6,10},{... | collective-permute-start | bytes 258056 | tf_op jit(solution)/shard_map/ppermute | solution.py:32
  21.4 3.2 %copy-start = (bf16[256,384]{1,0:T(8,128)(2,1)S(1)}, bf16[256,384]{1,0:T(8,128)(2,1)}, u32[]{:S(2)}) copy-start(bf16[256,384]{1,0:T(8,128)(2,1)} %constant.16.clone.p1) | copy-start | bytes 589828
  21.4 3.2 %copy-start.1 = (bf16[128,256]{1,0:T(8,128)(2,1)S(1)}, bf16[128,256]{1,0:T(8,128)(2,1)}, u32[]{:S(2)}) copy-start(bf16[128,256]{1,0:T(8,128)(2,1)} %constant.17.clone.p2) | copy-start | bytes 196612

commit v9 on v8

--- a/solution.py
+++ b/solution.py
@@ -397,8 +397,8 @@
 
 def edge_kernel(
     base, ysub, ystrip, c_inner, c1, c2,
-    b_out, u_out, b1_out, u1_out, c_out, a_msg, b_msg,
-    w0, al0, be0, u0, u0n, r0, w1, al1, be1, u1, u1n, r1,
+    b_out, u0n, b1_out, u1n, c_out, a_msg, b_msg,
+    w0, al0, be0, u0, r0, w1, al1, be1, u1, r1,
 ):
     count, span = base.shape[:2]
     depth = count - 2
@@ -428,8 +428,6 @@
         b_out, b_out[depth], b_out[depth + 1], 1.0, edge_inside((span, 128), rows, HX, HY, EDGE),
         w0, al0, be0, u0, u0n, depth,
     )
-    for z in range(depth):
-        u_out[z] = u0n[z + 1, 8 : span - 8, :]
     b1_out[...] = restrict(b_out, u0n, 1.0, r0, depth, c1[...])
     span1 = b1_out.shape[1]
     presmooth(
@@ -437,7 +435,6 @@
         edge_inside((span1, 128), rows // 2, HX // 2, HY // 2, EDGE // 2),
         w1, al1, be1, u1, u1n, depth,
     )
-    u1_out[...] = u1n[pl.ds(1, depth)]
     c_out[...] = c_inner[...] + restrict(b1_out, u1n, 0.25, r1, depth, c2[...])
     own2 = HX // 4
 
@@ -491,9 +488,9 @@
     )
     for z in range(depth):
         i = min(z, 1)
-        u0[z] = part0(u_in[z], u_edge[z])
+        u0[z] = part0(u_in[z], u_edge[z + 1, low:top, :])
         wb0[z] = w0[i] * part0(ext[z, low:top, :], edge[z, low:top, :])
-        u1[z] = part1(u1_in[z], u1_edge[z])
+        u1[z] = part1(u1_in[z], u1_edge[z + 1])
         wb1[z] = w1[i] * part1(b1_in[z], b1_edge[z])
 
 
@@ -675,10 +672,10 @@
     span1 = (span + 8) // 2
     span2 = span1 // 2
 
-    def down_scratch(width, width1):
+    def down_scratch(width, width1, fields=2):
         return (
-            [(2, span, width)] * 3 + [(depth + 2, span, width)] * 2 + [(count, width // 128, span + 8, 128)]
-            + [(2, span1, width1)] * 3 + [(depth + 2, span1, width1)] * 2 + [(count, width1 // 128, span1, 128)]
+            [(2, span, width)] * 3 + [(depth + 2, span, width)] * fields + [(count, width // 128, span + 8, 128)]
+            + [(2, span1, width1)] * 3 + [(depth + 2, span1, width1)] * fields + [(count, width1 // 128, span1, 128)]
         )
 
     u_in, b1_in, u1_in, c_in = call(
@@ -692,10 +689,10 @@
     edge, u_edge, b1_edge, u1_edge, c_own, a2, b2 = call(
         edge_kernel,
         [
-            (count, span, 128), (depth, small, 128), (count, span1, 128), (depth, span1, 128),
+            (count, span, 128), (depth + 2, span, 128), (count, span1, 128), (depth + 2, span1, 128),
             (count, span2, half), message2, message2,
         ],
-        down_scratch(128, 128),
+        down_scratch(128, 128, 1),
         base, sub, strip, c_in, c1_edge, c2_edge,
         aliases={0: 0},
     )

time: 29.3 us -> 29.6 us (1.010)
  Pallas kernels: 10.9 us -> 11.3 us
where the time goes in v9:
time: 29.6 us; the launch traced here: 29.4 us
  Pallas kernels  11.3 us (38%)
  starting transfers between devices  10.9 us (37%)
  waiting for transfers between devices  6.4 us (22%)
  between operations  0.77 us (3%)
    pallas_call x6, Pallas kernels, call(): pl.pallas_call(kernel, out_shape=[f32(s) for s in outs], in_specs=[VM] *...  5.36 us
    ppermute x8, starting transfers between devices, neighbour_swap(): lax.ppermute(x, (spare,) + axis if leading else axis + (spare,), pairs)  4.79 us
    pallas_call x1, Pallas kernels, body(): pl.pallas_call(up_kernel, out_shape=[f32(own), f32(own)], in_specs=[VM] *...  4.72 us
    ppermute x1, starting transfers between devices, body(): near = lax.ppermute(panels, 'tile', [(i, i ^ 1) for i in range(tiles)])  3.09 us
    ppermute x8, waiting for transfers between devices, neighbour_swap(): lax.ppermute(x, (spare,) + axis if leading else axis + (spare,), pairs)  3.05 us
    ppermute x1, starting transfers between devices, body(): panels = jnp.concatenate([panels, lax.ppermute(panels, 'tile', swap)], 0)  3.03 us
    ppermute x1, waiting for transfers between devices, body(): panels = jnp.concatenate([panels, lax.ppermute(panels, 'tile', swap)], 0)  1.85 us
    ppermute x1, waiting for transfers between devices, body(): near = lax.ppermute(panels, 'tile', [(i, i ^ 1) for i in range(tiles)])  1.5 us
  transfers between devices with their start and end apart: 10, of which 4 were waited for; matrix products, arithmetic and copies ran while one was open for 0% of the time, Pallas kernels for 13%

profile of v9, /device:TPU:0, one launch (start us, length us, event | category | flops | bytes accessed | tf_op | source)
XLA Modules:
  0.0 29.4 jit_solution(7134257407152912363)
XLA Ops:
  0.6 1.2 %shard_map.131 = (f32[18,32,256]{2,1,0:T(8,128)S(1)}, f32[1,8,128]{2,1,0:T(8,128)S(1)}, f32[27,8,256]{2,1,0:T(8,128)S(1)}, f32[27,8,256]{2,1,0:T(8,128)S(1)}) custom-call(f32[16,32,256]{2,1,0:T(8,128)} %rs.1, f32[32,256]{1,0:T(8,128)} %kh.1, f32[32,256]{1,0:T(8,128)} %kv.1, s32[4,128]{1,0:T(4,128)} %bitcast.3, s32[4,128]{1,0:T(4,128)} %bitcast.4, ...), custom_call_target="tpu_custom_call" | custom-call | tf_op jit(solution)/shard_map/pallas_call | solution.py:632
  1.8 3.1 %collective-permute-start.2 = (f32[1,8,128]{2,1,0:T(8,128)S(1)}, f32[1,8,128]{2,1,0:T(8,128)S(1)}, u32[]{:S(2)}, u32[]{:S(2)}) collective-permute-start(f32[1,8,128]{2,1,0:T(8,128)S(1)} %get-tuple-element.36), channel_id=1, source_target_pairs={{0,4},{4,0},{8,12},{12,8},{1,5},{5,1},{9,13},{13,9},{2,6},{6,2},{1... | collective-permute-start | bytes 12296 | tf_op jit(solution)/shard_map/ppermute | solution.py:648
  4.9 0.1 collective-permute-start
  5.0 0.0 collective-permute-start.1
  5.0 1.5 %collective-permute-done.2 = f32[1,8,128]{2,1,0:T(8,128)S(1)} collective-permute-done((f32[1,8,128]{2,1,0:T(8,128)S(1)}, f32[1,8,128]{2,1,0:T(8,128)S(1)}, u32[]{:S(2)}, u32[]{:S(2)}) %collective-permute-start.2) | collective-permute-done | bytes 4128 | tf_op jit(solution)/shard_map/ppermute | solution.py:648
  6.5 3.0 %collective-permute-start.3 = (f32[2,8,128]{2,1,0:T(8,128)S(1)}, f32[2,8,128]{2,1,0:T(8,128)S(1)}, u32[]{:S(2)}, u32[]{:S(2)}) collective-permute-start(f32[2,8,128]{2,1,0:T(8,128)S(1)} %pad_maximum_fusion.1), channel_id=1, source_target_pairs={{0,8},{4,12},{8,0},{12,4},{1,9},{5,13},{9,1},{13,5},{2,10},{6,14},... | collective-permute-start | bytes 24584 | tf_op jit(solution)/shard_map/ppermute | solution.py:658
  9.5 0.2 shard_map.132
  9.7 0.1 collective-permute-start.4
  9.8 1.6 %collective-permute-start.5 = (f32[6,32,128]{2,1,0:T(8,128)S(1)}, f32[6,32,128]{2,1,0:T(8,128)S(1)}, u32[]{:S(2)}, u32[]{:S(2)}) collective-permute-start(f32[6,32,128]{2,1,0:T(8,128)S(1)} %get-tuple-element.39), channel_id=1, source_target_pairs={{0,16},{1,2},{2,1},{3,19},{16,0},{17,18},{18,17},{19,3},{4,20},{5,... | collective-permute-start | bytes 294920 | tf_op jit(solution)/shard_map/ppermute | solution.py:32
  11.4 1.8 %collective-permute-done.3 = f32[2,8,128]{2,1,0:T(8,128)S(1)} collective-permute-done((f32[2,8,128]{2,1,0:T(8,128)S(1)}, f32[2,8,128]{2,1,0:T(8,128)S(1)}, u32[]{:S(2)}, u32[]{:S(2)}) %collective-permute-start.3) | collective-permute-done | bytes 8224 | tf_op jit(solution)/shard_map/ppermute | solution.py:658
  13.3 0.0 collective-permute-done.xa
  13.3 0.0 collective-permute-done.1.xb
  13.3 0.0 copy-start.2
  13.3 0.0 copy-start.5
  13.3 0.7 %shard_map.133 = (f32[18,56,256]{2,1,0:T(8,128)S(1)}, f32[7,24,128]{2,1,0:T(8,128)S(1)}, f32[7,24,128]{2,1,0:T(8,128)S(1)}) custom-call(f32[18,56,256]{2,1,0:T(8,128)S(1)} %get-tuple-element.33.ext_in, f32[27,8,256]{2,1,0:T(8,128)S(1)} %collective-permute-done.xa, f32[27,8,256]{2,1,0:T(8,128)S(1)} %collective-permute-done.1.xb, ...), custom_call_target="tpu_custom_call", output_to_operand_aliasing={{0}: (0, {})} | custom-call | tf_op jit(solution)/shard_map/pallas_call | solution.py:604
  14.0 0.1 collective-permute-start.6
  14.1 1.6 %collective-permute-start.7 = (f32[7,24,128]{2,1,0:T(8,128)S(1)}, f32[7,24,128]{2,1,0:T(8,128)S(1)}, u32[]{:S(2)}, u32[]{:S(2)}) collective-permute-start(f32[7,24,128]{2,1,0:T(8,128)S(1)} %get-tuple-element.41), channel_id=1, source_target_pairs={{0,16},{1,2},{2,1},{3,19},{16,0},{17,18},{18,17},{19,3},{4,20},{5,... | collective-permute-start | bytes 258056 | tf_op jit(solution)/shard_map/ppermute | solution.py:32
  15.6 0.0 copy-done.2
  15.6 0.0 copy-done.5
  15.6 2.1 %shard_map.135 = (f32[16,40,256]{2,1,0:T(8,128)S(1)}, f32[18,32,128]{2,1,0:T(8,128)S(1)}, f32[16,32,128]{2,1,0:T(8,128)S(1)}, f32[18,16,128]{2,1,0:T(8,128)S(1)}) custom-call(f32[18,56,256]{2,1,0:T(8,128)S(1)} %get-tuple-element.37.ext, bf16[256,128]{1,0:T(8,128)(2,1)S(1)} %copy-done.2, bf16[128,128]{1,0:T(8,128)(2,1)S(1)} %copy-done.5), custom_call_target="tpu_custom_call" | custom-call | tf_op jit(solution)/shard_map/pallas_call | solution.py:604
  17.8 0.0 copy-start.3
  17.8 0.0 copy-start.4
  17.8 0.0 collective-permute-done.4.ysub
  17.8 0.0 collective-permute-done.5.ystrip
  17.8 0.3 %shard_map.134.base = f32[18,56,128]{2,1,0:T(8,128)S(1)} custom-call(f32[18,56,256]{2,1,0:T(8,128)S(1)} %get-tuple-element.37.ext, f32[6,32,128]{2,1,0:T(8,128)S(1)} %collective-permute-done.4.ysub, f32[6,32,128]{2,1,0:T(8,128)S(1)} %collective-permute-done.5.ystrip), custom_call_target="tpu_custom_call" | custom-call | tf_op jit(solution)/shard_map/pallas_call | solution.py:604
  18.1 0.0 collective-permute-done.6.ysub
  18.1 0.5 %collective-permute-done.7.ystrip = f32[7,24,128]{2,1,0:T(8,128)S(1)} collective-permute-done((f32[7,24,128]{2,1,0:T(8,128)S(1)}, f32[7,24,128]{2,1,0:T(8,128)S(1)}, u32[]{:S(2)}, u32[]{:S(2)}) %collective-permute-start.7) | collective-permute-done | bytes 86048 | tf_op jit(solution)/shard_map/ppermute | solution.py:32
  18.6 0.0 copy-done.3
  18.6 0.0 copy-done.4
  18.6 1.4 %shard_map.136 = (f32[18,56,128]{2,1,0:T(8,128)S(1)}, f32[18,56,128]{2,1,0:T(8,128)S(1)}, f32[18,32,128]{2,1,0:T(8,128)S(1)}, f32[18,32,128]{2,1,0:T(8,128)S(1)}...) custom-call(f32[18,56,128]{2,1,0:T(8,128)S(1)} %shard_map.134.base, ...), custom_call_target="tpu_custom_call", output_to_operand_aliasing={{0}: (0, {})} | custom-call | tf_op jit(solution)/shard_map/pallas_call | solution.py:604
  20.0 1.4 %collective-permute-start.8 = (f32[21,8,128]{2,1,0:T(8,128)S(1)}, f32[21,8,128]{2,1,0:T(8,128)S(1)}, u32[]{:S(2)}, u32[]{:S(2)}) collective-permute-start(f32[21,8,128]{2,1,0:T(8,128)S(1)} %get-tuple-element.44), channel_id=1, source_target_pairs={{0,4},{4,0},{8,12},{12,8},{1,5},{5,1},{9,13},{13,9},{2,6},{6,2},{1... | collective-permute-start | bytes 258056 | tf_op jit(solution)/shard_map/ppermute | solution.py:32
  21.4 0.0 collective-permute-start.9
  21.4 0.0 copy-start
  21.4 0.0 copy-start.1
  21.4 0.7 %shard_map.137 = (f32[2,40,384]{2,1,0:T(8,128)S(1)}, f32[16,40,384]{2,1,0:T(8,128)S(1)}, f32[16,40,384]{2,1,0:T(8,128)S(1)}, f32[2,40,384]{2,1,0:T(8,128)S(1)}, ...) custom-call(f32[18,56,256]{2,1,0:T(8,128)S(1)} %get-tuple-element.37, ...), custom_call_target="tpu_custom_call" | custom-call | tf_op jit(solution)/shard_map/pallas_call | solution.py:604
  22.1 2.5 %collective-permute-done.8.xa = f32[21,8,128]{2,1,0:T(8,128)S(1)} collective-permute-done((f32[21,8,128]{2,1,0:T(8,128)S(1)}, f32[21,8,128]{2,1,0:T(8,128)S(1)}, u32[]{:S(2)}, u32[]{:S(2)}) %collective-permute-start.8) | collective-permute-done | bytes 86048 | tf_op jit(solution)/shard_map/ppermute | solution.py:32
  24.7 0.0 collective-permute-done.9.xb
  24.7 0.0 copy-done
  24.7 0.0 copy-done.1
  24.7 4.7 %shard_map.138 = (f32[16,32,256]{2,1,0:T(8,128)}, f32[16,32,256]{2,1,0:T(8,128)}) custom-call(f32[18,16,128]{2,1,0:T(8,128)S(1)} %get-tuple-element.43.c_in, f32[21,8,128]{2,1,0:T(8,128)S(1)} %collective-permute-done.8.xa, f32[21,8,128]{2,1,0:T(8,128)S(1)} %collective-permute-done.9.xb, f32[18,56,256]{2,1,0:T(8,128)S(1)} %get-tuple-element.37.ext, ...), custom_call_target="tpu_custom_call" | custom-call | tf_op jit(solution)/shard_map/pallas_call | solution.py:714
  (2 shorter events, 0.0 us)
Async XLA Ops:
  1.8 4.7 %collective-permute-start.2 = (f32[1,8,128]{2,1,0:T(8,128)S(1)}, f32[1,8,128]{2,1,0:T(8,128)S(1)}, u32[]{:S(2)}, u32[]{:S(2)}) collective-permute-start(f32[1,8,128]{2,1,0:T(8,128)S(1)} %get-tuple-element.36), channel_id=1, source_target_pairs={{0,4},{4,0},{8,12},{12,8},{1,5},{5,1},{9,13},{13,9},{2,6},{6,2},{1... | collective-permute-start | bytes 12296 | tf_op jit(solution)/shard_map/ppermute | solution.py:648
  4.9 8.3 %collective-permute-start = (f32[27,8,256]{2,1,0:T(8,128)S(1)}, f32[27,8,256]{2,1,0:T(8,128)S(1)}, u32[]{:S(2)}, u32[]{:S(2)}) collective-permute-start(f32[27,8,256]{2,1,0:T(8,128)S(1)} %get-tuple-element.34), channel_id=1, source_target_pairs={{0,4},{4,0},{8,12},{12,8},{1,5},{5,1},{9,13},{13,9},{2,6},{6,2},{1... | collective-permute-start | bytes 663560 | tf_op jit(solution)/shard_map/ppermute | solution.py:32
  5.0 8.3 %collective-permute-start.1 = (f32[27,8,256]{2,1,0:T(8,128)S(1)}, f32[27,8,256]{2,1,0:T(8,128)S(1)}, u32[]{:S(2)}, u32[]{:S(2)}) collective-permute-start(f32[27,8,256]{2,1,0:T(8,128)S(1)} %get-tuple-element.35), channel_id=1, source_target_pairs={{0,1},{4,8},{8,4},{12,13},{1,0},{5,9},{9,5},{13,12},{2,3},{6,10},{... | collective-permute-start | bytes 663560 | tf_op jit(solution)/shard_map/ppermute | solution.py:32
  6.5 6.7 %collective-permute-start.3 = (f32[2,8,128]{2,1,0:T(8,128)S(1)}, f32[2,8,128]{2,1,0:T(8,128)S(1)}, u32[]{:S(2)}, u32[]{:S(2)}) collective-permute-start(f32[2,8,128]{2,1,0:T(8,128)S(1)} %pad_maximum_fusion.1), channel_id=1, source_target_pairs={{0,8},{4,12},{8,0},{12,4},{1,9},{5,13},{9,1},{13,5},{2,10},{6,14},... | collective-permute-start | bytes 24584 | tf_op jit(solution)/shard_map/ppermute | solution.py:658
  9.7 8.0 %collective-permute-start.4 = (f32[6,32,128]{2,1,0:T(8,128)S(1)}, f32[6,32,128]{2,1,0:T(8,128)S(1)}, u32[]{:S(2)}, u32[]{:S(2)}) collective-permute-start(f32[6,32,128]{2,1,0:T(8,128)S(1)} %get-tuple-element.38), channel_id=1, source_target_pairs={{0,1},{1,0},{2,3},{3,2},{16,17},{17,16},{18,19},{19,18},{4,5},{5,4... | collective-permute-start | bytes 294920 | tf_op jit(solution)/shard_map/ppermute | solution.py:32
  9.8 8.0 %collective-permute-start.5 = (f32[6,32,128]{2,1,0:T(8,128)S(1)}, f32[6,32,128]{2,1,0:T(8,128)S(1)}, u32[]{:S(2)}, u32[]{:S(2)}) collective-permute-start(f32[6,32,128]{2,1,0:T(8,128)S(1)} %get-tuple-element.39), channel_id=1, source_target_pairs={{0,16},{1,2},{2,1},{3,19},{16,0},{17,18},{18,17},{19,3},{4,20},{5,... | collective-permute-start | bytes 294920 | tf_op jit(solution)/shard_map/ppermute | solution.py:32
  13.3 2.4 %copy-start.2 = (bf16[256,128]{1,0:T(8,128)(2,1)S(1)}, bf16[256,128]{1,0:T(8,128)(2,1)}, u32[]{:S(2)}) copy-start(bf16[256,128]{1,0:T(8,128)(2,1)} %constant.12.clone.c1) | copy-start | bytes 196612
  13.3 2.4 %copy-start.5 = (bf16[128,128]{1,0:T(8,128)(2,1)S(1)}, bf16[128,128]{1,0:T(8,128)(2,1)}, u32[]{:S(2)}) copy-start(bf16[128,128]{1,0:T(8,128)(2,1)} %constant.13.clone.c2) | copy-start | bytes 98308
  14.0 4.1 %collective-permute-start.6 = (f32[7,24,128]{2,1,0:T(8,128)S(1)}, f32[7,24,128]{2,1,0:T(8,128)S(1)}, u32[]{:S(2)}, u32[]{:S(2)}) collective-permute-start(f32[7,24,128]{2,1,0:T(8,128)S(1)} %get-tuple-element.40), channel_id=1, source_target_pairs={{0,1},{1,0},{2,3},{3,2},{16,17},{17,16},{18,19},{19,18},{4,5},{5,4... | collective-permute-start | bytes 258056 | tf_op jit(solution)/shard_map/ppermute | solution.py:32
  14.1 4.6 %collective-permute-start.7 = (f32[7,24,128]{2,1,0:T(8,128)S(1)}, f32[7,24,128]{2,1,0:T(8,128)S(1)}, u32[]{:S(2)}, u32[]{:S(2)}) collective-permute-start(f32[7,24,128]{2,1,0:T(8,128)S(1)} %get-tuple-element.41), channel_id=1, source_target_pairs={{0,16},{1,2},{2,1},{3,19},{16,0},{17,18},{18,17},{19,3},{4,20},{5,... | collective-permute-start | bytes 258056 | tf_op jit(solution)/shard_map/ppermute | solution.py:32
  17.8 0.9 %copy-start.3 = (bf16[128,128]{1,0:T(8,128)(2,1)S(1)}, bf16[128,128]{1,0:T(8,128)(2,1)}, u32[]{:S(2)}) copy-start(bf16[128,128]{1,0:T(8,128)(2,1)} %constant.15.clone.c2) | copy-start | bytes 98308
  17.8 0.8 %copy-start.4 = (bf16[128,128]{1,0:T(8,128)(2,1)S(1)}, bf16[128,128]{1,0:T(8,128)(2,1)}, u32[]{:S(2)}) copy-start(bf16[128,128]{1,0:T(8,128)(2,1)} %constant.14.clone.c1) | copy-start | bytes 98308
  20.0 4.6 %collective-permute-start.8 = (f32[21,8,128]{2,1,0:T(8,128)S(1)}, f32[21,8,128]{2,1,0:T(8,128)S(1)}, u32[]{:S(2)}, u32[]{:S(2)}) collective-permute-start(f32[21,8,128]{2,1,0:T(8,128)S(1)} %get-tuple-element.44), channel_id=1, source_target_pairs={{0,4},{4,0},{8,12},{12,8},{1,5},{5,1},{9,13},{13,9},{2,6},{6,2},{1... | collective-permute-start | bytes 258056 | tf_op jit(solution)/shard_map/ppermute | solution.py:32
  21.4 3.2 %collective-permute-start.9 = (f32[21,8,128]{2,1,0:T(8,128)S(1)}, f32[21,8,128]{2,1,0:T(8,128)S(1)}, u32[]{:S(2)}, u32[]{:S(2)}) collective-permute-start(f32[21,8,128]{2,1,0:T(8,128)S(1)} %get-tuple-element.45), channel_id=1, source_target_pairs={{0,1},{4,8},{8,4},{12,13},{1,0},{5,9},{9,5},{13,12},{2,3},{6,10},{... | collective-permute-start | bytes 258056 | tf_op jit(solution)/shard_map/ppermute | solution.py:32
  21.4 3.2 %copy-start = (bf16[256,384]{1,0:T(8,128)(2,1)S(1)}, bf16[256,384]{1,0:T(8,128)(2,1)}, u32[]{:S(2)}) copy-start(bf16[256,384]{1,0:T(8,128)(2,1)} %constant.16.clone.p1) | copy-start | bytes 589828
  21.4 3.2 %copy-start.1 = (bf16[128,256]{1,0:T(8,128)(2,1)S(1)}, bf16[128,256]{1,0:T(8,128)(2,1)}, u32[]{:S(2)}) copy-start(bf16[128,256]{1,0:T(8,128)(2,1)} %constant.17.clone.p2) | copy-start | bytes 196612
